TPU v7x, 32 devices: a whole 2x2x4 slice. The times are simulated.
32 devices in a mesh: dp: 8 (over z, y), tensor: 4 (over x, core).
Axes of the slice: x: 2, y: 2, z: 4, core: 2. Of those that a mesh axis runs over, the one named last changes fastest.
Arguments:
- text_in: bfloat16 [16384, 768], P(('dp', 'tensor')), may hold values from -6 to 6
- layout_in: bfloat16 [16384, 192], P(('dp', 'tensor')), may hold values from -6 to 6
- token_mask: int32 [16384], P(('dp', 'tensor')), may hold values 0 or 1
- box_mask: int32 [16384], P(('dp', 'tensor')), may hold values 0 or 1
- cot_text: bfloat16 [16384, 768], P(('dp', 'tensor')), may hold values from -6 to 6
- cot_layout: bfloat16 [16384, 192], P(('dp', 'tensor')), may hold values from -6 to 6
- text_query_weight: bfloat16 [768, 768], replicated, may hold values from -0.21875 to 0.21875
- text_query_bias: bfloat16 [768], replicated, may hold values from -2.5 to 2.5
- text_key_weight: bfloat16 [768, 768], replicated, may hold values from -0.21875 to 0.21875
- text_value_weight: bfloat16 [768, 768], replicated, may hold values from -0.21875 to 0.21875
- text_value_bias: bfloat16 [768], replicated, may hold values from -2.5 to 2.5
- text_output_weight: bfloat16 [768, 768], replicated, may hold values from -1.75 to 1.75
- text_output_bias: bfloat16 [768], replicated, may hold values from -2.5 to 2.5
- text_attend_gain: bfloat16 [768], replicated, may hold values from 0.25 to 1.75
- text_attend_shift: bfloat16 [768], replicated, may hold values from -2.5 to 2.5
- text_up_weight: bfloat16 [768, 3072], P(None, 'tensor'), may hold values from -0.21875 to 0.21875
- text_up_bias: bfloat16 [3072], P('tensor'), may hold values from -2.5 to 2.5
- text_down_weight: bfloat16 [3072, 768], P('tensor'), may hold values from -0.109375 to 0.109375
- text_down_bias: bfloat16 [768], replicated, may hold values from -2.5 to 2.5
- text_feed_gain: bfloat16 [768], replicated, may hold values from 0.25 to 1.75
- text_feed_shift: bfloat16 [768], replicated, may hold values from -2.5 to 2.5
- layout_query_weight: bfloat16 [192, 192], replicated, may hold values from -0.4375 to 0.4375
- layout_query_bias: bfloat16 [192], replicated, may hold values from -2.5 to 2.5
- layout_key_weight: bfloat16 [192, 192], replicated, may hold values from -0.4375 to 0.4375
- layout_value_weight: bfloat16 [192, 192], replicated, may hold values from -0.4375 to 0.4375
- layout_value_bias: bfloat16 [192], replicated, may hold values from -2.5 to 2.5
- layout_output_weight: bfloat16 [192, 192], replicated, may hold values from -3.5 to 3.5
- layout_output_bias: bfloat16 [192], replicated, may hold values from -2.5 to 2.5
- layout_attend_gain: bfloat16 [192], replicated, may hold values from 0.25 to 1.75
- layout_attend_shift: bfloat16 [192], replicated, may hold values from -2.5 to 2.5
- layout_up_weight: bfloat16 [192, 768], P(None, 'tensor'), may hold values from -0.4375 to 0.4375
- layout_up_bias: bfloat16 [768], P('tensor'), may hold values from -2.5 to 2.5
- layout_down_weight: bfloat16 [768, 192], P('tensor'), may hold values from -0.21875 to 0.21875
- layout_down_bias: bfloat16 [192], replicated, may hold values from -2.5 to 2.5
- layout_feed_gain: bfloat16 [192], replicated, may hold values from 0.25 to 1.75
- layout_feed_shift: bfloat16 [192], replicated, may hold values from -2.5 to 2.5
Outputs:
- text_out: bfloat16 [16384, 768], P(('dp', 'tensor'))
- layout_out: bfloat16 [16384, 192], P(('dp', 'tensor'))
- text_in_grad: float32 [16384, 768], P(('dp', 'tensor'))
- layout_in_grad: float32 [16384, 192], P(('dp', 'tensor'))
- grad_text_query_weight: float32 [768, 768], replicated
- grad_text_query_bias: float32 [768], replicated
- grad_text_key_weight: float32 [768, 768], replicated
- grad_text_value_weight: float32 [768, 768], replicated
- grad_text_value_bias: float32 [768], replicated
- grad_text_output_weight: float32 [768, 768], replicated
- grad_text_output_bias: float32 [768], replicated
- grad_text_attend_gain: float32 [768], replicated
- grad_text_attend_shift: float32 [768], replicated
- grad_text_up_weight: float32 [768, 3072], P(None, 'tensor')
- grad_text_up_bias: float32 [3072], P('tensor')
- grad_text_down_weight: float32 [3072, 768], P('tensor')
- grad_text_down_bias: float32 [768], replicated
- grad_text_feed_gain: float32 [768], replicated
- grad_text_feed_shift: float32 [768], replicated
- grad_layout_query_weight: float32 [192, 192], replicated
- grad_layout_query_bias: float32 [192], replicated
- grad_layout_key_weight: float32 [192, 192], replicated
- grad_layout_value_weight: float32 [192, 192], replicated
- grad_layout_value_bias: float32 [192], replicated
- grad_layout_output_weight: float32 [192, 192], replicated
- grad_layout_output_bias: float32 [192], replicated
- grad_layout_attend_gain: float32 [192], replicated
- grad_layout_attend_shift: float32 [192], replicated
- grad_layout_up_weight: float32 [192, 768], P(None, 'tensor')
- grad_layout_up_bias: float32 [768], P('tensor')
- grad_layout_down_weight: float32 [768, 192], P('tensor')
- grad_layout_down_bias: float32 [192], replicated
- grad_layout_feed_gain: float32 [192], replicated
- grad_layout_feed_shift: float32 [192], replicated
All inputs are finite; a program needn't handle non-finite values. No bound on the sum of `token_mask` or of `box_mask` on one device may be relied on, other than what follows from the above.
Results may differ from a plain program's by a relative error of at most 0.013.
The roundings to bfloat16 on the way count: a program that leaves them out, or rounds other values in their place, can miss the bound.
Values may be sent and summed in bfloat16 or wider, within the bound.
A program may use at most 192 MiB of HBM per device.

v0:
```python
import jax
import jax.numpy as jnp
from jax import lax
from jax.sharding import PartitionSpec as P

HEADS = 12
PAGE = 512


NORM_EPS = 1e-05


def rounded(values):
    return values.astype(jnp.bfloat16)


def matmul(first, second):
    return jnp.dot(first, second, preferred_element_type=jnp.float32)


def inner_rows(first, second):
    return lax.dot_general(
        first, second, (((0,), (0,)), ((), ())), preferred_element_type=jnp.float32
    )


def inner_cols(first, second):
    return lax.dot_general(
        first, second, (((1,), (1,)), ((), ())), preferred_element_type=jnp.float32
    )


def column_sum(values):
    return jnp.sum(values, axis=0, dtype=jnp.float32)


def norm_rows(values, gain, shift):
    average = jnp.mean(values, axis=-1, keepdims=True)
    centered = values - average
    variance = jnp.mean(centered * centered, axis=-1, keepdims=True)
    return centered * lax.rsqrt(variance + NORM_EPS) * gain + shift


def norm_back(values, gain, shift, grad):
    _, pullback = jax.vjp(norm_rows, values, gain.astype(jnp.float32), shift.astype(jnp.float32))
    return pullback(grad)


def project_three(inputs, query_weight, query_bias, key_weight, value_weight, value_bias):
    return (
        rounded(matmul(inputs, query_weight) + query_bias),
        rounded(matmul(inputs, key_weight)),
        rounded(matmul(inputs, value_weight) + value_bias),
    )


def page_scores(text_queries, text_keys, layout_queries, layout_keys):
    text_factor = text_queries.shape[-1] ** (-0.5)
    layout_factor = layout_queries.shape[-1] ** (-0.5)
    text_scores = (
        jnp.einsum("qhd,khd->hqk", text_queries, text_keys, preferred_element_type=jnp.float32)
        * text_factor
    )
    layout_scores = (
        jnp.einsum("qhd,khd->hqk", layout_queries, layout_keys, preferred_element_type=jnp.float32)
        * layout_factor
    )
    return (text_scores, layout_scores)


def page_forward(pieces):
    text_queries, text_keys, text_values, layout_queries, layout_keys, layout_values = pieces
    text_scores, layout_scores = page_scores(text_queries, text_keys, layout_queries, layout_keys)
    joint = text_scores + layout_scores
    highest = jnp.max(joint, axis=-1, keepdims=True)
    exponent = jnp.exp(joint - highest)
    totals = jnp.sum(exponent, axis=-1, keepdims=True)
    weights = rounded(exponent / totals)
    text_context = rounded(
        jnp.einsum("hqk,khd->qhd", weights, text_values, preferred_element_type=jnp.float32)
    )
    layout_context = rounded(
        jnp.einsum("hqk,khd->qhd", weights, layout_values, preferred_element_type=jnp.float32)
    )
    return (text_context, layout_context, (highest + jnp.log(totals))[..., 0])


def softmax_back(context_grad, values, weights_full):
    weights_grad = jnp.einsum(
        "qhd,khd->hqk", context_grad, values, preferred_element_type=jnp.float32
    )
    return weights_full * (
        weights_grad - jnp.sum(weights_grad * weights_full, axis=-1, keepdims=True)
    )


def page_backward(pieces):
    (
        text_queries,
        text_keys,
        text_values,
        layout_queries,
        layout_keys,
        layout_values,
        log_total,
        text_context_grad,
        layout_context_grad,
    ) = pieces
    text_factor = text_queries.shape[-1] ** (-0.5)
    layout_factor = layout_queries.shape[-1] ** (-0.5)
    text_scores, layout_scores = page_scores(text_queries, text_keys, layout_queries, layout_keys)
    weights_full = jnp.exp(text_scores + layout_scores - log_total[..., None])
    weights_low = rounded(weights_full)
    text_value_grad = rounded(
        jnp.einsum(
            "hqk,qhd->khd", weights_low, text_context_grad, preferred_element_type=jnp.float32
        )
    )
    layout_value_grad = rounded(
        jnp.einsum(
            "hqk,qhd->khd", weights_low, layout_context_grad, preferred_element_type=jnp.float32
        )
    )
    text_joint = softmax_back(text_context_grad, text_values, weights_full)
    layout_joint = softmax_back(layout_context_grad, layout_values, weights_full)
    text_score_grad = rounded(text_joint)
    layout_score_grad = rounded(text_joint + layout_joint)
    text_query_grad = rounded(
        jnp.einsum("hqk,khd->qhd", text_score_grad, text_keys, preferred_element_type=jnp.float32)
        * text_factor
    )
    text_key_grad = rounded(
        jnp.einsum(
            "hqk,qhd->khd", text_score_grad, text_queries, preferred_element_type=jnp.float32
        )
        * text_factor
    )
    layout_query_grad = rounded(
        jnp.einsum(
            "hqk,khd->qhd", layout_score_grad, layout_keys, preferred_element_type=jnp.float32
        )
        * layout_factor
    )
    layout_key_grad = rounded(
        jnp.einsum(
            "hqk,qhd->khd", layout_score_grad, layout_queries, preferred_element_type=jnp.float32
        )
        * layout_factor
    )
    return (
        text_query_grad,
        text_key_grad,
        text_value_grad,
        layout_query_grad,
        layout_key_grad,
        layout_value_grad,
    )


def feed_forward(rows_all, up_weight, up_bias, down_weight):
    preact = matmul(rows_all, up_weight) + up_bias
    active = rounded(jax.nn.gelu(preact))
    return (preact, active, matmul(active, down_weight))


def feed_backward(rows_all, preact, active, out_grad, up_weight, down_weight):
    active_grad = inner_cols(out_grad, down_weight)
    down_grad = inner_rows(active, out_grad)
    _, gelu_back = jax.vjp(jax.nn.gelu, preact)
    preact_grad = rounded(gelu_back(active_grad)[0])
    up_grad = inner_rows(rows_all, preact_grad)
    return (up_grad, column_sum(preact_grad), down_grad, inner_cols(preact_grad, up_weight))


def projection_grads(
    inputs, query_grad, key_grad, value_grad, query_weight, key_weight, value_weight, residual_grad
):
    input_grad = (
        residual_grad
        + inner_cols(query_grad, query_weight)
        + inner_cols(key_grad, key_weight)
        + inner_cols(value_grad, value_weight)
    )
    weight_grads = (
        inner_rows(inputs, query_grad),
        column_sum(query_grad),
        inner_rows(inputs, key_grad),
        inner_rows(inputs, value_grad),
        column_sum(value_grad),
    )
    return (weight_grads, input_grad)


def on_device(
    text_in,
    layout_in,
    token_mask,
    box_mask,
    cot_text,
    cot_layout,
    text_query_weight,
    text_query_bias,
    text_key_weight,
    text_value_weight,
    text_value_bias,
    text_output_weight,
    text_output_bias,
    text_attend_gain,
    text_attend_shift,
    text_up_weight,
    text_up_bias,
    text_down_weight,
    text_down_bias,
    text_feed_gain,
    text_feed_shift,
    layout_query_weight,
    layout_query_bias,
    layout_key_weight,
    layout_value_weight,
    layout_value_bias,
    layout_output_weight,
    layout_output_bias,
    layout_attend_gain,
    layout_attend_shift,
    layout_up_weight,
    layout_up_bias,
    layout_down_weight,
    layout_down_bias,
    layout_feed_gain,
    layout_feed_shift,
):
    row_count = text_in.shape[0]
    page_count = row_count // PAGE
    text_width = text_in.shape[1]
    layout_width = layout_in.shape[1]

    def by_page(matrix):
        return matrix.reshape(page_count, PAGE, HEADS, matrix.shape[1] // HEADS)

    text_parts = project_three(
        text_in,
        text_query_weight,
        text_query_bias,
        text_key_weight,
        text_value_weight,
        text_value_bias,
    )
    layout_parts = project_three(
        layout_in,
        layout_query_weight,
        layout_query_bias,
        layout_key_weight,
        layout_value_weight,
        layout_value_bias,
    )
    pieces = tuple((by_page(matrix) for matrix in text_parts + layout_parts))
    text_context, layout_context, log_total = lax.map(page_forward, pieces)
    text_context = text_context.reshape(row_count, text_width)
    layout_context = layout_context.reshape(row_count, layout_width)
    text_attend_sum = (
        text_in.astype(jnp.float32) + matmul(text_context, text_output_weight) + text_output_bias
    )
    layout_attend_sum = (
        layout_in.astype(jnp.float32)
        + matmul(layout_context, layout_output_weight)
        + layout_output_bias
    )
    text_hidden = norm_rows(text_attend_sum, text_attend_gain, text_attend_shift)
    layout_hidden = norm_rows(layout_attend_sum, layout_attend_gain, layout_attend_shift)
    text_low = rounded(text_hidden)
    layout_low = rounded(layout_hidden)
    text_all, layout_all = (
        lax.all_gather(text_low, "tensor", axis=0, tiled=True),
        lax.all_gather(layout_low, "tensor", axis=0, tiled=True),
    )
    text_up_full, text_up_bias_full, text_down_full = (
        text_up_weight,
        text_up_bias,
        text_down_weight,
    )
    layout_up_full, layout_up_bias_full, layout_down_full = (
        layout_up_weight,
        layout_up_bias,
        layout_down_weight,
    )
    text_preact, text_active, text_part = feed_forward(
        text_all, text_up_full, text_up_bias_full, text_down_full
    )
    layout_preact, layout_active, layout_part = feed_forward(
        layout_all, layout_up_full, layout_up_bias_full, layout_down_full
    )
    text_feed, layout_feed = (
        lax.psum_scatter(text_part, "tensor", scatter_dimension=0, tiled=True),
        lax.psum_scatter(layout_part, "tensor", scatter_dimension=0, tiled=True),
    )
    text_feed_sum = text_hidden + text_feed + text_down_bias
    layout_feed_sum = layout_hidden + layout_feed + layout_down_bias
    text_out = rounded(norm_rows(text_feed_sum, text_feed_gain, text_feed_shift))
    layout_out = rounded(norm_rows(layout_feed_sum, layout_feed_gain, layout_feed_shift))
    text_cot = cot_text.astype(jnp.float32) * (0.5 + 1.5 * token_mask.astype(jnp.float32))[:, None]
    layout_cot = (
        cot_layout.astype(jnp.float32) * (0.5 + 1.5 * box_mask.astype(jnp.float32))[:, None]
    )
    text_sum_grad, grad_text_feed_gain, grad_text_feed_shift = norm_back(
        text_feed_sum, text_feed_gain, text_feed_shift, text_cot
    )
    layout_sum_grad, grad_layout_feed_gain, grad_layout_feed_shift = norm_back(
        layout_feed_sum, layout_feed_gain, layout_feed_shift, layout_cot
    )
    text_feed_grad = rounded(text_sum_grad)
    layout_feed_grad = rounded(layout_sum_grad)
    grad_text_down_bias = column_sum(text_feed_grad)
    grad_layout_down_bias = column_sum(layout_feed_grad)
    text_grad_all, layout_grad_all = (
        lax.all_gather(text_feed_grad, "tensor", axis=0, tiled=True),
        lax.all_gather(layout_feed_grad, "tensor", axis=0, tiled=True),
    )
    text_ffn = feed_backward(
        text_all, text_preact, text_active, text_grad_all, text_up_full, text_down_full
    )
    layout_ffn = feed_backward(
        layout_all, layout_preact, layout_active, layout_grad_all, layout_up_full, layout_down_full
    )
    text_hidden_part, layout_hidden_part = (
        lax.psum_scatter(text_ffn[3], "tensor", scatter_dimension=0, tiled=True),
        lax.psum_scatter(layout_ffn[3], "tensor", scatter_dimension=0, tiled=True),
    )
    column_local = (
        text_ffn[0],
        text_ffn[1],
        text_ffn[2],
        layout_ffn[0],
        layout_ffn[1],
        layout_ffn[2],
    )
    text_hidden_grad = text_sum_grad + text_hidden_part
    layout_hidden_grad = layout_sum_grad + layout_hidden_part
    text_attend_grad, grad_text_attend_gain, grad_text_attend_shift = norm_back(
        text_attend_sum, text_attend_gain, text_attend_shift, text_hidden_grad
    )
    layout_attend_grad, grad_layout_attend_gain, grad_layout_attend_shift = norm_back(
        layout_attend_sum, layout_attend_gain, layout_attend_shift, layout_hidden_grad
    )
    text_mixed_grad = rounded(text_attend_grad)
    layout_mixed_grad = rounded(layout_attend_grad)
    grad_text_output_bias = column_sum(text_mixed_grad)
    grad_layout_output_bias = column_sum(layout_mixed_grad)
    grad_text_output_weight = inner_rows(text_context, text_mixed_grad)
    grad_layout_output_weight = inner_rows(layout_context, layout_mixed_grad)
    text_context_grad = rounded(inner_cols(text_mixed_grad, text_output_weight))
    layout_context_grad = rounded(inner_cols(layout_mixed_grad, layout_output_weight))
    back_pieces = pieces + (log_total, by_page(text_context_grad), by_page(layout_context_grad))
    paged_grads = lax.map(page_backward, back_pieces)
    (
        text_query_grad,
        text_key_grad,
        text_value_grad,
        layout_query_grad,
        layout_key_grad,
        layout_value_grad,
    ) = [paged.reshape(row_count, paged.shape[2] * paged.shape[3]) for paged in paged_grads]
    text_weight_grads, text_in_grad = projection_grads(
        text_in,
        text_query_grad,
        text_key_grad,
        text_value_grad,
        text_query_weight,
        text_key_weight,
        text_value_weight,
        text_attend_grad,
    )
    layout_weight_grads, layout_in_grad = projection_grads(
        layout_in,
        layout_query_grad,
        layout_key_grad,
        layout_value_grad,
        layout_query_weight,
        layout_key_weight,
        layout_value_weight,
        layout_attend_grad,
    )
    shared = lax.psum(
        (
            text_weight_grads[0],
            text_weight_grads[1],
            text_weight_grads[2],
            text_weight_grads[3],
            text_weight_grads[4],
            grad_text_output_weight,
            grad_text_output_bias,
            grad_text_attend_gain,
            grad_text_attend_shift,
            grad_text_down_bias,
            grad_text_feed_gain,
            grad_text_feed_shift,
            layout_weight_grads[0],
            layout_weight_grads[1],
            layout_weight_grads[2],
            layout_weight_grads[3],
            layout_weight_grads[4],
            grad_layout_output_weight,
            grad_layout_output_bias,
            grad_layout_attend_gain,
            grad_layout_attend_shift,
            grad_layout_down_bias,
            grad_layout_feed_gain,
            grad_layout_feed_shift,
        ),
        ("dp", "tensor"),
    )
    columns = lax.psum(
        (
            column_local[0],
            column_local[1],
            column_local[2],
            column_local[3],
            column_local[4],
            column_local[5],
        ),
        "dp",
    )
    return (
        text_out,
        layout_out,
        text_in_grad,
        layout_in_grad,
        shared[0],
        shared[1],
        shared[2],
        shared[3],
        shared[4],
        shared[5],
        shared[6],
        shared[7],
        shared[8],
        columns[0],
        columns[1],
        columns[2],
        shared[9],
        shared[10],
        shared[11],
        shared[12],
        shared[13],
        shared[14],
        shared[15],
        shared[16],
        shared[17],
        shared[18],
        shared[19],
        shared[20],
        columns[3],
        columns[4],
        columns[5],
        shared[21],
        shared[22],
        shared[23],
    )


def solution(mesh):
    in_specs = (
        P(("dp", "tensor"), None),
        P(("dp", "tensor"), None),
        P(("dp", "tensor")),
        P(("dp", "tensor")),
        P(("dp", "tensor"), None),
        P(("dp", "tensor"), None),
        P(),
        P(),
        P(),
        P(),
        P(),
        P(),
        P(),
        P(),
        P(),
        P(None, "tensor"),
        P("tensor"),
        P("tensor", None),
        P(),
        P(),
        P(),
        P(),
        P(),
        P(),
        P(),
        P(),
        P(),
        P(),
        P(),
        P(),
        P(None, "tensor"),
        P("tensor"),
        P("tensor", None),
        P(),
        P(),
        P(),
    )
    out_specs = (
        P(("dp", "tensor"), None),
        P(("dp", "tensor"), None),
        P(("dp", "tensor"), None),
        P(("dp", "tensor"), None),
        P(),
        P(),
        P(),
        P(),
        P(),
        P(),
        P(),
        P(),
        P(),
        P(None, "tensor"),
        P("tensor"),
        P("tensor", None),
        P(),
        P(),
        P(),
        P(),
        P(),
        P(),
        P(),
        P(),
        P(),
        P(),
        P(),
        P(),
        P(None, "tensor"),
        P("tensor"),
        P("tensor", None),
        P(),
        P(),
        P(),
    )
    return jax.shard_map(
        on_device, mesh=mesh, in_specs=in_specs, out_specs=out_specs, check_vma=False
    )
```

profile of v0, /device:TPU:0, one launch (start us, length us, event | category | flops | bytes accessed | tf_op | source)
XLA Modules:
  0.0 801.9 jit_solution(9276514240543734159)
XLA Ops:
  42.8 31.1 %all-gather.3.cloned.1.call-done = bf16[2048,768]{1,0:T(8,128)(2,1)} async-done(((bf16[512,768]{1,0:T(8,128)(2,1)}), bf16[2048,768]{1,0:T(8,128)(2,1)}) %all-gather.3.cloned.1.call-update) | async-done | bytes 3145744 | tf_op jit(solution)/shard_map/all_gather | solution.py:273
  73.9 8.4 %multiply_convert_fusion = (bf16[2048,768]{1,0:T(8,128)(2,1)S(1)}, f32[2048,768]{1,0:T(8,128)}) fusion(f32[768]{0:T(1024)S(1)} %convert_element_type.258, bf16[2048,768]{1,0:T(8,128)(2,1)} %all-gather.3.cloned.1.call-done, bf16[768,768]{1,0:T(8,128)(2,1)S(1)} %copy-done), kind=kOutput, calls=%fused_computation.24 | convolution fusion | flops 2431647744 | bytes 13765632 | tf_op jit(solution)/shard_map/dot_general | solution.py:18
  83.9 4.5 fusion.81
  94.0 8.7 %all_gather.13 = bf16[2048,192]{0,1:T(8,128)(2,1)S(1)} all-gather(bf16[512,192]{0,1:T(8,128)(2,1)S(1)} %fusion.58), channel_id=1, replica_groups=mesh['dp'=8,'tensor'=4] {'tensor'}, dimensions={0}, use_global_device_ids=true | all-gather | bytes 983040 | tf_op jit(solution)/shard_map/all_gather | solution.py:274
  107.9 39.1 %reduce-scatter.5.cloned.1.call-done = f32[512,768]{1,0:T(8,128)} async-done(((f32[2048,768]{1,0:T(8,128)}), f32[512,768]{1,0:T(8,128)}) %reduce-scatter.5.cloned.1.call-update) | async-done | bytes 1572880 | tf_op jit(solution)/shard_map/reduce_scatter | solution.py:293
  157.7 20.7 %reduce-scatter.7.cloned.1.call-done = f32[512,192]{0,1:T(8,128)} async-done(((f32[2048,192]{0,1:T(8,128)}), f32[512,192]{0,1:T(8,128)}) %reduce-scatter.7.cloned.1.call-update) | async-done | bytes 393232 | tf_op jit(solution)/shard_map/reduce_scatter | solution.py:294
  184.9 11.9 %all_gather.15 = bf16[2048,192]{0,1:T(8,128)(2,1)S(1)} all-gather(bf16[512,192]{0,1:T(8,128)(2,1)S(1)} %get-tuple-element.229), channel_id=1, replica_groups=mesh['dp'=8,'tensor'=4] {'tensor'}, dimensions={0}, use_global_device_ids=true | all-gather | bytes 983040 | tf_op jit(solution)/shard_map/all_gather | solution.py:316
  201.3 9.8 %all-gather.5.cloned.1.call-done = bf16[2048,768]{1,0:T(8,128)(2,1)} async-done(((bf16[512,768]{1,0:T(8,128)(2,1)}), bf16[2048,768]{1,0:T(8,128)(2,1)}) %all-gather.5.cloned.1.call-update) | async-done | bytes 3145744 | tf_op jit(solution)/shard_map/all_gather | solution.py:315
  211.1 9.4 %convert_reduce_fusion = (f32[768]{0:T(1024)}, bf16[2048,768]{1,0:T(8,128)(2,1)S(1)}) fusion(f32[2048,768]{1,0:T(8,128)} %get-tuple-element.257, f32[768]{0:T(1024)} %copy-done.109, bf16[2048,768]{1,0:T(8,128)(2,1)} %all-gather.5.cloned.1.call-done, bf16[768,768]{1,0:T(8,128)(2,1)} %param.53), kind=kOutput, calls=%fused_computation.22 | convolution fusion | flops 2452094208 | bytes 13768704 | tf_op jit(solution)/shard_map/dot_general | solution.py:28
  222.1 4.5 fusion.82
  227.5 15.1 %reduce-scatter.11.cloned.1.call-done = f32[512,192]{0,1:T(8,128)} async-done(((f32[2048,192]{0,1:T(8,128)}), f32[512,192]{0,1:T(8,128)}) %reduce-scatter.11.cloned.1.call-update) | async-done | bytes 393232 | tf_op jit(solution)/shard_map/reduce_scatter | solution.py:326
  247.3 8.1 %convert_reduce_fusion.8 = (f32[12,16]{1,0:T(8,128)}, bf16[12,16,512]{2,1,0:T(8,128)(2,1)S(1)}) fusion(bf16[512,12,16]{0,2,1:T(8,128)(2,1)S(1)} %bitcast.162, f32[12,512,512]{1,2,0:T(8,128)} %copy-done.2, f32[12,512]{1,0:T(8,128)S(1)} %log_add_fusion), kind=kOutput, calls=%fused_computation.102 | convolution fusion | flops 107249472 | bytes 13001472 | tf_op jit(solution)/shard_map/while/body/eval_jaxpr/hqk,qhd->khd/dot_general | solution.py:120
  256.3 6.4 fusion.85
  262.7 40.9 %reduce-scatter.9.cloned.1.call-done = f32[512,768]{1,0:T(8,128)} async-done(((f32[2048,768]{1,0:T(8,128)}), f32[512,768]{1,0:T(8,128)}) %reduce-scatter.9.cloned.1.call-update) | async-done | bytes 1572880 | tf_op jit(solution)/shard_map/reduce_scatter | solution.py:325
  313.5 6.9 convert_reduce_fusion.4
  320.3 9.2 %multiply_reduce_fusion.1 = (f32[12,512]{1,0:T(8,128)S(1)}, f32[12,512,512]{1,2,0:T(8,128)}) fusion(f32[12,512,512]{1,2,0:T(8,128)} %copy-done.2, f32[12,512]{1,0:T(8,128)S(1)} %copy-done.39, bf16[512,12,64]{0,2,1:T(8,128)(2,1)S(1)} %bitcast.145, bf16[512,12,64]{0,2,1:T(8,128)(2,1)S(1)} %bitcast.141), kind=kOutput, calls=%fused_computation.5 | convolution fusion | flops 412084224 | bytes 26787840 | tf_op jit(solution)/shard_map/while/body/eval_jaxpr/qhd,khd->hqk/dot_general | solution.py:89
  329.5 6.9 fusion.3
  340.5 21.9 %fusion.45 = bf16[12,16,512]{2,1,0:T(8,128)(2,1)} fusion(bf16[512,12,16]{0,2,1:T(8,128)(2,1)} %bitcast.167, f32[12,512,512]{1,2,0:T(8,128)} %fusion.85, f32[12,512,512]{1,2,0:T(8,128)} %get-tuple-element.261, f32[12,512,512]{1,2,0:T(8,128)} %copy-done.2, f32[12,512]{1,0:T(8,128)S(1)} %get-tuple-element.260, f32[12,512]{1,0:T(8,128)S(1)} %copy-done.39), kind=kOutput, calls=%fused_computation.85 | convolution fusion | flops 129178112 | bytes 38191104 | tf_op jit(solution)/shard_map/while/body/eval_jaxpr/hqk,qhd->khd/dot_general | solution.py:145
  362.5 25.8 %convert_reduce_fusion.9 = (f32[12,16]{1,0:T(8,128)}, bf16[12,16,512]{2,1,0:T(8,128)(2,1)}) fusion(bf16[512,12,16]{0,2,1:T(8,128)(2,1)S(1)} %bitcast.165, f32[12,512,512]{1,2,0:T(8,128)} %fusion.85, f32[12,512,512]{1,2,0:T(8,128)} %get-tuple-element.261, f32[12,512,512]{1,2,0:T(8,128)} %copy-done.2, f32[12,512]{1,0:T(8,128)S(1)} %get-tuple-element.260, ...), kind=kOutput, calls=%fused_computation.103 | convolution fusion | flops 129374528 | bytes 38191872 | tf_op jit(solution)/shard_map/while/body/eval_jaxpr/hqk,khd->qhd/dot_general | solution.py:139
  402.7 6.6 fusion.88
  414.2 23.9 %all-reduce.2 = (f32[768]{0:T(1024)}, f32[192]{0:T(256)}) all-reduce(f32[768]{0:T(1024)S(1)} %copy-done.108, f32[192]{0:T(256)S(1)} %copy-done.118), channel_id=1, replica_groups=mesh['dp'=8,'tensor'=4] {'dp'}, use_global_device_ids=true, to_apply=%region_40.41 | all-reduce | flops 960 | bytes 7680 | tf_op jit(solution)/shard_map/psum | solution.py:411
  438.4 39.2 %all-reduce = (f32[768]{0:T(1024)}, f32[768]{0:T(1024)}, f32[768]{0:T(1024)}, f32[768]{0:T(1024)}, f32[768]{0:T(1024)}, /*index=5*/f32[768]{0:T(1024)}, f32[768]...) all-reduce(f32[768]{0:T(1024)S(1)} %reduce_sum.379, ...), channel_id=1, replica_groups=mesh['dp'=8,'tensor'=4] {'dp','tensor'}, use_global_device_ids=true, to_apply=%region_26.27 | all-reduce | flops 7680 | bytes 61440 | tf_op jit(solution)/shard_map/psum | solution.py:382
  484.5 115.8 %all-reduce.7.cloned.1.call-done = (f32[768,768]{0,1:T(8,128)}, f32[768,768]{0,1:T(8,128)}, f32[768,768]{0,1:T(8,128)}, f32[768,768]{1,0:T(8,128)}, f32[192,192]...) async-done(((f32[768,768]{0,1:T(8,128)}, f32[768,768]{0,1:T(8,128)}, f32[768,768]{0,1:T(8,128)}, f32[768,768]{1,0:T(8,128)}, ...) | async-done | bytes 10027024 | tf_op jit(solution)/shard_map/psum | solution.py:382
  611.2 174.8 %all-reduce.9.cloned.1.call-done = (f32[768,768]{1,0:T(8,128)}, f32[768,768]{1,0:T(8,128)}, f32[192,192]{1,0:T(8,128)}, f32[192,192]{1,0:T(8,128)}) async-done(((f32[768,768]{1,0:T(8,128)}, f32[768,768]{1,0:T(8,128)}, f32[192,192]{1,0:T(8,128)}, f32[192,192]{1,0:T(8,128)}), (f32[768,768]{1,0:T(8,128)}, f32[768,768]{1,0:T(8,128)}, f32[192,192]{1,0:T(8,128)}, ...) | async-done | bytes 5013520 | tf_op jit(solution)/shard_map/psum | solution.py:411
  (415 shorter events, 136.4 us)
Async XLA Ops:
  7.2 66.6 %copy-start = (bf16[768,768]{1,0:T(8,128)(2,1)S(1)}, bf16[768,768]{1,0:T(8,128)(2,1)}, u32[]{:S(2)}) copy-start(bf16[768,768]{1,0:T(8,128)(2,1)} %param.51) | copy-start | bytes 3538948
  7.2 66.6 %all-gather.3.cloned.1.call-start = ((), (), s32[]{:S(2)}) async-start(), calls=%async_computation.4 | async-start | bytes 3932160 | tf_op jit(solution)/shard_map/all_gather | solution.py:273
  10.0 31.3 %copy-start.72 = (f32[768]{0:T(1024)}, f32[768]{0:T(1024)S(1)}, u32[]{:S(2)}) copy-start(f32[768]{0:T(1024)S(1)} %convert_element_type.256) | copy-start | bytes 9220
  42.5 104.5 %reduce-scatter.5.cloned.1.call-start = ((), (), s32[]{:S(2)}) async-start(), calls=%async_computation.5 | async-start | bytes 7864320 | tf_op jit(solution)/shard_map/reduce_scatter | solution.py:293
  42.8 39.5 %copy-start.109 = (f32[768]{0:T(1024)}, f32[768]{0:T(1024)S(1)}, u32[]{:S(2)}) copy-start(f32[768]{0:T(1024)S(1)} %convert_element_type.258) | copy-start | bytes 9220
  88.4 90.0 %reduce-scatter.7.cloned.1.call-start = ((), (), s32[]{:S(2)}) async-start(), calls=%async_computation.6 | async-start | bytes 1966080 | tf_op jit(solution)/shard_map/reduce_scatter | solution.py:294
  107.2 39.8 %copy-start.73 = (f32[768]{0:T(1024)S(1)}, f32[768]{0:T(1024)}, u32[]{:S(2)}) copy-start(f32[768]{0:T(1024)} %copy-done.72) | copy-start | bytes 9220
  107.2 103.9 %all-gather.5.cloned.1.call-start = ((), (), s32[]{:S(2)}) async-start(), calls=%async_computation.7 | async-start | bytes 3932160 | tf_op jit(solution)/shard_map/all_gather | solution.py:315
  156.0 86.7 %reduce-scatter.11.cloned.1.call-start = ((), (), s32[]{:S(2)}) async-start(), calls=%async_computation.9 | async-start | bytes 1966080 | tf_op jit(solution)/shard_map/reduce_scatter | solution.py:326
  201.2 102.4 %reduce-scatter.9.cloned.1.call-start = ((), (), s32[]{:S(2)}) async-start(), calls=%async_computation.8 | async-start | bytes 7864320 | tf_op jit(solution)/shard_map/reduce_scatter | solution.py:325
  226.8 373.5 %all-reduce.7.cloned.1.call-start = ((), (), s32[]{:S(2)}) async-start(), calls=%async_computation.10 | async-start | bytes 20447232 | tf_op jit(solution)/shard_map/psum | solution.py:382
  256.3 47.3 %copy-start.90 = (f32[512]{0:T(512)S(1)}, f32[512]{0:T(512)}, u32[]{:S(2)}) copy-start(f32[512]{0:T(512)} %copy-done.89) | copy-start | bytes 6148
  262.7 44.2 %copy-start.84 = (f32[512]{0:T(512)S(1)}, f32[512]{0:T(512)}, u32[]{:S(2)}) copy-start(f32[512]{0:T(512)} %copy-done.83) | copy-start | bytes 6148
  362.4 25.8 %copy-start.18 = (bf16[512,768]{1,0:T(8,128)(2,1)S(1)}, bf16[512,768]{1,0:T(8,128)(2,1)}, u32[]{:S(2)}) copy-start(bf16[512,768]{1,0:T(8,128)(2,1)} %param.36) | copy-start | bytes 2359300
  396.6 389.4 %all-reduce.9.cloned.1.call-start = ((), (), s32[]{:S(2)}) async-start(), calls=%async_computation.11 | async-start | bytes 10223616 | tf_op jit(solution)/shard_map/psum | solution.py:411
  413.5 24.9 %copy-start.95 = (f32[768]{0:T(1024)S(1)}, f32[768]{0:T(1024)}, u32[]{:S(2)}) copy-start(f32[768]{0:T(1024)} %get-tuple-element.182) | copy-start | bytes 9220
  413.5 24.9 %copy-start.96 = (f32[768]{0:T(1024)S(1)}, f32[768]{0:T(1024)}, u32[]{:S(2)}) copy-start(f32[768]{0:T(1024)} %get-tuple-element.187) | copy-start | bytes 9220
  413.5 24.9 %copy-start.97 = (f32[768]{0:T(1024)S(1)}, f32[768]{0:T(1024)}, u32[]{:S(2)}) copy-start(f32[768]{0:T(1024)} %get-tuple-element.232) | copy-start | bytes 9220
  413.5 24.9 %copy-start.98 = (f32[768]{0:T(1024)S(1)}, f32[768]{0:T(1024)}, u32[]{:S(2)}) copy-start(f32[768]{0:T(1024)} %get-tuple-element.234) | copy-start | bytes 9220
  413.6 64.0 %copy-start.51 = (bf16[192,192]{1,0:T(8,128)(2,1)S(1)}, bf16[192,192]{1,0:T(8,128)(2,1)}, u32[]{:S(2)}) copy-start(bf16[192,192]{1,0:T(8,128)(2,1)} %param.57) | copy-start | bytes 221188
  413.6 64.0 %copy-start.80 = (f32[512]{0:T(512)S(1)}, f32[512]{0:T(512)}, u32[]{:S(2)}) copy-start(f32[512]{0:T(512)} %copy-done.79) | copy-start | bytes 6148
  413.6 64.2 %copy-start.53 = (bf16[192,192]{1,0:T(8,128)(2,1)S(1)}, bf16[192,192]{1,0:T(8,128)(2,1)}, u32[]{:S(2)}) copy-start(bf16[192,192]{1,0:T(8,128)(2,1)} %param.59) | copy-start | bytes 221188
  413.7 64.4 %copy-start.55 = (bf16[192,192]{1,0:T(8,128)(2,1)S(1)}, bf16[192,192]{1,0:T(8,128)(2,1)}, u32[]{:S(2)}) copy-start(bf16[192,192]{1,0:T(8,128)(2,1)} %param.60) | copy-start | bytes 221188
  607.9 178.2 %copy-start.30 = (f32[768,768]{1,0:T(8,128)S(1)}, f32[768,768]{1,0:T(8,128)}, u32[]{:S(2)}) copy-start(f32[768,768]{1,0:T(8,128)} %get-tuple-element.279) | copy-start | bytes 7077892
  (126 other events, 841.8 us)
Sparse Core Ops, SparseCore 0:
  42.6 31.2 all-gather.2
  88.6 58.3 reduce-scatter.4
  150.2 28.1 reduce-scatter.6
  180.4 30.6 all-gather.4
  214.1 28.5 reduce-scatter.10
  245.2 58.3 reduce-scatter.8
  396.7 203.5 all-reduce.6
  604.9 181.1 all-reduce.8
where the time goes:
time: 811 us; the launch traced here: 802 us
  waiting for transfers between devices  447 us (55%)
  matrix products  169 us (21%)
  blocking collectives  83.7 us (10%)
  local copies, waits for them, and re-layouts  43.7 us (5%)
  other arithmetic  40.8 us (5%)
  between operations  16 us (2%)
    psum x1, waiting for transfers between devices, on_device(): lax.psum((column_local[0], column_local[1], column_local[2], column_local...  175 us
    psum x1, waiting for transfers between devices, on_device(): lax.psum((text_weight_grads[0], text_weight_grads[1], text_weight_grads[2...  116 us
    reduce_scatter x1, waiting for transfers between devices, on_device(): lax.psum_scatter(text_ffn[3], 'tensor', scatter_dimension=0, tiled=True)  40.9 us
    unnamed x296, local copies, waits for them, and re-layouts  40.2 us
    psum x1, blocking collectives, on_device(): lax.psum((text_weight_grads[0], text_weight_grads[1], text_weight_grads[2...  39.2 us
    reduce_scatter x1, waiting for transfers between devices, on_device(): lax.psum_scatter(text_part, 'tensor', scatter_dimension=0, tiled=True)  39.1 us
    all_gather x1, waiting for transfers between devices, on_device(): lax.all_gather(text_low, 'tensor', axis=0, tiled=True)  31.1 us
    dot_general x12, matrix products, inner_rows(): lax.dot_general(first, second, (((0,), (0,)), ((), ())), preferred_elemen...  28 us
  transfers between devices with their start and end apart: 8, of which 8 were waited for; matrix products, arithmetic and copies ran while one was open for 11% of the time, Pallas kernels for 0%

commit v1 on v0

v1 whole, which is shorter than its diff:
```python
import functools

import jax
import jax.numpy as jnp
from jax import lax
from jax.experimental import pallas as pl
from jax.experimental.pallas import tpu as pltpu
from jax.sharding import PartitionSpec as P

HEADS = 12
PAGE = 512
NORM_EPS = 1e-05
MESH = pl.DeviceIdType.MESH
F32 = jnp.float32
BF16 = jnp.bfloat16
TILE = 256
ROWS = 64


def low(values):
    return values.astype(BF16)


def dot(first, second):
    return jnp.dot(first, second, preferred_element_type=F32)


def dot_nt(first, second):
    return lax.dot_general(first, second, (((1,), (1,)), ((), ())), preferred_element_type=F32)


def tile(index, size=TILE):
    return pl.ds(pl.multiple_of(index * size, size), size)


def loop(count, body):
    def step(index, carry):
        body(index)
        return carry

    lax.fori_loop(0, count, step, 0)


def flip(bit):
    return 1 - 2 * bit


def wide(vector_ref):
    return vector_ref[...].astype(F32)[None, :]


def lane_mean(values):
    return jnp.mean(values, axis=-1, keepdims=True)


def row_sum(values):
    return jnp.sum(values, axis=0, keepdims=True)


def normed(values):
    centered = values - lane_mean(values)
    scale = lax.rsqrt(lane_mean(centered * centered) + NORM_EPS)
    return centered * scale, scale


def normed_back(unit, scale, grad):
    return (grad - lane_mean(grad) - unit * lane_mean(grad * unit)) * scale


def padded(rows, unit):
    return -(-rows // unit) * unit


def landing(rows, stages):
    total = 0
    for _ in range(stages):
        rows = rows // 2 if rows % 32 == 0 else rows
        total += rows
    return total


def copy_to(source, target, send, recv, device):
    return pltpu.make_async_remote_copy(
        src_ref=source,
        dst_ref=target,
        send_sem=send,
        recv_sem=recv,
        device_id=device,
        device_id_type=MESH,
    )


def greet(devices):
    barrier = pltpu.get_barrier_semaphore()
    for device in devices:
        pl.semaphore_signal(barrier, inc=1, device_id=device, device_id_type=MESH)
    pl.semaphore_wait(barrier, len(devices))


def mask_column(mask_ref, column_ref):
    scale = 0.5 + 1.5 * mask_ref[...].astype(F32)
    column_ref[...] = jnp.transpose(jnp.broadcast_to(scale, (8, PAGE)))


def head_rows(target, text_rows, layout_rows, pair, side):
    head = 2 * pair + side
    target[side, 128:256, :] = jnp.zeros((128, PAGE), BF16)
    target[side, side * 64 : side * 64 + 64, :] = text_rows[tile(head, 64), :]
    spot = pl.ds(pl.multiple_of(128 + (head % 8) * 16, 16), 16)
    target[side, spot, :] = layout_rows[tile(head, 16), :]


def forward_kernel(shapes, *refs):
    (
        x_ref,
        lx_t_ref,
        token_mask,
        box_mask,
        cot_ref,
        lcot_ref,
        wq,
        bq,
        wk,
        wv,
        bv,
        wo,
        bo,
        attend_gain,
        attend_shift,
        up_hbm,
        up_bias,
        down_hbm,
        down_bias,
        feed_gain,
        feed_shift,
        lwq,
        lbq,
        lwk,
        lwv,
        lbv,
        lwo,
        lbo,
        lattend_gain,
        lattend_shift,
        lup,
        lup_bias,
        ldown,
        ldown_bias,
        lfeed_gain,
        lfeed_shift,
        out_ref,
        lout_ref,
        qn,
        kn,
        vn,
        q_t,
        lqn,
        lkn,
        lvn,
        lq_t,
        lse,
        ctx_t,
        lctx_t,
        asum,
        lasum,
        hidden_grad,
        lhidden_grad,
        grads_up,
        grads_down,
        vec,
        wu,
        wd,
        small,
        small_bias,
        v_t,
        lv_t,
        masked,
        ctx,
        lctx,
        hid,
        lhid,
        hlow,
        lhlow,
        h_t,
        lh_t,
        feed,
        lfeed,
        act,
        lact,
        slope,
        lslope,
        fgrad,
        lfgrad,
        pgrad,
        column,
        lcolumn,
        rises,
        lx,
        lcot,
        lout,
        local_sem,
        send_sem,
        recv_sem,
    ) = refs
    up_rows, down_rows = shapes
    d, me = lax.axis_index("dp"), lax.axis_index("tensor")
    c, x, y = me % 2, me // 2, d % 2
    width, lwidth = x_ref.shape[1], lx_t_ref.shape[0]
    core = (d, me + flip(c))
    across = (d, me + 2 * flip(x))
    beside = (d + flip(y), me)
    other = me + 2 * flip(x)
    half = width // 2
    mine = pl.ds(pl.multiple_of(y * half, half), half)

    small[me, 0:lwidth, 0:lwidth] = lup[...]
    small[me, lwidth : 2 * lwidth, 0:lwidth] = ldown[...]
    for j in range(width // TILE):
        small_bias[me, j : j + 1, :] = wide(up_bias)[:, j * TILE : (j + 1) * TILE]
    small_bias[me, 3:4, 0:lwidth] = wide(lup_bias)

    keep_up = pltpu.make_async_copy(up_hbm, wu.at[me], local_sem.at[0])
    keep_down = pltpu.make_async_copy(down_hbm, wd.at[me], local_sem.at[1])
    keep_up.start()
    keep_down.start()
    greet((core, across, beside))

    def send(index, source, target, device):
        return copy_to(source, target, send_sem.at[index], recv_sem.at[index], device)

    copies = [
        send(0, up_hbm.at[mine], wu.at[me, mine], across),
        send(1, small.at[me], small.at[me], across),
        send(2, small_bias.at[me], small_bias.at[me], across),
        send(3, up_hbm, wu.at[me], core),
        send(4, small.at[me], small.at[me], core),
        send(5, small_bias.at[me], small_bias.at[me], core),
        send(6, down_hbm.at[mine], wd.at[me, mine], across),
        send(7, down_hbm, wd.at[me], core),
        send(8, wu.at[other, mine], wu.at[other, mine], beside),
        send(9, wu.at[other, mine], wu.at[other, mine], core),
        send(10, small.at[other], small.at[other], core),
        send(11, small_bias.at[other], small_bias.at[other], core),
        send(12, wd.at[other, mine], wd.at[other, mine], beside),
        send(13, wd.at[other, mine], wd.at[other, mine], core),
    ]
    rest = pl.ds(pl.multiple_of((1 - y) * half, half), half)
    copies += [
        send(14, wu.at[other, rest], wu.at[other, rest], core),
        send(15, wd.at[other, rest], wd.at[other, rest], core),
    ]
    for copy in copies[:8]:
        copy.start()

    lx[...] = jnp.transpose(lx_t_ref[...])
    lcot[...] = jnp.transpose(lcot_ref[...])
    mask_column(token_mask, column)
    mask_column(box_mask, lcolumn)
    masked[...] = jnp.zeros_like(masked)
    vec[...] = jnp.zeros_like(vec)

    rises[0:1, :] = wide(bq)
    rises[1:2, :] = wide(bv)
    rises[2:3, :] = wide(bo)

    def project(j):
        cols = tile(j)
        rows = x_ref[...]
        queries = low(dot(rows, wq[:, cols]) + rises[0:1, cols]) * 0.125
        qn[:, cols] = queries
        q_t[cols, :] = jnp.transpose(queries)
        kn[:, cols] = low(dot(rows, wk[:, cols]))
        values = low(dot(rows, wv[:, cols]) + rises[1:2, cols])
        vn[:, cols] = values
        v_t[cols, :] = jnp.transpose(values)

    loop(width // TILE, project)
    pad = jnp.zeros((PAGE, 256 - lwidth), BF16)
    rows = lx[...]
    queries = low(dot(rows, lwq[...]) + wide(lbq)) * 0.25
    queries = jnp.concatenate([queries, pad], axis=1)
    lqn[...] = queries
    lq_t[...] = jnp.transpose(queries)
    lkn[...] = jnp.concatenate([low(dot(rows, lwk[...])), pad], axis=1)
    values = low(dot(rows, lwv[...]) + wide(lbv))
    values = jnp.concatenate([values, pad], axis=1)
    lvn[...] = values
    lv_t[...] = jnp.transpose(values)
    lctx_t[...] = jnp.zeros_like(lctx_t)

    def attend(pair):
        keys = jnp.concatenate([kn[:, tile(pair, 128)], lkn[:, tile(pair // 4, 128)]], axis=1)
        for side in range(2):
            head = 2 * pair + side
            head_rows(masked, q_t, lq_t, pair, side)
            joint = dot(keys, masked[side])
            highest = jnp.max(joint, axis=0, keepdims=True)
            exponent = jnp.exp(joint - highest)
            totals = row_sum(exponent)
            weights = low(exponent * (1.0 / totals))
            lse[pl.ds(head, 1), :] = highest + jnp.log(totals)
            values = jnp.concatenate([v_t[tile(head, 64), :], lv_t[tile(head, 16), :]], axis=0)
            context = low(dot(values, weights))
            ctx_t[tile(head, 64), :] = context[0:64]
            lctx_t[tile(head, 16), :] = context[64:80]

    loop(HEADS // 2, attend)
    copies[0].wait_recv()
    copies[8].start()
    copies[9].start()
    copies[1].wait_recv()
    copies[2].wait_recv()
    copies[10].start()
    copies[11].start()

    def untranspose(j):
        ctx[:, tile(j)] = jnp.transpose(ctx_t[tile(j), :])

    loop(width // TILE, untranspose)
    lctx[...] = jnp.transpose(lctx_t[...])

    def mix(j):
        cols = tile(j)
        asum[:, cols] = (
            x_ref[:, cols].astype(F32) + dot(ctx[...], wo[:, cols]) + rises[2:3, cols]
        )

    loop(width // TILE, mix)
    lasum[...] = lx[...].astype(F32) + dot(lctx[:, 0:lwidth], lwo[...]) + wide(lbo)

    def first_norm(source, gain, shift, hidden, hidden_low):
        gain, shift = wide(gain), wide(shift)

        def rows_of(i):
            r = tile(i, ROWS)
            unit, _ = normed(source[r, :])
            value = unit * gain + shift
            hidden[r, :] = value
            hidden_low[r, :] = low(value)

        loop(PAGE // ROWS, rows_of)

    first_norm(asum, attend_gain, attend_shift, hid, hlow)
    first_norm(lasum, lattend_gain, lattend_shift, lhid, lhlow)
    h_t[...] = jnp.transpose(hlow[...])
    lh_t[...] = jnp.transpose(lhlow[...])
    feed[...] = jnp.zeros_like(feed)
    lfeed[...] = jnp.zeros_like(lfeed)

    def shard_at(s):
        return (x + s // 2 - 2 * x * (s // 2)) * 2 + c + s % 2 - 2 * c * (s % 2)

    def gelu(u):
        square = u * u
        inner = 0.7978845608028654 * (u + 0.044715 * (square * u))
        wave = jnp.tanh(inner)
        rise = 0.5 * (1.0 + wave)
        bend = 0.5 * u * (1.0 - wave * wave)
        grow = 0.7978845608028654 * (1.0 + 0.134145 * square)
        return u * rise, rise + bend * grow

    def feed_forward(s):
        t = shard_at(s)

        @pl.when(s == 0)
        def _():
            keep_up.wait()
            keep_down.wait()

        @pl.when(s == 1)
        def _():
            for index in (3, 4, 5, 7):
                copies[index].wait_recv()

        @pl.when(s == 2)
        def _():
            copies[6].wait_recv()
            copies[12].start()
            copies[13].start()
            copies[8].wait_recv()
            copies[14].start()
            copies[12].wait_recv()
            copies[15].start()

        @pl.when(s == 3)
        def _():
            for index in (9, 10, 11, 13, 14, 15):
                copies[index].wait_recv()

        def up(j):
            cols = tile(j)
            preact = dot(hlow[...], wu[t, :, cols]) + small_bias[t, pl.ds(j, 1), :]
            value, gradient = gelu(preact)
            act[s, :, cols] = low(value)
            slope[s, :, cols] = low(gradient)

        loop(width // TILE, up)

        def down(j):
            cols = tile(j)
            feed[:, cols] += dot(act[s], wd[t, :, cols])

        loop(width // TILE, down)
        preact = dot(lhlow[...], small[t, 0:lwidth, 0:lwidth]) + small_bias[t, 3:4, 0:lwidth]
        value, gradient = gelu(preact)
        lact[s] = low(value)
        lslope[s] = low(gradient)
        lfeed[...] += dot(lact[s], small[t, lwidth : 2 * lwidth, 0:lwidth])

    loop(4, feed_forward)

    def second_norm(hidden, fed, bias, gain, shift, cot, scale, out, grad, grad_low):
        bias, gain, shift = wide(bias), wide(gain), wide(shift)

        def rows_of(i, sums):
            r = tile(i, ROWS)
            unit, spread = normed(hidden[r, :] + fed[r, :] + bias)
            out[r, :] = low(unit * gain + shift)
            outer = cot[r, :].astype(F32) * scale[r, 0:1]
            value = normed_back(unit, spread, outer * gain)
            grad[r, :] = value
            rounded = low(value)
            grad_low[r, :] = rounded
            return (
                sums[0] + row_sum(outer * unit),
                sums[1] + row_sum(outer),
                sums[2] + row_sum(rounded.astype(F32)),
            )

        zero = jnp.zeros((1, hidden.shape[1]), F32)
        return lax.fori_loop(0, PAGE // ROWS, rows_of, (zero, zero, zero))

    sums = second_norm(
        hid,
        feed,
        down_bias,
        feed_gain,
        feed_shift,
        cot_ref,
        column,
        out_ref,
        hidden_grad,
        fgrad,
    )
    for i in range(3):
        vec[i : i + 1, :] = sums[i]
    sums = second_norm(
        lhid,
        lfeed,
        ldown_bias,
        lfeed_gain,
        lfeed_shift,
        lcot,
        lcolumn,
        lout,
        lhidden_grad,
        lfgrad,
    )
    lout_ref[...] = jnp.transpose(lout[...])
    for i in range(3):
        vec[7:8, i * 256 : i * 256 + lwidth] = sums[i]

    down_half = down_rows // 2

    def up_place(t):
        return ((t % 2) * 2 + t // 2) * up_rows

    def down_place(t, piece):
        row = piece * 64
        return (
            (t % 2) * 2 * down_rows
            + (row // down_half) * down_rows
            + (t // 2) * down_half
            + row % down_half
        )

    def put_down(t, piece, cols, value):
        spot = pl.ds(pl.multiple_of(down_place(t, piece), 16), 64)
        grads_down[spot, cols] = value

    def feed_backward(s):
        t = shard_at(s)

        def hidden_units(j):
            cols = tile(j)
            active_grad = dot_nt(fgrad[...], wd[t, cols, :])
            value = active_grad * slope[s, :, cols].astype(F32)
            rounded = low(value)
            pgrad[:, cols] = rounded
            vec[pl.ds(3 + t, 1), cols] = row_sum(rounded.astype(F32))
            block = low(dot(jnp.transpose(act[s, :, cols]), fgrad[...]))
            for q in range(TILE // 64):
                put_down(t, j * (TILE // 64) + q, slice(None), block[q * 64 : q * 64 + 64])
            place = pl.ds(pl.multiple_of(up_place(t), 16), width)
            grads_up[place, cols] = low(dot(h_t[...], rounded))

        loop(width // TILE, hidden_units)

        def back(j):
            cols = tile(j)
            hidden_grad[:, cols] += dot_nt(pgrad[...], wu[t, cols, :])

        loop(width // TILE, back)

        active_grad = dot_nt(lfgrad[...], small[t, lwidth : 2 * lwidth, 0:lwidth])
        rounded = low(active_grad * lslope[s].astype(F32))
        spots = ((8, 0), (8, 256), (8, 512), (9, 0))
        for k, (row, lane) in enumerate(spots):

            @pl.when(t == k)
            def _():
                vec[row : row + 1, lane : lane + lwidth] = row_sum(rounded.astype(F32))

        lhidden_grad[...] += dot_nt(rounded, small[t, 0:lwidth, 0:lwidth])
        up_block = low(dot(lh_t[...], rounded))
        down_block = low(dot(jnp.transpose(lact[s]), lfgrad[...]))
        empty = jnp.zeros((64, 256 - lwidth), BF16)
        for which, block in enumerate((up_block, down_block)):
            for q in range(lwidth // 64):
                piece = jnp.concatenate([block[q * 64 : q * 64 + 64], empty], axis=1)
                put_down(t, width // 64 + which, slice(q * 256, q * 256 + 256), piece)

    loop(4, feed_backward)
    for copy in copies:
        copy.wait_send()


class Flow:
    def __init__(self, where, rows, axes, spread, source, base, work, recv, whole, sems):
        self.where, self.rows, self.axes, self.spread = where, rows, axes, spread
        self.source, self.base, self.work, self.recv = source, base, work, recv
        self.whole = whole
        self.halved = []
        for axis in axes:
            if rows % 32 == 0:
                rows //= 2
                self.halved.append(axis)
        self.send_sem, self.recv_sem, self.first = sems
        self.offset, self.size, self.stage = 0, self.rows, 0
        self.place, self.pending, self.sent = 0, None, []
        self.gathers = None

    def span(self, ref, offset, size):
        return ref.at[pl.ds(pl.multiple_of(offset, 16), size)]

    def launch(self, source, target, device):
        index = self.first + len(self.sent)
        copy = copy_to(source, target, self.send_sem.at[index], self.recv_sem.at[index], device)
        copy.start()
        self.sent.append(copy)
        return copy

    def scatter(self):
        bit, device = self.where[self.axes[self.stage]]
        if self.axes[self.stage] in self.halved:
            half = self.size // 2
            kept, given = self.offset + bit * half, self.offset + (1 - bit) * half
        else:
            half, kept, given = self.size, self.offset, self.offset
        outside = self.stage == 0 and self.source is not None
        origin = self.source if outside else self.work
        base = 0 if outside else self.base
        target = self.recv.at[pl.ds(self.place, half)]
        copy = self.launch(self.span(origin, base + given, half), target, device)
        if outside:
            kept = 0
        self.pending = (copy, kept, half)

    def absorb(self):
        copy, kept, half = self.pending
        copy.wait_recv()
        if half == self.size:
            copy.wait_send()
            self.sent[-1] = None
        block = max(b for b in range(16, 129, 16) if half % b == 0)
        place = self.place
        target, start = self.work, self.base + kept
        if self.stage + 1 == len(self.axes):
            target, start = self.whole, 0
            whole = self.whole.shape[0]
            self.gathers = []
            for axis in [a for a in self.spread if a in self.halved]:
                whole //= 2
                bit, _ = self.where[axis]
                start = start + bit * whole
                self.gathers.insert(0, (axis, whole))
            self.spot = start

        def add(i):
            mine = pl.ds(pl.multiple_of(self.base + kept + i * block, 16), block)
            theirs = pl.ds(pl.multiple_of(place + i * block, 16), block)
            result = pl.ds(pl.multiple_of(start + i * block, 16), block)
            target[result, :] = self.work[mine, :] + self.recv[theirs, :]

        loop(half // block, add)
        self.place += half
        self.offset, self.size = kept, half
        self.stage += 1

    def gather(self):
        axis, half = self.gathers.pop(0)
        bit, device = self.where[axis]
        span = self.span(self.whole, self.spot, half)
        copy = self.launch(span, span, device)
        self.pending = (copy, bit, half)

    def advance(self):
        if self.gathers is None:
            if self.stage > 0 or self.pending is not None:
                self.absorb()
            if self.stage < len(self.axes):
                self.scatter()
            else:
                self.gather()
            return
        if self.pending is None:
            return
        copy, bit, half = self.pending
        copy.wait_recv()
        self.pending = None
        self.spot = self.spot - bit * half
        if self.gathers:
            self.gather()

    def done(self):
        return self.gathers is not None and self.pending is None

    def drain(self):
        for copy in self.sent:
            if copy is not None:
                copy.wait_send()


def backward_kernel(plan, *refs):
    (
        x_ref,
        lx_t,
        wq,
        wk,
        wv,
        wo,
        attend_gain,
        lwq,
        lwk,
        lwv,
        lwo,
        lattend_gain,
        qn,
        kn,
        vn,
        q_t,
        lqn,
        lkn,
        lvn,
        lq_t,
        lse,
        ctx_t,
        lctx_t,
        asum,
        lasum,
        hidden_grad,
        lhidden_grad,
        up_hbm,
        down_hbm,
        vec_in,
        in_grad,
        lin_grad,
        up_out,
        down_out,
        shared_out,
        acc_up,
        acc_down,
        recv_up,
        recv_down,
        shared,
        recv_shared,
        sum_up,
        sum_down,
        sum_shared,
        mixed,
        lmixed,
        cgrad,
        cgrad_t,
        lcgrad,
        lcgrad_t,
        k_t,
        lk_t,
        x_t,
        lin,
        masked_q,
        masked_c,
        ldq_t,
        dq,
        dk,
        dv,
        ldq,
        ldk,
        ldv,
        vec,
        local_sem,
        send_sem,
        recv_sem,
    ) = refs
    dp_bits, up_rows, down_rows, shared_flows = plan
    d, me = lax.axis_index("dp"), lax.axis_index("tensor")
    c, x = me % 2, me // 2
    width, lwidth = x_ref.shape[1], lx_t.shape[0]
    where = {"core": (c, (d, me + flip(c))), "x": (x, (d, me + 2 * flip(x)))}
    for k in range(dp_bits):
        bit = (d // 2**k) % 2
        where[k] = (bit, (d + 2**k * flip(bit), me))
    deep = list(range(1, dp_bits))
    x_first, x_later = ["core", "x", 0] + deep, ["core", 0, "x"] + deep
    steps = 2 * (dp_bits + 2)

    keep_up = pltpu.make_async_copy(
        up_hbm.at[pl.ds(pl.multiple_of(c * 2 * up_rows, 16), 2 * up_rows)],
        acc_up,
        local_sem.at[0],
    )
    keep_down = pltpu.make_async_copy(
        down_hbm.at[pl.ds(pl.multiple_of(c * 2 * down_rows, 16), 2 * down_rows)],
        acc_down,
        local_sem.at[1],
    )
    keep_up.start()
    keep_down.start()

    def flow(rows, axes, spread, source, base, work, recv, whole, number):
        sems = (send_sem, recv_sem, number * steps)
        return Flow(where, rows, axes, spread, source, base, work, recv, whole, sems)

    pages = [0] + deep
    up_flow = flow(4 * up_rows, x_first, pages, up_hbm, 0, acc_up, recv_up, sum_up, 0)
    down_flow = flow(
        4 * down_rows, x_later, pages, down_hbm, 0, acc_down, recv_down, sum_down, 1
    )
    shared_list = []
    spot = 0
    for i, (base, rows) in enumerate(shared_flows):
        axes = x_later if i % 2 else x_first
        size = landing(rows, len(axes))
        target, whole = recv_shared.at[pl.ds(spot, size)], sum_shared.at[pl.ds(base, rows)]
        spot += size
        shared_list.append(flow(rows, axes, axes, None, base, shared, target, whole, 2 + i))

    greet([device for _, device in where.values()])
    up_flow.advance()
    down_flow.advance()

    shared[pl.ds(4 * width, shared.shape[0] - 4 * width), :] = jnp.zeros(
        (shared.shape[0] - 4 * width, width), BF16
    )
    masked_q[...] = jnp.zeros_like(masked_q)
    masked_c[...] = jnp.zeros_like(masked_c)
    vec[...] = vec_in[...]

    def norm_grad(source, gain, grad, result, result_low):
        gain = wide(gain)

        def rows_of(i, sums):
            r = tile(i, ROWS)
            unit, spread = normed(source[r, :])
            outer = grad[r, :]
            value = normed_back(unit, spread, outer * gain)
            result[r, :] = value
            rounded = low(value)
            result_low[r, :] = rounded
            return (
                sums[0] + row_sum(rounded.astype(F32)),
                sums[1] + row_sum(outer * unit),
                sums[2] + row_sum(outer),
            )

        zero = jnp.zeros((1, source.shape[1]), F32)
        return lax.fori_loop(0, PAGE // ROWS, rows_of, (zero, zero, zero))

    sums = norm_grad(asum, attend_gain, hidden_grad, in_grad, mixed)
    for i in range(3):
        vec[12 + i : 13 + i, :] = sums[i]
    sums = norm_grad(lasum, lattend_gain, lhidden_grad, lin, lmixed)
    for i in range(3):
        vec[15:16, i * 256 : i * 256 + lwidth] = sums[i]

    def context_back(j):
        cols = tile(j)
        value = low(dot_nt(mixed[...], wo[cols, :]))
        cgrad[:, cols] = value
        cgrad_t[cols, :] = jnp.transpose(value)
        shared[3 * width : 4 * width, cols] = low(dot(ctx_t[...], mixed[:, cols]))
        k_t[cols, :] = jnp.transpose(kn[:, cols])
        x_t[cols, :] = jnp.transpose(x_ref[:, cols])

    loop(width // TILE, context_back)
    pad = jnp.zeros((PAGE, 256 - lwidth), BF16)
    value = jnp.concatenate([low(dot_nt(lmixed[...], lwo[...])), pad], axis=1)
    lcgrad[...] = value
    lcgrad_t[...] = jnp.transpose(value)
    lk_t[...] = jnp.transpose(lkn[...])
    empty = jnp.zeros((64, 256 - lwidth), BF16)

    def put_layout(index, block):
        base = 4 * width + 64 * index
        for q in range(lwidth // 64):
            piece = jnp.concatenate([block[q * 64 : q * 64 + 64], empty], axis=1)
            shared[base : base + 64, q * 256 : q * 256 + 256] = piece

    put_layout(3, low(dot(lctx_t[0:lwidth, :], lmixed[...])))

    keep_up.wait()
    keep_down.wait()
    up_flow.advance()
    down_flow.advance()

    lane = lax.broadcasted_iota(jnp.int32, (PAGE, 128), 1)

    def attend_back(pair):
        text, block = tile(pair, 128), tile(pair // 4, 128)
        keys = jnp.concatenate([kn[:, text], lkn[:, block]], axis=1)
        values = jnp.concatenate([vn[:, text], lvn[:, block]], axis=1)
        grads = jnp.concatenate([cgrad[:, text], lcgrad[:, block]], axis=1)
        found = []
        for side in range(2):
            head = 2 * pair + side
            head_rows(masked_q, q_t, lq_t, pair, side)
            head_rows(masked_c, cgrad_t, lcgrad_t, pair, side)
            weights = jnp.exp(dot(keys, masked_q[side]) - lse[pl.ds(head, 1), :])
            value_grad = dot(low(weights), grads)
            text_wave = dot(vn[:, text], masked_c[side, 0:128, :])
            text_part = row_sum(text_wave * weights)
            text_score = low(weights * (text_wave - text_part))
            both_wave = dot(values, masked_c[side])
            both_part = row_sum(both_wave * weights)
            both_score = low(weights * (both_wave - both_part))
            query_grad = low(dot(k_t[tile(head, 64), :], text_score) * 0.125)
            ldq_t[tile(head, 16), :] = low(dot(lk_t[tile(head, 16), :], both_score) * 0.25)
            key_grad = dot(text_score, qn[:, text])
            lkey_grad = dot(both_score, lqn[:, block])
            own = (lane // 16) == (head % 8)
            ldv[:, block] = jnp.where(own, value_grad[:, 128:256], ldv[:, block])
            ldk[:, block] = jnp.where(own, lkey_grad, ldk[:, block])
            found.append((value_grad[:, 0:128], key_grad, query_grad))
        first = lane < 64
        dv[:, text] = low(jnp.where(first, found[0][0], found[1][0]))
        dk[:, text] = low(jnp.where(first, found[0][1], found[1][1]))
        dq[:, text] = jnp.transpose(jnp.concatenate([found[0][2], found[1][2]], axis=0))

    ldv[...] = jnp.zeros_like(ldv)
    ldk[...] = jnp.zeros_like(ldk)
    ldq_t[...] = jnp.zeros_like(ldq_t)
    loop(HEADS // 2, attend_back)

    up_flow.advance()

    ldq[...] = jnp.transpose(ldq_t[...])

    def project_back(j):
        cols = tile(j)
        shared[0:width, cols] = low(dot(x_t[...], dq[:, cols]))
        shared[width : 2 * width, cols] = low(dot(x_t[...], dk[:, cols]))
        shared[2 * width : 3 * width, cols] = low(dot(x_t[...], dv[:, cols]))
        vec[10:11, cols] = row_sum(dq[:, cols].astype(F32))
        vec[11:12, cols] = row_sum(dv[:, cols].astype(F32))

    loop(width // TILE, project_back)
    query, key, value = ldq[:, 0:lwidth], low(ldk[:, 0:lwidth]), low(ldv[:, 0:lwidth])
    put_layout(0, low(dot(lx_t[...], query)))
    put_layout(1, low(dot(lx_t[...], key)))
    put_layout(2, low(dot(lx_t[...], value)))
    vec[9:10, 256 : 256 + lwidth] = row_sum(query.astype(F32))
    vec[9:10, 512 : 512 + lwidth] = row_sum(value.astype(F32))
    shared[4 * width + 256 : 4 * width + 272, :] = low(vec[...])

    for item in shared_list:
        item.advance()
    down_flow.advance()

    def input_back(j):
        cols = tile(j)
        in_grad[:, cols] += (
            dot_nt(dq[...], wq[cols, :])
            + dot_nt(dk[...], wk[cols, :])
            + dot_nt(dv[...], wv[cols, :])
        )

    loop(width // TILE, input_back)
    lin_grad[...] = jnp.transpose(
        lin[...] + dot_nt(query, lwq[...]) + dot_nt(key, lwk[...]) + dot_nt(value, lwv[...])
    )

    flows = shared_list + [up_flow, down_flow]
    while not all(item.done() for item in flows):
        for item in flows:
            item.advance()
    outs = [
        pltpu.make_async_copy(sum_up, up_out, local_sem.at[2]),
        pltpu.make_async_copy(sum_down, down_out, local_sem.at[3]),
        pltpu.make_async_copy(sum_shared, shared_out, local_sem.at[4]),
    ]
    for copy in outs:
        copy.start()
    for item in flows:
        item.drain()
    for copy in outs:
        copy.wait()


def on_device(dp, tensor, *args):
    (
        text_in,
        layout_in,
        token_mask,
        box_mask,
        cot_text,
        cot_layout,
    ) = args[:6]
    text, layout = args[6:21], args[21:36]
    width, lwidth = text_in.shape[1], layout_in.shape[1]
    dp_bits = dp.bit_length() - 1
    up_rows, down_rows = width, width + 128
    first, second = padded(2 * width, 512), padded(2 * width + 272, 512)
    shared_flows = ((0, first), (first, second))
    shared_total = first + second

    def row(vector):
        return vector.reshape(1, vector.shape[0])

    vmem = pl.BlockSpec(memory_space=pltpu.VMEM)
    hbm = pl.BlockSpec(memory_space=pl.ANY)
    page = PAGE

    def shape(*dims, dtype=BF16):
        return jax.ShapeDtypeStruct(dims, dtype)

    inputs = (text_in, layout_in.T, row(token_mask), row(box_mask), cot_text, cot_layout.T)
    inputs += text + layout
    specs = [vmem] * len(inputs)
    specs[15] = hbm
    specs[17] = hbm
    outs = (
        shape(page, width),
        shape(lwidth, page),
        shape(page, width),
        shape(page, width),
        shape(page, width),
        shape(width, page),
        shape(page, 256),
        shape(page, 256),
        shape(page, 256),
        shape(256, page),
        shape(16, page, dtype=F32),
        shape(width, page),
        shape(256, page),
        shape(page, width, dtype=F32),
        shape(page, lwidth, dtype=F32),
        shape(page, width, dtype=F32),
        shape(page, lwidth, dtype=F32),
        shape(4 * up_rows, width),
        shape(4 * down_rows, width),
        shape(16, width, dtype=F32),
    )
    scratch = [
        pltpu.VMEM((4, width, width), BF16),
        pltpu.VMEM((4, width, width), BF16),
        pltpu.VMEM((4, 2 * lwidth, 256), BF16),
        pltpu.VMEM((4, 8, 256), F32),
        pltpu.VMEM((width, page), BF16),
        pltpu.VMEM((256, page), BF16),
        pltpu.VMEM((2, 256, page), BF16),
        pltpu.VMEM((page, width), BF16),
        pltpu.VMEM((page, 256), BF16),
        pltpu.VMEM((page, width), F32),
        pltpu.VMEM((page, lwidth), F32),
        pltpu.VMEM((page, width), BF16),
        pltpu.VMEM((page, lwidth), BF16),
        pltpu.VMEM((width, page), BF16),
        pltpu.VMEM((lwidth, page), BF16),
        pltpu.VMEM((page, width), F32),
        pltpu.VMEM((page, lwidth), F32),
        pltpu.VMEM((4, page, width), BF16),
        pltpu.VMEM((4, page, lwidth), BF16),
        pltpu.VMEM((4, page, width), BF16),
        pltpu.VMEM((4, page, lwidth), BF16),
        pltpu.VMEM((page, width), BF16),
        pltpu.VMEM((page, lwidth), BF16),
        pltpu.VMEM((page, width), BF16),
        pltpu.VMEM((page, 8), F32),
        pltpu.VMEM((page, 8), F32),
        pltpu.VMEM((8, width), F32),
        pltpu.VMEM((page, lwidth), BF16),
        pltpu.VMEM((page, lwidth), BF16),
        pltpu.VMEM((page, lwidth), BF16),
        pltpu.SemaphoreType.DMA((2,)),
        pltpu.SemaphoreType.DMA((16,)),
        pltpu.SemaphoreType.DMA((16,)),
    ]
    made = pl.pallas_call(
        functools.partial(forward_kernel, (up_rows, down_rows)),
        out_shape=outs,
        in_specs=specs,
        out_specs=[vmem] * len(outs),
        scratch_shapes=scratch,
        compiler_params=pltpu.CompilerParams(
            collective_id=0, has_side_effects=True, vmem_limit_bytes=67043328
        ),
        name="attend_and_feed",
    )(*inputs)
    text_out, layout_out = made[:2]

    inputs = (text_in, layout_in.T)
    inputs += (text[0], text[2], text[3], text[5], text[7])
    inputs += (layout[0], layout[2], layout[3], layout[5], layout[7])
    inputs += tuple(made[2:])
    specs = [vmem] * len(inputs)
    specs[-3] = hbm
    specs[-2] = hbm
    outs = (
        shape(page, width, dtype=F32),
        shape(lwidth, page, dtype=F32),
        shape(up_rows, width),
        shape(down_rows, width),
        shape(shared_total, width),
    )
    count = 2 * (dp_bits + 2) * (2 + len(shared_flows))
    scratch = [
        pltpu.VMEM((2 * up_rows, width), BF16),
        pltpu.VMEM((2 * down_rows, width), BF16),
        pltpu.VMEM((landing(4 * up_rows, dp_bits + 2), width), BF16),
        pltpu.VMEM((landing(4 * down_rows, dp_bits + 2), width), BF16),
        pltpu.VMEM((shared_total, width), BF16),
        pltpu.VMEM((sum(landing(rows, dp_bits + 2) for _, rows in shared_flows), width), BF16),
        pltpu.VMEM((up_rows, width), BF16),
        pltpu.VMEM((down_rows, width), BF16),
        pltpu.VMEM((shared_total, width), BF16),
        pltpu.VMEM((page, width), BF16),
        pltpu.VMEM((page, lwidth), BF16),
        pltpu.VMEM((page, width), BF16),
        pltpu.VMEM((width, page), BF16),
        pltpu.VMEM((page, 256), BF16),
        pltpu.VMEM((256, page), BF16),
        pltpu.VMEM((width, page), BF16),
        pltpu.VMEM((256, page), BF16),
        pltpu.VMEM((width, page), BF16),
        pltpu.VMEM((page, lwidth), F32),
        pltpu.VMEM((2, 256, page), BF16),
        pltpu.VMEM((2, 256, page), BF16),
        pltpu.VMEM((256, page), BF16),
        pltpu.VMEM((page, width), BF16),
        pltpu.VMEM((page, width), BF16),
        pltpu.VMEM((page, width), BF16),
        pltpu.VMEM((page, 256), BF16),
        pltpu.VMEM((page, 256), F32),
        pltpu.VMEM((page, 256), F32),
        pltpu.VMEM((16, width), F32),
        pltpu.SemaphoreType.DMA((5,)),
        pltpu.SemaphoreType.DMA((count,)),
        pltpu.SemaphoreType.DMA((count,)),
    ]
    in_grad, lin_grad, up_sum, down_sum, shared = pl.pallas_call(
        functools.partial(backward_kernel, (dp_bits, up_rows, down_rows, shared_flows)),
        out_shape=outs,
        in_specs=specs,
        out_specs=[vmem, vmem, hbm, hbm, hbm],
        scratch_shapes=scratch,
        compiler_params=pltpu.CompilerParams(
            collective_id=1, has_side_effects=True, vmem_limit_bytes=67043328
        ),
        name="backward_and_reduce",
    )(*inputs)

    me = lax.axis_index("tensor")
    vec = shared[4 * width + 256 : 4 * width + 272].astype(F32)

    def square(index):
        return shared[index * width : (index + 1) * width].astype(F32)

    def unpack(block):
        parts = [block[:, q * 256 : q * 256 + lwidth] for q in range(lwidth // 64)]
        return jnp.concatenate(parts, axis=0).astype(F32)

    def layout_square(index):
        base = 4 * width + 64 * index
        return unpack(shared[base : base + 64])

    def strip(index, part):
        return vec[index, part * 256 : part * 256 + lwidth]

    up_bias = lax.dynamic_index_in_dim(vec, 3 + me, 0, keepdims=False)
    lup_bias = lax.dynamic_index_in_dim(
        jnp.stack([strip(8, 0), strip(8, 1), strip(8, 2), strip(9, 0)]), me, 0, keepdims=False
    )
    return (
        text_out,
        layout_out.T,
        in_grad,
        lin_grad.T,
        square(0),
        vec[10],
        square(1),
        square(2),
        vec[11],
        square(3),
        vec[12],
        vec[13],
        vec[14],
        up_sum[:width].astype(F32),
        up_bias,
        down_sum[:width].astype(F32),
        vec[2],
        vec[0],
        vec[1],
        layout_square(0),
        strip(9, 1),
        layout_square(1),
        layout_square(2),
        strip(9, 2),
        layout_square(3),
        strip(15, 0),
        strip(15, 1),
        strip(15, 2),
        unpack(down_sum[width : width + 64]),
        lup_bias,
        unpack(down_sum[width + 64 : width + 128]),
        strip(7, 2),
        strip(7, 0),
        strip(7, 1),
    )


def solution(mesh):
    rows = P(("dp", "tensor"), None)
    line = P(("dp", "tensor"))
    weights = (P(),) * 9 + (P(None, "tensor"), P("tensor"), P("tensor", None)) + (P(),) * 3
    in_specs = (rows, rows, line, line, rows, rows) + weights + weights
    out_specs = (rows,) * 4 + weights + weights
    return jax.shard_map(
        functools.partial(on_device, mesh.shape["dp"], mesh.shape["tensor"]),
        mesh=mesh,
        in_specs=in_specs,
        out_specs=out_specs,
        check_vma=False,
    )
```

time: 811 us -> 299 us (0.37)
  waiting for transfers between devices: 447 us -> 0 us
  Pallas kernels: 0 us -> 275 us
  matrix products: 169 us -> 0 us
  blocking collectives: 83.7 us -> 0 us
  local copies, waits for them, and re-layouts: 43.7 us -> 5.95 us
  other arithmetic: 40.8 us -> 14.4 us
  between operations: 16 us -> 0.73 us
    psum x2 -> x0, waiting for transfers between devices: 291 us -> none  [the longest x1 175 us: on_device(): lax.psum((column_local[0], column_local[1], column_local[2], column_local...]
    pallas_call x0 -> x2, Pallas kernels: none -> 275 us  [the longest x1 183 us: on_device(): pl.pallas_call(functools.partial(backward_kernel, (dp_bits, up_rows, down...]
    dot_general x48 -> x0, matrix products: 169 us -> none  [the longest x12 28 us: inner_rows(): lax.dot_general(first, second, (((0,), (0,)), ((), ())), preferred_elemen...]
    reduce_scatter x4 -> x0, waiting for transfers between devices: 116 us -> none  [the longest x1 40.9 us: on_device(): lax.psum_scatter(text_ffn[3], 'tensor', scatter_dimension=0, tiled=True)]
    psum x2 -> x0, blocking collectives: 63.1 us -> none  [the longest x1 39.2 us: on_device(): lax.psum((text_weight_grads[0], text_weight_grads[1], text_weight_grads[2...]
    all_gather x2 -> x0, waiting for transfers between devices: 40.9 us -> none  [the longest x1 31.1 us: on_device(): lax.all_gather(text_low, 'tensor', axis=0, tiled=True)]
    unnamed x296 -> x14, local copies, waits for them, and re-layouts: 40.2 us -> 3.55 us
    reduce_sum x18 -> x0, other arithmetic: 23.7 us -> none  [the longest x5 10.7 us: norm_rows(): return centered * lax.rsqrt(variance + NORM_EPS) * gain + shift]
  transfers between devices with their start and end apart: 8 -> 0, of which waited for: 8 -> 0; matrix products, arithmetic and copies ran while one was open for 11% -> 0% of each run, Pallas kernels for 0% -> 0%
where the time goes in v1:
time: 299 us; the launch traced here: 296 us
  Pallas kernels  275 us (92%)
  other arithmetic  14.4 us (5%)
  local copies, waits for them, and re-layouts  5.95 us (2%)
    pallas_call x1, Pallas kernels, on_device(): pl.pallas_call(functools.partial(backward_kernel, (dp_bits, up_rows, down...  183 us
    pallas_call x1, Pallas kernels, on_device(): pl.pallas_call(functools.partial(forward_kernel, (up_rows, down_rows)), o...  91.8 us
    convert_element_type x1, other arithmetic, square(): return shared[index * width:(index + 1) * width].astype(F32)  7.34 us

profile of v1, /device:TPU:0, one launch (start us, length us, event | category | flops | bytes accessed | tf_op | source)
XLA Modules:
  0.0 295.8 jit_solution(13050843244453152406)
XLA Ops:
  0.7 91.8 %attend_and_feed.1 = (bf16[512,768]{1,0:T(8,128)(2,1)}, bf16[192,512]{1,0:T(8,128)(2,1)}, bf16[512,768]{1,0:T(8,128)(2,1)}, bf16[512,768]{1,0:T(8,128)(2,1)}, bf...) custom-call(bf16[512,768]{1,0:T(8,128)(2,1)} %refs_0_.3, ...), custom_call_target="tpu_custom_call" | custom-call | tf_op jit(solution)/shard_map/attend_and_feed/pallas_call | solution.py:997
  92.5 182.9 %backward_and_reduce.1 = (f32[512,768]{1,0:T(8,128)}, f32[192,512]{1,0:T(8,128)}, bf16[768,768]{1,0:T(8,128)(2,1)}, bf16[896,768]{1,0:T(8,128)(2,1)}, bf16[3584,768]{1,0:T(8,128)(2,1)}) custom-call(bf16[512,768]{1,0:T(8,128)(2,1)} %refs_0_.3, bf16[192,512]{1,0:T(8,128)(2,1)} %bitcast.16, bf16[768,768]{1,0:T(8,128)(2,1)} %refs_2_.1, ...), custom_call_target="tpu_custom_call" | custom-call | tf_op jit(solution)/shard_map/backward_and_reduce/pallas_call | solution.py:1059
  275.4 0.0 copy-start.1
  275.4 7.3 %slice_convert_fusion.1 = (f32[768,768]{1,0:T(8,128)}, f32[768,768]{1,0:T(8,128)}, f32[768,768]{1,0:T(8,128)}, f32[768,768]{1,0:T(8,128)}, f32[768,768]{1,0:T(8,128)}) fusion(bf16[3584,768]{1,0:T(8,128)(2,1)} %get-tuple-element.81, bf16[896,768]{1,0:T(8,128)(2,1)} %get-tuple-element.83), kind=kLoop, calls=%fused_computation.1 | loop fusion | flops 2949120 | bytes 17694720 | tf_op jit(solution)/shard_map/convert_element_type | solution.py:1075
  282.8 0.7 slice_convert_fusion.5
  283.5 0.7 slice_reduce_fusion
  284.2 0.0 copy-done.1
  284.2 1.6 convert_element_type.44
  285.7 1.1 fusion.3
  286.9 0.7 maximum_convert_fusion
  287.6 0.6 fusion.5
  288.2 0.7 maximum_convert_fusion.1
  288.9 0.7 maximum_convert_fusion.2
  289.6 0.7 maximum_convert_fusion.3
  290.3 0.7 maximum_convert_fusion.4
  290.9 0.6 fusion.2
  291.5 0.7 maximum_convert_fusion.5
  292.2 0.0 copy-done.2
  292.2 0.9 copy.74
  293.1 0.0 copy-done.4
  293.1 0.7 copy.75
  293.8 1.1 copy.76
  294.9 0.1 copy-done.3
  295.0 0.7 copy.77
  (5 shorter events, 0.0 us)
Async XLA Ops:
  275.4 8.8 %copy-start.1 = (bf16[768,768]{1,0:T(8,128)(2,1)S(1)}, bf16[768,768]{1,0:T(8,128)(2,1)}, u32[]{:S(2)}) copy-start(bf16[768,768]{1,0:T(8,128)(2,1)} %get-tuple-element.82) | copy-start | bytes 3538948
  285.7 6.5 %copy-start.2 = (bf16[512,768]{1,0:T(8,128)(2,1)S(1)}, bf16[512,768]{1,0:T(8,128)(2,1)}, u32[]{:S(2)}) copy-start(bf16[512,768]{1,0:T(8,128)(2,1)} %get-tuple-element.168) | copy-start | bytes 2359300
  287.6 5.5 %copy-start.4 = (bf16[192,512]{1,0:T(8,128)(2,1)S(1)}, bf16[192,512]{1,0:T(8,128)(2,1)}, u32[]{:S(2)}) copy-start(bf16[192,512]{1,0:T(8,128)(2,1)} %get-tuple-element.60) | copy-start | bytes 589828
  288.9 4.9 %copy-start = (f32[512,768]{1,0:T(8,128)S(1)}, f32[512,768]{1,0:T(8,128)}, u32[]{:S(2)}) copy-start(f32[512,768]{1,0:T(8,128)} %get-tuple-element.170) | copy-start | bytes 4718596
  293.8 1.2 copy-start.3

commit v2 on v1

v2 whole, which is shorter than its diff:
```python
import functools

import jax
import jax.numpy as jnp
from jax import lax
from jax.experimental import pallas as pl
from jax.experimental.pallas import tpu as pltpu
from jax.sharding import PartitionSpec as P

HEADS = 12
PAGE = 512
NORM_EPS = 1e-05
MESH = pl.DeviceIdType.MESH
F32 = jnp.float32
BF16 = jnp.bfloat16
TILE = 256
ROWS = 64


def low(values):
    return values.astype(BF16)


def dot(first, second):
    return jnp.dot(first, second, preferred_element_type=F32)


def dot_nt(first, second):
    return lax.dot_general(first, second, (((1,), (1,)), ((), ())), preferred_element_type=F32)


def tile(index, size=TILE):
    return pl.ds(pl.multiple_of(index * size, size), size)


def loop(count, body):
    def step(index, carry):
        body(index)
        return carry

    lax.fori_loop(0, count, step, 0)


def flip(bit):
    return 1 - 2 * bit


def wide(vector_ref):
    return vector_ref[...].astype(F32)[None, :]


def lane_mean(values):
    return jnp.mean(values, axis=-1, keepdims=True)


def row_sum(values):
    return jnp.sum(values, axis=0, keepdims=True)


def normed(values):
    centered = values - lane_mean(values)
    scale = lax.rsqrt(lane_mean(centered * centered) + NORM_EPS)
    return centered * scale, scale


def normed_back(unit, scale, grad):
    return (grad - lane_mean(grad) - unit * lane_mean(grad * unit)) * scale


def landing(rows, stages):
    total = 0
    for stage in range(stages):
        rows = rows // 2 if rows % 32 == 0 and stage + 1 < stages else rows
        total += rows
    return total


def copy_to(source, target, send, recv, device):
    return pltpu.make_async_remote_copy(
        src_ref=source,
        dst_ref=target,
        send_sem=send,
        recv_sem=recv,
        device_id=device,
        device_id_type=MESH,
    )


def greet(devices):
    barrier = pltpu.get_barrier_semaphore()
    for device in devices:
        pl.semaphore_signal(barrier, inc=1, device_id=device, device_id_type=MESH)
    pl.semaphore_wait(barrier, len(devices))


def mask_column(text_mask, layout_mask, column_ref):
    parts = []
    for mask_ref in (text_mask, layout_mask):
        scale = 0.5 + 1.5 * mask_ref[...].astype(F32)
        parts.append(jnp.broadcast_to(scale, (8, PAGE)))
    column_ref[...] = jnp.transpose(jnp.concatenate(parts, axis=0))


def head_rows(target, text_rows, layout_rows, pair, side):
    head = 2 * pair + side
    top = side * 256
    target[top + 128 : top + 256, :] = jnp.zeros((128, PAGE), BF16)
    target[top + side * 64 : top + side * 64 + 64, :] = text_rows[tile(head, 64), :]
    spot = pl.ds(pl.multiple_of(top + 128 + (head % 8) * 16, 16), 16)
    target[spot, :] = layout_rows[tile(head, 16), :]


class Flow:
    def __init__(self, where, axes, spread, rows, give, keep, lands, whole, sems, ready):
        self.steps, self.ready = [], ready
        send_sem, recv_sem, index = sems
        offset, size, place = 0, rows, 0
        halved = []
        for stage, axis in enumerate(axes):
            bit, device = where[axis]
            recv = lands[min(stage, 1)]
            if stage == 1:
                place = 0
            if size % 32 == 0 and stage + 1 < len(axes):
                half = size // 2
                kept, given = offset + bit * half, offset + (1 - bit) * half
                halved.append(axis)
            else:
                half, kept, given = size, offset, offset
            first = stage == 0 and give is not keep
            source = give.at[pl.ds(0, half)] if first else self.span(keep, given, half)
            kept = 0 if first else kept
            copy = copy_to(
                source,
                recv.at[pl.ds(place, half)],
                send_sem.at[index],
                recv_sem.at[index],
                device,
            )
            last = stage + 1 == len(axes)
            target, start = keep, kept
            if last:
                target, start = whole, 0
                step, gathers = whole.shape[0], []
                for other in spread:
                    if other in halved:
                        step //= 2
                        start = start + where[other][0] * step
                        gathers.insert(0, (other, step))
            swap = half == size and not last
            self.steps.append((axis, copy, (keep, kept, recv, place, target, start, half, swap)))
            offset, size = kept, half
            place += half
            index += 1
        spot = start
        for axis, step in gathers:
            bit, device = where[axis]
            span = self.span(whole, spot, step)
            copy = copy_to(span, span, send_sem.at[index], recv_sem.at[index], device)
            self.steps.append((axis, copy, None))
            spot = spot - bit * step
            index += 1

    def span(self, ref, offset, size):
        return ref.at[pl.ds(pl.multiple_of(offset, 16), size)]

    def launch(self, step, waits):
        axis, copy, _ = self.steps[step]
        if waits:
            pl.semaphore_wait(self.ready[axis], 1)
        copy.start()

    def absorb(self, step):
        _, copy, rest = self.steps[step]
        copy.wait_recv()
        if rest is not None:
            keep, kept, recv, place, target, start, half, swap = rest
            if swap:
                copy.wait_send()
            block = max(b for b in range(16, 129, 16) if half % b == 0)

            def add(i):
                mine = pl.ds(pl.multiple_of(kept + i * block, 16), block)
                theirs = pl.ds(pl.multiple_of(place + i * block, 16), block)
                result = pl.ds(pl.multiple_of(start + i * block, 16), block)
                target[result, :] = keep[mine, :] + recv[theirs, :]

            loop(half // block, add)

    def drain(self):
        for _, copy, rest in self.steps[1 if self.ready is None else 0 :]:
            if rest is None or not rest[-1]:
                copy.wait_send()


class Script:
    def __init__(self, flows, greeted):
        self.flows, self.greeted = flows, greeted
        self.started, self.taken = [0] * len(flows), [0] * len(flows)
        self.points = {}

    def write(self, point, number):
        kind, flow = divmod(number, len(self.flows))
        done = self.started if kind else self.taken
        step = done[flow]
        done[flow] += 1
        waits = False
        if kind and self.flows[flow].ready is not None:
            axis = self.flows[flow].steps[step][0]
            waits = axis not in self.greeted
            self.greeted.add(axis)
        self.points.setdefault(point, []).append((kind, flow, step, waits))

    def play(self, point):
        for kind, flow, step, waits in self.points.get(point, ()):
            if kind:
                self.flows[flow].launch(step, waits)
            else:
                self.flows[flow].absorb(step)

    def finish(self, point):
        flows, going = self.flows, True
        while going:
            going = False
            for i, flow in enumerate(flows):
                if self.started[i] > self.taken[i]:
                    self.write(point, i)
                    going = True
                if self.started[i] == self.taken[i] and self.taken[i] < len(flow.steps):
                    self.write(point, len(flows) + i)
                    going = True


def layer_kernel(plan, *refs):
    (
        x_ref,
        lx_t,
        token_mask,
        box_mask,
        cot_ref,
        lcot_ref,
        wq_hbm,
        bq,
        wk_hbm,
        wv_hbm,
        bv,
        wo_hbm,
        bo,
        attend_gain,
        attend_shift,
        up_hbm,
        up_bias,
        down_hbm,
        down_bias,
        feed_gain,
        feed_shift,
        lwq,
        lbq,
        lwk,
        lwv,
        lbv,
        lwo,
        lbo,
        lattend_gain,
        lattend_shift,
        lup,
        lup_bias,
        ldown,
        ldown_bias,
        lfeed_gain,
        lfeed_shift,
        out_ref,
        lout_ref,
        in_grad_out,
        lin_grad,
        sums_out,
        pool,
        acc,
        staging,
        recv,
        sums,
        small,
        small_bias,
        qn,
        kn,
        vn,
        q_t,
        v_t,
        lqn,
        lkn,
        lvn,
        lq_t,
        lv_t,
        lse,
        masked,
        masked_c,
        ctx_t,
        lctx_t,
        lctx,
        asum,
        lasum,
        hlow,
        lhlow,
        h_t,
        lh_t,
        feed,
        lfeed,
        lact,
        lslope,
        column,
        rises,
        lx,
        lcot,
        lcgrad_t,
        ldq_t,
        ldk,
        ldv,
        vec,
        local_sem,
        gather_send,
        gather_recv,
        send_sem,
        recv_sem,
        ready_sem,
    ) = refs
    dp_bits, feed_flows, shared_flows, moves = plan
    fgrad, lfgrad, lout, turned = hlow, lhlow, lx, masked_c
    d, me = lax.axis_index("dp"), lax.axis_index("tensor")
    c, x = me % 2, me // 2
    width, lwidth = x_ref.shape[1], lx_t.shape[0]
    tiles = width // TILE
    where = {"core": (c, (d, me + flip(c))), "x": (x, (d, me + 2 * flip(x)))}
    for k in range(dp_bits):
        bit = (d // 2**k) % 2
        where[k] = (bit, (d + 2**k * flip(bit), me))
    core, across = where["core"][1], where["x"][1]
    y, beside = where[0]
    z, ahead = where[1]
    other = me + 2 * flip(x)

    def part(start, size):
        return pool.at[pl.ds(start, size)]

    wu, wd = part(0, 4 * width), part(4 * width, 4 * width)
    act_at, slope_at = 8 * width, 8 * width + 4 * PAGE
    wq, wk = part(act_at, width), part(act_at + width, width)
    wv, wo = part(act_at + 2 * width, width), part(act_at + 3 * width, width)
    ctx = part(act_at + 4 * width, PAGE)
    shared_rows = sum(rows for rows, _ in shared_flows)
    shared, shared_sum = part(0, shared_rows), part(shared_rows, shared_rows)
    spot = 2 * shared_rows
    dq, dk, dv = part(spot, PAGE), part(spot + PAGE, PAGE), part(spot + 2 * PAGE, PAGE)
    cgrad = part(spot + 3 * PAGE, PAGE)
    x_t = pool.at[pl.ds(spot + 4 * PAGE, width), pl.ds(0, PAGE)]

    def shard_rows(base, t, start=0, size=width):
        return pl.ds(pl.multiple_of(base + t * width + start, 16), size)

    small[me, 0:lwidth, 0:lwidth] = lup[...]
    small[me, lwidth : 2 * lwidth, 0:lwidth] = ldown[...]
    for j in range(tiles):
        small_bias[me, j : j + 1, :] = wide(up_bias)[:, j * TILE : (j + 1) * TILE]
    small_bias[me, 3:4, 0:lwidth] = wide(lup_bias)

    def load(index, source, target):
        copy = pltpu.make_async_copy(source, target, local_sem.at[index])
        copy.start()
        return copy

    loads = [load(i, s, t) for i, (s, t) in enumerate(((wq_hbm, wq), (wk_hbm, wk), (wv_hbm, wv)))]
    load_wo = load(3, wo_hbm, wo)
    keep_up = load(4, up_hbm, pool.at[shard_rows(0, me)])
    keep_down = load(5, down_hbm, pool.at[shard_rows(4 * width, me)])
    greet([device for _, device in where.values()])

    count = [0]

    def send(source, target, device):
        index = count[0]
        count[0] += 1
        return copy_to(source, target, gather_send.at[index], gather_recv.at[index], device)

    def relay(place, device):
        return send(pool.at[place], pool.at[place], device)

    quarter = width // 4
    first = {}
    y_at, z_at = y * quarter, 2 * quarter + z * quarter
    for name, base, hbm in (("up", 0, up_hbm), ("down", 4 * width, down_hbm)):
        for way, start in (("y", y_at), ("z", z_at)):
            source = hbm.at[pl.ds(pl.multiple_of(start, 16), quarter)]
            place = shard_rows(base, me, start, quarter)
            first[name, way] = send(source, pool.at[place], across)
    small_across = [send(ref.at[me], ref.at[me], across) for ref in (small, small_bias)]
    small_core = [send(ref.at[me], ref.at[me], core) for ref in (small, small_bias)]
    up_core = send(up_hbm, pool.at[shard_rows(0, me)], core)
    down_core = send(down_hbm, pool.at[shard_rows(4 * width, me)], core)
    small_relay = [send(ref.at[other], ref.at[other], core) for ref in (small, small_bias)]
    forward, pass_own, pass_got = {}, {}, {}
    for name, base in (("up", 0), ("down", 4 * width)):
        for way, start, rest, device in (
            ("y", y_at, (1 - y) * quarter, beside),
            ("z", z_at, 2 * quarter + (1 - z) * quarter, ahead),
        ):
            own = shard_rows(base, other, start, quarter)
            got = shard_rows(base, other, rest, quarter)
            forward[name, way] = relay(own, device)
            pass_own[name, way] = relay(own, core)
            pass_got[name, way] = relay(got, core)
    gather_all = (
        list(first.values())
        + small_across
        + small_core
        + [up_core, down_core]
        + small_relay
        + list(forward.values())
        + list(pass_own.values())
        + list(pass_got.values())
    )
    first["up", "y"].start()
    first["up", "z"].start()
    for copy in small_across + small_core + [up_core, down_core]:
        copy.start()
    first["down", "y"].start()
    first["down", "z"].start()

    def hand_on(name, way):
        first[name, way].wait_recv()
        forward[name, way].start()
        pass_own[name, way].start()

    def hand_over(name, way):
        forward[name, way].wait_recv()
        pass_got[name, way].start()

    lx[...] = jnp.transpose(lx_t[...])
    lcot[...] = jnp.transpose(lcot_ref[...])
    mask_column(token_mask, box_mask, column)
    masked[...] = jnp.zeros_like(masked)
    vec[...] = jnp.zeros_like(vec)
    rises[0:1, :] = wide(bq)
    rises[1:2, :] = wide(bv)
    rises[2:3, :] = wide(bo)
    for copy in loads:
        copy.wait()

    def project(j):
        cols = tile(j)
        rows = x_ref[...]
        queries = low(dot(rows, wq[:, cols]) + rises[0:1, cols]) * 0.125
        qn[:, cols] = queries
        q_t[cols, :] = jnp.transpose(queries)
        kn[:, cols] = low(dot(rows, wk[:, cols]))
        values = low(dot(rows, wv[:, cols]) + rises[1:2, cols])
        vn[:, cols] = values
        v_t[cols, :] = jnp.transpose(values)

    loop(tiles, project)
    pad = jnp.zeros((PAGE, 256 - lwidth), BF16)
    rows = lx[...]
    queries = low(dot(rows, lwq[...]) + wide(lbq)) * 0.25
    queries = jnp.concatenate([queries, pad], axis=1)
    lqn[...] = queries
    lq_t[...] = jnp.transpose(queries)
    lkn[...] = jnp.concatenate([low(dot(rows, lwk[...])), pad], axis=1)
    values = low(dot(rows, lwv[...]) + wide(lbv))
    values = jnp.concatenate([values, pad], axis=1)
    lvn[...] = values
    lv_t[...] = jnp.transpose(values)
    lctx_t[...] = jnp.zeros_like(lctx_t)

    def attend(pair):
        keys = jnp.concatenate([kn[:, tile(pair, 128)], lkn[:, tile(pair // 4, 128)]], axis=1)
        for side in range(2):
            head = 2 * pair + side
            head_rows(masked, q_t, lq_t, pair, side)
            joint = dot(keys, masked[side * 256 : side * 256 + 256, :])
            highest = jnp.max(joint, axis=0, keepdims=True)
            exponent = jnp.exp(joint - highest)
            totals = row_sum(exponent)
            weights = low(exponent * (1.0 / totals))
            lse[pl.ds(head, 1), :] = highest + jnp.log(totals)
            values = jnp.concatenate([v_t[tile(head, 64), :], lv_t[tile(head, 16), :]], axis=0)
            context = low(dot(values, weights))
            ctx_t[tile(head, 64), :] = context[0:64]
            lctx_t[tile(head, 16), :] = context[64:80]

        @pl.when(pair == 3)
        def _():
            hand_on("up", "y")

    loop(HEADS // 2, attend)

    def untranspose(j):
        ctx[:, tile(j)] = jnp.transpose(ctx_t[tile(j), :])

    loop(tiles, untranspose)
    lctx[...] = jnp.transpose(lctx_t[...])
    load_wo.wait()

    def mix(j):
        cols = tile(j)
        asum[:, cols] = x_ref[:, cols].astype(F32) + dot(ctx[...], wo[:, cols]) + rises[2:3, cols]

    loop(tiles, mix)
    lasum[...] = lx[...].astype(F32) + dot(lctx[:, 0:lwidth], lwo[...]) + wide(lbo)

    def first_norm(source, gain, shift, hidden, hidden_low):
        gain, shift = wide(gain), wide(shift)

        def rows_of(i):
            r = tile(i, ROWS)
            unit, _ = normed(source[r, :])
            value = unit * gain + shift
            hidden[r, :] = value
            hidden_low[r, :] = low(value)

        loop(PAGE // ROWS, rows_of)

    hand_on("up", "z")
    for copy in small_across:
        copy.wait_recv()
    for copy in small_relay:
        copy.start()
    first_norm(asum, attend_gain, attend_shift, feed, hlow)
    first_norm(lasum, lattend_gain, lattend_shift, lfeed, lhlow)
    h_t[...] = jnp.transpose(hlow[...])
    lh_t[...] = jnp.transpose(lhlow[...])

    def shard_at(s):
        return (x + s // 2 - 2 * x * (s // 2)) * 2 + c + s % 2 - 2 * c * (s % 2)

    def page_rows(base, s):
        return pl.ds(pl.multiple_of(base + s * PAGE, PAGE), PAGE)

    def gelu(u):
        square = u * u
        inner = 0.7978845608028654 * (u + 0.044715 * (square * u))
        wave = jnp.tanh(inner)
        rise = 0.5 * (1.0 + wave)
        bend = 0.5 * u * (1.0 - wave * wave)
        grow = 0.7978845608028654 * (1.0 + 0.134145 * square)
        return u * rise, rise + bend * grow

    keep_up.wait()

    def feed_up(s):
        t = shard_at(s)

        @pl.when(s == 1)
        def _():
            up_core.wait_recv()
            for copy in small_core:
                copy.wait_recv()
            hand_over("up", "y")

        @pl.when(s == 2)
        def _():
            hand_on("down", "y")
            hand_over("up", "z")

        @pl.when(s == 3)
        def _():
            for copy in small_relay:
                copy.wait_recv()
            for way in ("y", "z"):
                pass_own["up", way].wait_recv()
                pass_got["up", way].wait_recv()

        def up(j):
            cols = tile(j)
            weights = pool[shard_rows(0, t), cols]
            preact = dot(hlow[...], weights) + small_bias[t, pl.ds(j, 1), :]
            value, gradient = gelu(preact)
            pool[page_rows(act_at, s), cols] = low(value)
            pool[page_rows(slope_at, s), cols] = low(gradient)

        loop(tiles, up)
        preact = dot(lhlow[...], small[t, 0:lwidth, 0:lwidth]) + small_bias[t, 3:4, 0:lwidth]
        value, gradient = gelu(preact)
        lact[s] = low(value)
        lslope[s] = low(gradient)

    loop(4, feed_up)
    keep_down.wait()

    def feed_down(s):
        t = shard_at(s)

        @pl.when(s == 1)
        def _():
            down_core.wait_recv()
            hand_on("down", "z")

        @pl.when(s == 2)
        def _():
            hand_over("down", "y")
            hand_over("down", "z")

        @pl.when(s == 3)
        def _():
            for way in ("y", "z"):
                pass_own["down", way].wait_recv()
                pass_got["down", way].wait_recv()

        def down(j):
            cols = tile(j)
            active = pool[page_rows(act_at, s), :]
            feed[:, cols] += dot(active, pool[shard_rows(4 * width, t), cols])

        loop(tiles, down)
        lfeed[...] += dot(lact[s], small[t, lwidth : 2 * lwidth, 0:lwidth])

    loop(4, feed_down)

    def second_norm(fed, bias, gain, shift, cot, scale, out, grad_low):
        bias, gain, shift = wide(bias), wide(gain), wide(shift)

        def rows_of(i, sums):
            r = tile(i, ROWS)
            unit, spread = normed(fed[r, :] + bias)
            out[r, :] = low(unit * gain + shift)
            outer = cot[r, :].astype(F32) * column[r, scale : scale + 1]
            value = normed_back(unit, spread, outer * gain)
            fed[r, :] = value
            rounded = low(value)
            grad_low[r, :] = rounded
            return (
                sums[0] + row_sum(outer * unit),
                sums[1] + row_sum(outer),
                sums[2] + row_sum(rounded.astype(F32)),
            )

        zero = jnp.zeros((1, fed.shape[1]), F32)
        return lax.fori_loop(0, PAGE // ROWS, rows_of, (zero, zero, zero))

    found = second_norm(
        feed, down_bias, feed_gain, feed_shift, cot_ref, 0, out_ref, fgrad
    )
    for i in range(3):
        vec[i : i + 1, :] = found[i]
    found = second_norm(
        lfeed, ldown_bias, lfeed_gain, lfeed_shift, lcot, 8, lout, lfgrad
    )
    lout_ref[...] = jnp.transpose(lout[...])
    for i in range(3):
        vec[7:8, i * 256 : i * 256 + lwidth] = found[i]

    deep = tuple(range(2, dp_bits))
    flows = []
    index, keep_at, recv_at, sum_at = 0, 0, 2 * sums.shape[0], 0
    places = []
    for rows, order in feed_flows:
        order = order + deep
        depth = order.index("x")
        places.append((keep_at, rows >> depth))
        size = landing(4 * rows, len(order) + 1) - 2 * rows
        lands = recv.at[pl.ds(keep_at, 2 * rows)], recv.at[pl.ds(recv_at, size)]
        flows.append(
            Flow(
                where,
                ("core",) + order,
                [axis for axis in order if axis != "x"],
                4 * rows,
                staging.at[pl.ds(keep_at, 2 * rows)],
                acc.at[pl.ds(keep_at, 2 * rows)],
                lands,
                sums.at[pl.ds(sum_at, rows)],
                (send_sem, recv_sem, index),
                None,
            )
        )
        index += len(flows[-1].steps)
        keep_at += 2 * rows
        recv_at += size
        sum_at += rows
    feed_count = len(flows)
    ready = {axis: ready_sem.at[i] for i, axis in enumerate(where)}
    keep_at, recv_at = 0, 0
    for rows, order in shared_flows:
        order = ("core",) + order + deep
        size = landing(rows, len(order))
        mine = shared.at[pl.ds(keep_at, rows)]
        lands = (
            staging.at[pl.ds(recv_at, rows // 2)],
            staging.at[pl.ds(recv_at + rows // 2, size - rows // 2)],
        )
        flows.append(
            Flow(
                where,
                order,
                order,
                rows,
                mine,
                mine,
                lands,
                shared_sum.at[pl.ds(keep_at, rows)],
                (send_sem, recv_sem, index),
                ready,
            )
        )
        index += len(flows[-1].steps)
        keep_at += rows
        recv_at += size

    script = Script(flows, set())
    last = len(flows) - 1
    made = [("d", i) for i in range(tiles)] + [("up", i) for i in range(tiles)]
    made += [("context", 0)] + [("weight", i) for i in range(tiles)]
    if moves:
        for point, numbers in moves.items():
            for number in numbers:
                script.write(point, number)
    else:
        for i, point in enumerate(made):
            script.write(point, len(flows) + i)
            if point[0] == "up" and i + 1 == 2 * tiles:
                for k in range(feed_count):
                    script.write("sync", k)
        script.write(made[-1], len(flows) + last)
    script.finish("tail")
    act_now = script.play

    def put(number, target, xs, start, block, cols):
        base, grain = places[number]
        size = block.shape[0]
        row = start
        while row < start + size:
            high, inner = row // grain, row % grain
            length = min(grain - inner, start + size - row)
            place = pl.ds(pl.multiple_of(base + high * 2 * grain + xs * grain + inner, 16), length)
            target[place, cols] = block[row - start : row - start + length]
            row += length

    def down_grad(number, first_unit, units):
        def both(g):
            xs = x + g - 2 * x * g
            for parity, target in ((0, acc), (1, staging)):
                s = 2 * g + parity
                unit = pl.ds(first_unit, units)
                turned[0:units, :] = jnp.transpose(pool[page_rows(act_at, s), unit])

                def block(j):
                    cols = tile(j)
                    value = low(dot(turned[0:units, :], fgrad[:, cols]))
                    put(number, target, xs, 0, value, cols)

                loop(tiles, block)

        loop(2, both)

    for i in range(tiles):
        down_grad(i, i * TILE, TILE)
        if i + 1 < tiles:
            act_now(("d", i))
    empty = jnp.zeros((64, 256 - lwidth), BF16)

    def layout_grad(g):
        xs = x + g - 2 * x * g
        for parity, target in ((0, acc), (1, staging)):
            s = 2 * g + parity
            t = shard_at(s)
            active_grad = dot_nt(lfgrad[...], small[t, lwidth : 2 * lwidth, 0:lwidth])
            rounded = low(active_grad * lslope[s].astype(F32))
            total = row_sum(rounded.astype(F32))
            for k, (row, lane) in enumerate(((8, 0), (8, 256), (8, 512), (9, 0))):

                @pl.when(t == k)
                def _():
                    vec[row : row + 1, lane : lane + lwidth] = total

            lfeed[...] += dot_nt(rounded, small[t, 0:lwidth, 0:lwidth])
            up_block = low(dot(lh_t[...], rounded))
            down_block = low(dot(jnp.transpose(lact[s]), lfgrad[...]))
            for which, block in enumerate((up_block, down_block)):
                for q in range(lwidth // 64):
                    piece = jnp.concatenate([block[q * 64 : q * 64 + 64], empty], axis=1)
                    cols = slice(q * 256, q * 256 + 256)
                    put(tiles - 1, target, xs, TILE + 64 * which, piece, cols)

    loop(2, layout_grad)
    act_now(("d", tiles - 1))

    def units_grad(s):
        t = shard_at(s)

        def units(j):
            cols = tile(j)
            place = pl.ds(pl.multiple_of(4 * width + t * width + j * TILE, 16), TILE)
            active_grad = dot_nt(fgrad[...], pool[place, :])
            slope = pool[page_rows(slope_at, s), cols].astype(F32)
            rounded = low(active_grad * slope)
            pool[page_rows(slope_at, s), cols] = rounded
            vec[pl.ds(3 + t, 1), cols] = row_sum(rounded.astype(F32))

        loop(tiles, units)
        for k in range(4):

            @pl.when(s == k)
            def _():
                act_now(("units", k))

    loop(4, units_grad)

    def up_grad(number, start):
        def both(g):
            xs = x + g - 2 * x * g
            for parity, target in ((0, acc), (1, staging)):
                s = 2 * g + parity

                def block(j):
                    cols = tile(j)
                    value = low(
                        dot(h_t[start : start + TILE, :], pool[page_rows(slope_at, s), cols])
                    )
                    put(number, target, xs, 0, value, cols)

                loop(tiles, block)

        loop(2, both)

    for i in range(tiles):
        up_grad(tiles + i, i * TILE)
        act_now(("up", i))

    def hidden_back(s):
        t = shard_at(s)

        def back(j):
            cols = tile(j)
            place = pl.ds(pl.multiple_of(t * width + j * TILE, 16), TILE)
            feed[:, cols] += dot_nt(pool[page_rows(slope_at, s), :], pool[place, :])

        loop(tiles, back)
        for k in range(4):

            @pl.when(s == k)
            def _():
                act_now(("back", k))

    loop(4, hidden_back)
    for copy in gather_all:
        copy.wait_send()
    for item in flows[:feed_count]:
        item.steps[0][1].wait_send()
    for axis, (_, device) in where.items():
        pl.semaphore_signal(
            ready_sem.at[list(where).index(axis)],
            inc=1,
            device_id=device,
            device_id_type=MESH,
        )
    act_now("sync")
    wo_again, wq_again, wk_again, wv_again = (
        recv.at[pl.ds(i * width, width)] for i in range(4)
    )
    again = [
        load(3, wo_hbm, wo_again),
        load(0, wq_hbm, wq_again),
        load(1, wk_hbm, wk_again),
        load(2, wv_hbm, wv_again),
    ]
    mixed, lmixed = fgrad, lfgrad

    def norm_grad(source, gain, grad, grad_low):
        gain = wide(gain)

        def rows_of(i, sums):
            r = tile(i, ROWS)
            unit, spread = normed(source[r, :])
            outer = grad[r, :]
            value = normed_back(unit, spread, outer * gain)
            grad[r, :] = value
            rounded = low(value)
            grad_low[r, :] = rounded
            return (
                sums[0] + row_sum(rounded.astype(F32)),
                sums[1] + row_sum(outer * unit),
                sums[2] + row_sum(outer),
            )

        zero = jnp.zeros((1, source.shape[1]), F32)
        return lax.fori_loop(0, PAGE // ROWS, rows_of, (zero, zero, zero))

    found = norm_grad(asum, attend_gain, feed, mixed)
    for i in range(3):
        vec[12 + i : 13 + i, :] = found[i]
    found = norm_grad(lasum, lattend_gain, lfeed, lmixed)
    for i in range(3):
        vec[15:16, i * 256 : i * 256 + lwidth] = found[i]
    act_now(("norm", 0))
    again[0].wait()
    k_t, lk_t, cgrad_t, lcgrad = v_t, lv_t, h_t, lctx
    masked_c[...] = jnp.zeros_like(masked_c)

    def turn(j):
        x_t[tile(j), :] = jnp.transpose(x_ref[:, tile(j)])

    def context_back(j):
        cols = tile(j)
        value = low(dot_nt(mixed[...], wo_again[cols, :]))
        cgrad[:, cols] = value
        cgrad_t[cols, :] = jnp.transpose(value)
        shared[0:width, cols] = low(dot(ctx_t[...], mixed[:, cols]))
        k_t[cols, :] = jnp.transpose(kn[:, cols])

    loop(tiles, context_back)
    value = jnp.concatenate([low(dot_nt(lmixed[...], lwo[...])), pad], axis=1)
    lcgrad[...] = value
    lcgrad_t[...] = jnp.transpose(value)
    lk_t[...] = jnp.transpose(lkn[...])
    loop(tiles, turn)
    act_now(("context", 0))

    lane = lax.broadcasted_iota(jnp.int32, (PAGE, 128), 1)
    ldv[...] = jnp.zeros_like(ldv)
    ldk[...] = jnp.zeros_like(ldk)
    ldq_t[...] = jnp.zeros_like(ldq_t)

    def attend_back(pair):
        text, block = tile(pair, 128), tile(pair // 4, 128)
        keys = jnp.concatenate([kn[:, text], lkn[:, block]], axis=1)
        values = jnp.concatenate([vn[:, text], lvn[:, block]], axis=1)
        grads = jnp.concatenate([cgrad[:, text], lcgrad[:, block]], axis=1)
        found = []
        for side in range(2):
            head = 2 * pair + side
            head_rows(masked, q_t, lq_t, pair, side)
            head_rows(masked_c, cgrad_t, lcgrad_t, pair, side)
            span = slice(side * 256, side * 256 + 256)
            weights = jnp.exp(dot(keys, masked[span, :]) - lse[pl.ds(head, 1), :])
            value_grad = dot(low(weights), grads)
            text_wave = dot(vn[:, text], masked_c[side * 256 : side * 256 + 128, :])
            text_part = row_sum(text_wave * weights)
            text_score = low(weights * (text_wave - text_part))
            both_wave = dot(values, masked_c[span, :])
            both_part = row_sum(both_wave * weights)
            both_score = low(weights * (both_wave - both_part))
            query_grad = low(dot(k_t[tile(head, 64), :], text_score) * 0.125)
            ldq_t[tile(head, 16), :] = low(dot(lk_t[tile(head, 16), :], both_score) * 0.25)
            key_grad = dot(text_score, qn[:, text])
            lkey_grad = dot(both_score, lqn[:, block])
            own = (lane // 16) == (head % 8)
            ldv[:, block] = jnp.where(own, value_grad[:, 128:256], ldv[:, block])
            ldk[:, block] = jnp.where(own, lkey_grad, ldk[:, block])
            found.append((value_grad[:, 0:128], key_grad, query_grad))
        first_half = lane < 64
        dv[:, text] = low(jnp.where(first_half, found[0][0], found[1][0]))
        dk[:, text] = low(jnp.where(first_half, found[0][1], found[1][1]))
        dq[:, text] = jnp.transpose(jnp.concatenate([found[0][2], found[1][2]], axis=0))
        for k in range(HEADS // 2):

            @pl.when(pair == k)
            def _():
                act_now(("attend", k))

        @pl.when(pair % 2 == 1)
        def _():
            weight_grad(pair // 2)

        for k in range(tiles - 1):

            @pl.when(pair == 2 * k + 1)
            def _():
                act_now(("weight", k))

    def weight_grad(group):
        cols = tile(group)
        place = pl.ds(pl.multiple_of((1 + group) * width, 16), width)
        for i, source in enumerate((dq, dk, dv)):
            shared[place, i * TILE : (i + 1) * TILE] = low(dot(x_t[...], source[:, cols]))
        vec[10:11, cols] = row_sum(dq[:, cols].astype(F32))
        vec[11:12, cols] = row_sum(dv[:, cols].astype(F32))

    loop(HEADS // 2, attend_back)

    query = jnp.transpose(ldq_t[...])[:, 0:lwidth]
    key, value = low(ldk[:, 0:lwidth]), low(ldv[:, 0:lwidth])
    parts = [low(dot(lx_t[...], item)) for item in (query, key, value)]
    parts.append(low(dot(lctx_t[0:lwidth, :], lmixed[...])))
    base = 4 * width
    shared[base : base + lwidth, :] = jnp.concatenate(parts, axis=1)
    vec[9:10, 256 : 256 + lwidth] = row_sum(query.astype(F32))
    vec[9:10, 512 : 512 + lwidth] = row_sum(value.astype(F32))
    base += lwidth
    shared[base : base + 16, :] = low(vec[...])
    shared[base + 16 : shared_rows, :] = jnp.zeros((shared_rows - base - 16, width), BF16)
    act_now(("weight", tiles - 1))
    for copy in again[1:]:
        copy.wait()

    def input_back(j):
        cols = tile(j)
        feed[:, cols] += (
            dot_nt(dq[...], wq_again[cols, :])
            + dot_nt(dk[...], wk_again[cols, :])
            + dot_nt(dv[...], wv_again[cols, :])
        )
        for k in range(tiles):

            @pl.when(j == k)
            def _():
                act_now(("input", k))

    loop(tiles, input_back)
    in_grad_copy = load(4, feed, in_grad_out)
    lin_grad[...] = jnp.transpose(
        lfeed[...] + dot_nt(query, lwq[...]) + dot_nt(key, lwk[...]) + dot_nt(value, lwv[...])
    )
    act_now(("end", 0))
    act_now("tail")
    total = sums.shape[0]
    outs = [
        load(0, sums, sums_out.at[pl.ds(0, total)]),
        load(1, shared_sum, sums_out.at[pl.ds(total, shared_rows)]),
    ]
    for item in flows:
        item.drain()
    for copy in outs + [in_grad_copy]:
        copy.wait()


MOVES = {
    ("d", 0): (11,),
    ("d", 1): (12,),
    ("d", 2): (13, 0, 11, 1, 12),
    ("units", 2): (2, 13),
    ("up", 0): (14,),
    ("up", 1): (15,),
    ("up", 2): (16, 0, 11, 1, 12, 3),
    ("back", 0): (14, 4, 15, 5),
    ("back", 3): (0, 11, 1, 12),
    ("norm", 0): (16, 2, 13, 0, 11),
    ("context", 0): (17, 1, 12, 3, 14, 4),
    ("attend", 0): (15, 0, 11, 6, 17, 2),
    ("attend", 1): (13, 5, 1, 12, 0, 11, 3, 14),
    ("weight", 0): (18, 16, 4, 15),
    ("attend", 2): (1, 12, 2, 13, 7, 3, 6),
    ("attend", 3): (17, 18, 4, 0, 5),
    ("weight", 1): (19,),
    ("attend", 4): (16, 1, 2, 13, 8, 19, 14, 6),
    ("attend", 5): (7, 18, 17),
    ("weight", 2): (20, 21, 15, 2, 5),
    ("input", 0): (16, 8, 19, 7, 18, 9, 20, 3, 10, 21, 6),
    ("input", 1): (17,),
    ("input", 2): (7,),
    ("end", 0): (18, 8, 4),
    "tail": (10, 21, 5, 19, 9, 20, 6, 17, 10, 21, 9, 20, 7, 18, 14, 8, 6, 17, 19, 7, 18, 10, 9, 20, 3, 14, 21, 6, 17, 8, 19, 15, 7, 9, 20, 10, 21, 8, 19, 18, 3, 6, 17, 4, 15, 9, 20, 6, 10, 8, 19, 21, 9, 20, 16, 4, 13, 7, 18, 10, 21, 5, 16, 7, 8, 19, 9, 20, 8, 9, 10, 21, 2, 5, 10),
}
FEED_ORDERS = (("x", 0, 1), (0, "x", 1), (1, "x", 0), (0, "x", 1), ("x", 0, 1), (0, "x", 1))
SHARED_ORDERS = (("x", 0, 1), (1, 0, "x"), ("x", 0, 1), (0, "x", 1), ("x", 0, 1))


def on_device(dp, tensor, *args):
    (
        text_in,
        layout_in,
        token_mask,
        box_mask,
        cot_text,
        cot_layout,
    ) = args[:6]
    text, layout = args[6:21], args[21:36]
    width, lwidth = text_in.shape[1], layout_in.shape[1]
    dp_bits = dp.bit_length() - 1
    half = width // 2
    feed_flows = tuple(zip((TILE, TILE, TILE + 128, TILE, TILE, TILE), FEED_ORDERS))
    shared_flows = tuple(zip((width, width, width, half + 128, half + 128), SHARED_ORDERS))
    moves = MOVES if dp_bits == 3 else {}
    feed_rows = sum(rows for rows, _ in feed_flows)
    shared_rows = sum(rows for rows, _ in shared_flows)
    land = sum(landing(4 * rows, dp_bits + 2) for rows, _ in feed_flows)
    shared_land = sum(landing(rows, dp_bits + 2) for rows, _ in shared_flows)
    pool_rows = max(8 * width + 8 * PAGE, 2 * shared_rows + 4 * PAGE + width)
    count = (2 * dp_bits + 2) * len(feed_flows) + (2 * dp_bits + 4) * len(shared_flows)

    vmem = pl.BlockSpec(memory_space=pltpu.VMEM)
    hbm = pl.BlockSpec(memory_space=pl.ANY)
    page = PAGE

    def shape(*dims, dtype=BF16):
        return jax.ShapeDtypeStruct(dims, dtype)

    def row(vector):
        return vector.reshape(1, vector.shape[0])

    inputs = (text_in, layout_in.T, row(token_mask), row(box_mask), cot_text, cot_layout.T)
    inputs += text + layout
    specs = [vmem] * len(inputs)
    for i in (6, 8, 9, 11, 15, 17):
        specs[i] = hbm
    outs = (
        shape(page, width),
        shape(lwidth, page),
        shape(page, width, dtype=F32),
        shape(lwidth, page, dtype=F32),
        shape(feed_rows + shared_rows, width),
    )
    scratch = [
        pltpu.VMEM((pool_rows, width), BF16),
        pltpu.VMEM((2 * feed_rows, width), BF16),
        pltpu.VMEM((max(2 * feed_rows, shared_land), width), BF16),
        pltpu.VMEM((land, width), BF16),
        pltpu.VMEM((feed_rows, width), BF16),
        pltpu.VMEM((4, 2 * lwidth, 256), BF16),
        pltpu.VMEM((4, 8, 256), F32),
        pltpu.VMEM((page, width), BF16),
        pltpu.VMEM((page, width), BF16),
        pltpu.VMEM((page, width), BF16),
        pltpu.VMEM((width, page), BF16),
        pltpu.VMEM((width, page), BF16),
        pltpu.VMEM((page, 256), BF16),
        pltpu.VMEM((page, 256), BF16),
        pltpu.VMEM((page, 256), BF16),
        pltpu.VMEM((256, page), BF16),
        pltpu.VMEM((256, page), BF16),
        pltpu.VMEM((16, page), F32),
        pltpu.VMEM((512, page), BF16),
        pltpu.VMEM((512, page), BF16),
        pltpu.VMEM((width, page), BF16),
        pltpu.VMEM((256, page), BF16),
        pltpu.VMEM((page, 256), BF16),
        pltpu.VMEM((page, width), F32),
        pltpu.VMEM((page, lwidth), F32),
        pltpu.VMEM((page, width), BF16),
        pltpu.VMEM((page, lwidth), BF16),
        pltpu.VMEM((width, page), BF16),
        pltpu.VMEM((lwidth, page), BF16),
        pltpu.VMEM((page, width), F32),
        pltpu.VMEM((page, lwidth), F32),
        pltpu.VMEM((4, page, lwidth), BF16),
        pltpu.VMEM((4, page, lwidth), BF16),
        pltpu.VMEM((page, 16), F32),
        pltpu.VMEM((8, width), F32),
        pltpu.VMEM((page, lwidth), BF16),
        pltpu.VMEM((page, lwidth), BF16),
        pltpu.VMEM((256, page), BF16),
        pltpu.VMEM((256, page), BF16),
        pltpu.VMEM((page, 256), F32),
        pltpu.VMEM((page, 256), F32),
        pltpu.VMEM((16, width), F32),
        pltpu.SemaphoreType.DMA((6,)),
        pltpu.SemaphoreType.DMA((24,)),
        pltpu.SemaphoreType.DMA((24,)),
        pltpu.SemaphoreType.DMA((count,)),
        pltpu.SemaphoreType.DMA((count,)),
        pltpu.SemaphoreType.REGULAR((dp_bits + 2,)),
    ]
    text_out, layout_out, in_grad, lin_grad, sums = pl.pallas_call(
        functools.partial(layer_kernel, (dp_bits, feed_flows, shared_flows, moves)),
        out_shape=outs,
        in_specs=specs,
        out_specs=[vmem, vmem, hbm, vmem, hbm],
        scratch_shapes=scratch,
        compiler_params=pltpu.CompilerParams(
            collective_id=0, has_side_effects=True, vmem_limit_bytes=67043328
        ),
        name="layer",
    )(*inputs)

    me = lax.axis_index("tensor")
    shared = sums[feed_rows:]
    at = 4 * width
    packed = shared[at : at + lwidth].astype(F32)
    vec = shared[at + lwidth : at + lwidth + 16].astype(F32)

    def square(index):
        parts = [
            shared[(1 + g) * width : (2 + g) * width, index * TILE : (index + 1) * TILE]
            for g in range(width // TILE)
        ]
        return jnp.concatenate(parts, axis=1).astype(F32)

    def unpack(block):
        parts = [block[:, q * 256 : q * 256 + lwidth] for q in range(lwidth // 64)]
        return jnp.concatenate(parts, axis=0).astype(F32)

    def layout_square(index):
        return packed[:, index * lwidth : (index + 1) * lwidth]

    def strip(index, part):
        return vec[index, part * 256 : part * 256 + lwidth]

    up_bias = lax.dynamic_index_in_dim(vec, 3 + me, 0, keepdims=False)
    lup_bias = lax.dynamic_index_in_dim(
        jnp.stack([strip(8, 0), strip(8, 1), strip(8, 2), strip(9, 0)]), me, 0, keepdims=False
    )
    return (
        text_out,
        layout_out.T,
        in_grad,
        lin_grad.T,
        square(0),
        vec[10],
        square(1),
        square(2),
        vec[11],
        shared[0:width].astype(F32),
        vec[12],
        vec[13],
        vec[14],
        sums[width + 128 : 2 * width + 128].astype(F32),
        up_bias,
        sums[0:width].astype(F32),
        vec[2],
        vec[0],
        vec[1],
        layout_square(0),
        strip(9, 1),
        layout_square(1),
        layout_square(2),
        strip(9, 2),
        layout_square(3),
        strip(15, 0),
        strip(15, 1),
        strip(15, 2),
        unpack(sums[width : width + 64]),
        lup_bias,
        unpack(sums[width + 64 : width + 128]),
        strip(7, 2),
        strip(7, 0),
        strip(7, 1),
    )


def solution(mesh):
    rows = P(("dp", "tensor"), None)
    line = P(("dp", "tensor"))
    weights = (P(),) * 9 + (P(None, "tensor"), P("tensor"), P("tensor", None)) + (P(),) * 3
    in_specs = (rows, rows, line, line, rows, rows) + weights + weights
    out_specs = (rows,) * 4 + weights + weights
    return jax.shard_map(
        functools.partial(on_device, mesh.shape["dp"], mesh.shape["tensor"]),
        mesh=mesh,
        in_specs=in_specs,
        out_specs=out_specs,
        check_vma=False,
    )
```

time: 299 us -> 207 us (0.69); the launches traced: 296 us -> 207 us
  Pallas kernels: 275 us -> 186 us
    pallas_call x2 -> x1, Pallas kernels: 275 us -> 186 us  [on_device(): pl.pallas_call(functools.partial(layer_kernel, (dp_bits, feed_flows, shar...]
    convert_element_type x6 -> x1, other arithmetic: 4.14 us -> 0.77 us  [unpack(): return jnp.concatenate(parts, axis=0).astype(F32)]
    slice x0 -> x2, local copies, waits for them, and re-layouts: none -> 3.2 us  [the longest x1 2.22 us: square(): shared[(1 + g) * width:(2 + g) * width, index * TILE:(index + 1) * TILE]]
    convert_element_type x3 -> x4, other arithmetic: 9.66 us -> 10.1 us  [the longest x1 5.83 us: on_device(): sums[0:width].astype(F32)]
where the time goes in v2:
time: 207 us
  Pallas kernels  186 us (90%)
  other arithmetic  11.5 us (6%)
  local copies, waits for them, and re-layouts  8.89 us (4%)
    pallas_call x1, Pallas kernels, on_device(): pl.pallas_call(functools.partial(layer_kernel, (dp_bits, feed_flows, shar...  186 us
    convert_element_type x1, other arithmetic, on_device(): sums[0:width].astype(F32)  5.83 us

profile of v2, /device:TPU:0, one launch (start us, length us, event | category | flops | bytes accessed | tf_op | source)
XLA Modules:
  0.0 206.8 jit_solution(4199693316473334200)
XLA Ops:
  0.7 185.7 %layer.1 = (bf16[512,768]{1,0:T(8,128)(2,1)}, bf16[192,512]{1,0:T(8,128)(2,1)}, f32[512,768]{1,0:T(8,128)}, f32[192,512]{1,0:T(8,128)}, bf16[4992,768]{1,0:T(8,128)(2,1)}) custom-call(bf16[512,768]{1,0:T(8,128)(2,1)} %refs_0_.1, bf16[192,512]{1,0:T(8,128)(2,1)} %bitcast.17, s32[1,512]{1,0:T(1,128)} %bitcast.19, s32[1,512]{1,0:T(1,128)} %bitcast.20, ...), custom_call_target="tpu_custom_call" | custom-call | tf_op jit(solution)/shard_map/layer/pallas_call | solution.py:1149
  186.4 0.7 slice_convert_fusion.4
  187.1 0.6 fusion.6
  187.7 0.7 slice_reduce_fusion
  188.4 0.6 fusion.2
  189.0 0.9 fusion.3
  189.8 0.8 maximum_convert_fusion.3
  190.6 1.0 slice_convert_fusion.3
  191.6 1.0 fusion.5
  192.6 2.2 %fusion.4 = (bf16[768,256]{1,0:T(8,128)(2,1)S(1)}, bf16[768,256]{1,0:T(8,128)(2,1)S(1)}, bf16[768,256]{1,0:T(8,128)(2,1)S(1)}, bf16[768,256]{1,0:T(8,128)(2,1)S(...) fusion(bf16[4992,768]{1,0:T(8,128)(2,1)} %get-tuple-element.43), kind=kLoop, calls=%fused_computation.27 | loop fusion | bytes 7077888 | tf_op jit(solution)/shard_map/slice | solution.py:1169
  194.8 5.8 %slice_convert_fusion = (f32[768,768]{1,0:T(8,128)}, f32[768,768]{1,0:T(8,128)}, f32[768,768]{1,0:T(8,128)}, f32[768,768]{1,0:T(8,128)}) fusion(bf16[4992,768]{1,0:T(8,128)(2,1)} %get-tuple-element.43, bf16[768,256]{1,0:T(8,128)(2,1)S(1)} %get-tuple-element.63, bf16[768,256]{1,0:T(8,128)(2,1)S(1)} %get-tuple-element.64, bf16[768,256]{1,0:T(8,128)(2,1)S(1)} %get-tuple-element.62), kind=kLoop, calls=%fused_computation.3 | loop fusion | flops 5308416 | bytes 14155776 | tf_op jit(solution)/shard_map/convert_element_type | solution.py:1204
  200.6 0.0 copy-start.1
  200.6 0.0 copy-start.3
  200.7 2.5 %maximum_convert_fusion = (f32[768,768]{1,0:T(8,128)}, f32[768,768]{1,0:T(8,128)}) fusion(bf16[768,256]{1,0:T(8,128)(2,1)S(1)} %get-tuple-element.68, bf16[768,256]{1,0:T(8,128)(2,1)S(1)} %get-tuple-element.69, bf16[768,256]{1,0:T(8,128)(2,1)S(1)} %get-tuple-element.70, bf16[768,256]{1,0:T(8,128)(2,1)S(1)} %get-tuple-element.65, ...), kind=kLoop, calls=%fused_computation | loop fusion | flops 7077888 | bytes 7077888 | tf_op jit(solution)/shard_map/convert_element_type | solution.py:1172
  203.2 0.0 copy-start
  203.2 0.0 copy-done.1
  203.2 0.0 copy-start.2
  203.2 0.9 copy.74
  204.1 0.0 copy-done.3
  204.1 0.7 copy.75
  204.8 0.1 copy-done
  204.9 1.1 copy.76
  206.0 0.0 copy-done.2
  206.0 0.7 copy.77
Async XLA Ops:
  200.6 2.6 %copy-start.1 = (bf16[512,768]{1,0:T(8,128)(2,1)S(1)}, bf16[512,768]{1,0:T(8,128)(2,1)}, u32[]{:S(2)}) copy-start(bf16[512,768]{1,0:T(8,128)(2,1)} %get-tuple-element.126) | copy-start | bytes 2359300
  200.6 3.4 %copy-start.3 = (bf16[192,512]{1,0:T(8,128)(2,1)S(1)}, bf16[192,512]{1,0:T(8,128)(2,1)}, u32[]{:S(2)}) copy-start(bf16[192,512]{1,0:T(8,128)(2,1)} %get-tuple-element.40) | copy-start | bytes 589828
  203.2 1.7 copy-start
  203.2 2.8 %copy-start.2 = (f32[192,512]{1,0:T(8,128)S(1)}, f32[192,512]{1,0:T(8,128)}, u32[]{:S(2)}) copy-start(f32[192,512]{1,0:T(8,128)} %get-tuple-element.42) | copy-start | bytes 1179652

commit v3 on v2

--- a/solution.py
+++ b/solution.py
@@ -14,7 +14,10 @@
 F32 = jnp.float32
 BF16 = jnp.bfloat16
 TILE = 256
-ROWS = 64
+ROWS = 128
+CORE, ACROSS = 100, 101
+SETUP, PROJECT, LAYOUT, HEAD, MIX, FIRST, FEED, FED, DOWN, DONE = range(10)
+D, UNITS, UP, BACK, NORM, CONTEXT, ATTEND, WEIGHT, INPUT, END, TAIL, SYNC = range(10, 22)
 
 
 def low(values):
@@ -38,7 +41,7 @@
         body(index)
         return carry
 
-    lax.fori_loop(0, count, step, 0)
+    lax.fori_loop(0, count, step, 0, unroll=count if count < 4 else 1)
 
 
 def flip(bit):
@@ -111,8 +114,9 @@
 
 
 class Flow:
-    def __init__(self, where, axes, spread, rows, give, keep, lands, whole, sems, ready):
+    def __init__(self, where, axes, spread, rows, give, keep, lands, whole, sems, ready, result):
         self.steps, self.ready = [], ready
+        self.result = pltpu.make_async_copy(whole, *result)
         send_sem, recv_sem, index = sems
         offset, size, place = 0, rows, 0
         halved = []
@@ -186,8 +190,11 @@
                 target[result, :] = keep[mine, :] + recv[theirs, :]
 
             loop(half // block, add)
+        if step + 1 == len(self.steps):
+            self.result.start()
 
     def drain(self):
+        self.result.wait()
         for _, copy, rest in self.steps[1 if self.ready is None else 0 :]:
             if rest is None or not rest[-1]:
                 copy.wait_send()
@@ -292,13 +299,11 @@
         lq_t,
         lv_t,
         lse,
-        masked,
-        masked_c,
+        masks,
         ctx_t,
         lctx_t,
         lctx,
         asum,
-        lasum,
         hlow,
         lhlow,
         h_t,
@@ -321,19 +326,22 @@
         gather_recv,
         send_sem,
         recv_sem,
+        out_sem,
         ready_sem,
     ) = refs
     dp_bits, feed_flows, shared_flows, moves = plan
-    fgrad, lfgrad, lout, turned = hlow, lhlow, lx, masked_c
+    fgrad, lfgrad, lout, lasum = hlow, lhlow, lx, ldk
+    masked, masked_c = masks.at[pl.ds(0, 512)], masks.at[pl.ds(512, 512)]
+    fgrad_t = masks.at[pl.ds(0, x_ref.shape[1])]
     d, me = lax.axis_index("dp"), lax.axis_index("tensor")
     c, x = me % 2, me // 2
     width, lwidth = x_ref.shape[1], lx_t.shape[0]
     tiles = width // TILE
-    where = {"core": (c, (d, me + flip(c))), "x": (x, (d, me + 2 * flip(x)))}
+    where = {CORE: (c, (d, me + flip(c))), ACROSS: (x, (d, me + 2 * flip(x)))}
     for k in range(dp_bits):
         bit = (d // 2**k) % 2
         where[k] = (bit, (d + 2**k * flip(bit), me))
-    core, across = where["core"][1], where["x"][1]
+    core, across = where[CORE][1], where[ACROSS][1]
     y, beside = where[0]
     z, ahead = where[1]
     other = me + 2 * flip(x)
@@ -373,76 +381,77 @@
     keep_down = load(5, down_hbm, pool.at[shard_rows(4 * width, me)])
     greet([device for _, device in where.values()])
 
-    count = [0]
-
-    def send(source, target, device):
-        index = count[0]
-        count[0] += 1
-        return copy_to(source, target, gather_send.at[index], gather_recv.at[index], device)
-
-    def relay(place, device):
-        return send(pool.at[place], pool.at[place], device)
-
-    quarter = width // 4
-    first = {}
-    y_at, z_at = y * quarter, 2 * quarter + z * quarter
-    for name, base, hbm in (("up", 0, up_hbm), ("down", 4 * width, down_hbm)):
-        for way, start in (("y", y_at), ("z", z_at)):
-            source = hbm.at[pl.ds(pl.multiple_of(start, 16), quarter)]
-            place = shard_rows(base, me, start, quarter)
-            first[name, way] = send(source, pool.at[place], across)
-    small_across = [send(ref.at[me], ref.at[me], across) for ref in (small, small_bias)]
-    small_core = [send(ref.at[me], ref.at[me], core) for ref in (small, small_bias)]
-    up_core = send(up_hbm, pool.at[shard_rows(0, me)], core)
-    down_core = send(down_hbm, pool.at[shard_rows(4 * width, me)], core)
-    small_relay = [send(ref.at[other], ref.at[other], core) for ref in (small, small_bias)]
-    forward, pass_own, pass_got = {}, {}, {}
-    for name, base in (("up", 0), ("down", 4 * width)):
-        for way, start, rest, device in (
-            ("y", y_at, (1 - y) * quarter, beside),
-            ("z", z_at, 2 * quarter + (1 - z) * quarter, ahead),
-        ):
-            own = shard_rows(base, other, start, quarter)
-            got = shard_rows(base, other, rest, quarter)
-            forward[name, way] = relay(own, device)
-            pass_own[name, way] = relay(own, core)
-            pass_got[name, way] = relay(got, core)
-    gather_all = (
-        list(first.values())
-        + small_across
-        + small_core
-        + [up_core, down_core]
-        + small_relay
-        + list(forward.values())
-        + list(pass_own.values())
-        + list(pass_got.values())
-    )
-    first["up", "y"].start()
-    first["up", "z"].start()
-    for copy in small_across + small_core + [up_core, down_core]:
-        copy.start()
-    first["down", "y"].start()
-    first["down", "z"].start()
-
-    def hand_on(name, way):
-        first[name, way].wait_recv()
-        forward[name, way].start()
-        pass_own[name, way].start()
-
-    def hand_over(name, way):
-        forward[name, way].wait_recv()
-        pass_got[name, way].start()
+    messages, needs = [], []
+
+    def message(source, target, device, *after):
+        index = len(messages)
+        copy = copy_to(source, target, gather_send.at[index], gather_recv.at[index], device)
+        messages.append(copy)
+        needs.append(set(after))
+
+    for base, hbm in ((0, up_hbm), (4 * width, down_hbm)):
+        grain = width // 12
+        zero = len(messages)
+
+        def relay(start, size, device, *after):
+            place = pool.at[shard_rows(base, other, start * grain, size * grain)]
+            message(place, place, device, *(zero + item for item in after))
+
+        own = (y, 2 + z, 4 + 2 * z + y, 8 + 2 * y + z)
+        for start in own:
+            source = hbm.at[pl.ds(pl.multiple_of(start * grain, 16), grain)]
+            message(source, pool.at[shard_rows(base, me, start * grain, grain)], across)
+        relay(own[0], 1, beside, 0)
+        relay(own[1], 1, ahead, 1)
+        relay(own[2], 1, beside, 2)
+        relay(4 + 2 * z, 2, ahead, 2, 6)
+        relay(own[3], 1, ahead, 3)
+        relay(8 + 2 * y, 2, beside, 3, 8)
+        relay(own[0], 1, core, 0)
+        relay(1 - y, 1, core, 4)
+        relay(own[1], 1, core, 1)
+        relay(3 - z, 1, core, 5)
+        relay(4 + 2 * z, 2, core, 2, 6)
+        relay(6 - 2 * z, 2, core, 7)
+        relay(8 + 2 * y, 2, core, 3, 8)
+        relay(10 - 2 * y, 2, core, 9)
+        message(hbm, pool.at[shard_rows(base, me)], core)
+    for ref in (small, small_bias):
+        message(ref.at[me], ref.at[me], across)
+        message(ref.at[me], ref.at[me], core)
+        message(ref.at[other], ref.at[other], core, len(messages) - 2)
+    begun, got = set(START), set()
+    for index in START:
+        messages[index].start()
+
+    def take(stage, k=0):
+        for index in GATHER.get((stage, k), ()):
+            messages[index].wait_recv()
+            got.add(index)
+            for later, after in enumerate(needs):
+                if later not in begun and after <= got:
+                    messages[later].start()
+                    begun.add(later)
+
+    def take_at(index, stage):
+        for k in range(8):
+            if (stage, k) in GATHER:
+
+                @pl.when(index == k)
+                def _():
+                    take(stage, k)
 
     lx[...] = jnp.transpose(lx_t[...])
     lcot[...] = jnp.transpose(lcot_ref[...])
     mask_column(token_mask, box_mask, column)
-    masked[...] = jnp.zeros_like(masked)
+    masks[...] = jnp.zeros_like(masks)
     vec[...] = jnp.zeros_like(vec)
     rises[0:1, :] = wide(bq)
     rises[1:2, :] = wide(bv)
     rises[2:3, :] = wide(bo)
     for copy in loads:
         copy.wait()
+    take(SETUP)
 
     def project(j):
         cols = tile(j)
@@ -454,6 +463,7 @@
         values = low(dot(rows, wv[:, cols]) + rises[1:2, cols])
         vn[:, cols] = values
         v_t[cols, :] = jnp.transpose(values)
+        take_at(j, PROJECT)
 
     loop(tiles, project)
     pad = jnp.zeros((PAGE, 256 - lwidth), BF16)
@@ -468,6 +478,7 @@
     lvn[...] = values
     lv_t[...] = jnp.transpose(values)
     lctx_t[...] = jnp.zeros_like(lctx_t)
+    take(LAYOUT)
 
     def attend(pair):
         keys = jnp.concatenate([kn[:, tile(pair, 128)], lkn[:, tile(pair // 4, 128)]], axis=1)
@@ -485,9 +496,7 @@
             ctx_t[tile(head, 64), :] = context[0:64]
             lctx_t[tile(head, 16), :] = context[64:80]
 
-        @pl.when(pair == 3)
-        def _():
-            hand_on("up", "y")
+        take_at(pair, HEAD)
 
     loop(HEADS // 2, attend)
 
@@ -503,29 +512,26 @@
         asum[:, cols] = x_ref[:, cols].astype(F32) + dot(ctx[...], wo[:, cols]) + rises[2:3, cols]
 
     loop(tiles, mix)
-    lasum[...] = lx[...].astype(F32) + dot(lctx[:, 0:lwidth], lwo[...]) + wide(lbo)
-
-    def first_norm(source, gain, shift, hidden, hidden_low):
-        gain, shift = wide(gain), wide(shift)
-
-        def rows_of(i):
-            r = tile(i, ROWS)
-            unit, _ = normed(source[r, :])
-            value = unit * gain + shift
-            hidden[r, :] = value
-            hidden_low[r, :] = low(value)
-
-        loop(PAGE // ROWS, rows_of)
-
-    hand_on("up", "z")
-    for copy in small_across:
-        copy.wait_recv()
-    for copy in small_relay:
-        copy.start()
-    first_norm(asum, attend_gain, attend_shift, feed, hlow)
-    first_norm(lasum, lattend_gain, lattend_shift, lfeed, lhlow)
+    lasum[:, 0:lwidth] = lx[...].astype(F32) + dot(lctx[:, 0:lwidth], lwo[...]) + wide(lbo)
+
+    def first_norm(r, source, gain, shift, hidden, hidden_low):
+        unit, _ = normed(source[r, 0 : hidden.shape[1]])
+        value = unit * gain + shift
+        hidden[r, :] = value
+        hidden_low[r, :] = low(value)
+
+    gains = [wide(item) for item in (attend_gain, attend_shift, lattend_gain, lattend_shift)]
+
+    def first_norms(i):
+        r = tile(i, ROWS)
+        first_norm(r, asum, gains[0], gains[1], feed, hlow)
+        first_norm(r, lasum, gains[2], gains[3], lfeed, lhlow)
+
+    take(MIX)
+    loop(PAGE // ROWS, first_norms)
     h_t[...] = jnp.transpose(hlow[...])
     lh_t[...] = jnp.transpose(lhlow[...])
+    take(FIRST)
 
     def shard_at(s):
         return (x + s // 2 - 2 * x * (s // 2)) * 2 + c + s % 2 - 2 * c * (s % 2)
@@ -547,25 +553,7 @@
     def feed_up(s):
         t = shard_at(s)
 
-        @pl.when(s == 1)
-        def _():
-            up_core.wait_recv()
-            for copy in small_core:
-                copy.wait_recv()
-            hand_over("up", "y")
-
-        @pl.when(s == 2)
-        def _():
-            hand_on("down", "y")
-            hand_over("up", "z")
-
-        @pl.when(s == 3)
-        def _():
-            for copy in small_relay:
-                copy.wait_recv()
-            for way in ("y", "z"):
-                pass_own["up", way].wait_recv()
-                pass_got["up", way].wait_recv()
+        take_at(s, FEED)
 
         def up(j):
             cols = tile(j)
@@ -580,6 +568,7 @@
         value, gradient = gelu(preact)
         lact[s] = low(value)
         lslope[s] = low(gradient)
+        take_at(s, FED)
 
     loop(4, feed_up)
     keep_down.wait()
@@ -587,21 +576,7 @@
     def feed_down(s):
         t = shard_at(s)
 
-        @pl.when(s == 1)
-        def _():
-            down_core.wait_recv()
-            hand_on("down", "z")
-
-        @pl.when(s == 2)
-        def _():
-            hand_over("down", "y")
-            hand_over("down", "z")
-
-        @pl.when(s == 3)
-        def _():
-            for way in ("y", "z"):
-                pass_own["down", way].wait_recv()
-                pass_got["down", way].wait_recv()
+        take_at(s, DOWN)
 
         def down(j):
             cols = tile(j)
@@ -610,41 +585,41 @@
 
         loop(tiles, down)
         lfeed[...] += dot(lact[s], small[t, lwidth : 2 * lwidth, 0:lwidth])
+        take_at(s, DONE)
 
     loop(4, feed_down)
 
-    def second_norm(fed, bias, gain, shift, cot, scale, out, grad_low):
-        bias, gain, shift = wide(bias), wide(gain), wide(shift)
-
-        def rows_of(i, sums):
-            r = tile(i, ROWS)
-            unit, spread = normed(fed[r, :] + bias)
-            out[r, :] = low(unit * gain + shift)
-            outer = cot[r, :].astype(F32) * column[r, scale : scale + 1]
-            value = normed_back(unit, spread, outer * gain)
-            fed[r, :] = value
-            rounded = low(value)
-            grad_low[r, :] = rounded
-            return (
-                sums[0] + row_sum(outer * unit),
-                sums[1] + row_sum(outer),
-                sums[2] + row_sum(rounded.astype(F32)),
-            )
-
-        zero = jnp.zeros((1, fed.shape[1]), F32)
-        return lax.fori_loop(0, PAGE // ROWS, rows_of, (zero, zero, zero))
-
-    found = second_norm(
-        feed, down_bias, feed_gain, feed_shift, cot_ref, 0, out_ref, fgrad
-    )
+    def second_norm(r, sums, fed, bias, gain, shift, cot, scale, out, grad_low):
+        unit, spread = normed(fed[r, :] + bias)
+        out[r, :] = low(unit * gain + shift)
+        outer = cot[r, :].astype(F32) * column[r, scale : scale + 1]
+        value = normed_back(unit, spread, outer * gain)
+        fed[r, :] = value
+        rounded = low(value)
+        grad_low[r, :] = rounded
+        return (
+            sums[0] + row_sum(outer * unit),
+            sums[1] + row_sum(outer),
+            sums[2] + row_sum(rounded.astype(F32)),
+        )
+
+    tops = [wide(item) for item in (down_bias, feed_gain, feed_shift)]
+    ltops = [wide(item) for item in (ldown_bias, lfeed_gain, lfeed_shift)]
+
+    def second_norms(i, sums):
+        r = tile(i, ROWS)
+        return (
+            second_norm(r, sums[0], feed, *tops, cot_ref, 0, out_ref, fgrad),
+            second_norm(r, sums[1], lfeed, *ltops, lcot, 8, lout, lfgrad),
+        )
+
+    none, lnone = jnp.zeros((1, width), F32), jnp.zeros((1, lwidth), F32)
+    start = ((none, none, none), (lnone, lnone, lnone))
+    found, lfound = lax.fori_loop(0, PAGE // ROWS, second_norms, start)
+    lout_ref[...] = jnp.transpose(lout[...])
     for i in range(3):
         vec[i : i + 1, :] = found[i]
-    found = second_norm(
-        lfeed, ldown_bias, lfeed_gain, lfeed_shift, lcot, 8, lout, lfgrad
-    )
-    lout_ref[...] = jnp.transpose(lout[...])
-    for i in range(3):
-        vec[7:8, i * 256 : i * 256 + lwidth] = found[i]
+        vec[7:8, i * 256 : i * 256 + lwidth] = lfound[i]
 
     deep = tuple(range(2, dp_bits))
     flows = []
@@ -652,15 +627,15 @@
     places = []
     for rows, order in feed_flows:
         order = order + deep
-        depth = order.index("x")
+        depth = order.index(ACROSS)
         places.append((keep_at, rows >> depth))
         size = landing(4 * rows, len(order) + 1) - 2 * rows
         lands = recv.at[pl.ds(keep_at, 2 * rows)], recv.at[pl.ds(recv_at, size)]
         flows.append(
             Flow(
                 where,
-                ("core",) + order,
-                [axis for axis in order if axis != "x"],
+                (CORE,) + order,
+                [axis for axis in order if axis != ACROSS],
                 4 * rows,
                 staging.at[pl.ds(keep_at, 2 * rows)],
                 acc.at[pl.ds(keep_at, 2 * rows)],
@@ -668,6 +643,7 @@
                 sums.at[pl.ds(sum_at, rows)],
                 (send_sem, recv_sem, index),
                 None,
+                (sums_out.at[pl.ds(sum_at, rows)], out_sem.at[len(flows)]),
             )
         )
         index += len(flows[-1].steps)
@@ -678,7 +654,7 @@
     ready = {axis: ready_sem.at[i] for i, axis in enumerate(where)}
     keep_at, recv_at = 0, 0
     for rows, order in shared_flows:
-        order = ("core",) + order + deep
+        order = (CORE,) + order + deep
         size = landing(rows, len(order))
         mine = shared.at[pl.ds(keep_at, rows)]
         lands = (
@@ -697,6 +673,7 @@
                 shared_sum.at[pl.ds(keep_at, rows)],
                 (send_sem, recv_sem, index),
                 ready,
+                (sums_out.at[pl.ds(sum_at + keep_at, rows)], out_sem.at[len(flows)]),
             )
         )
         index += len(flows[-1].steps)
@@ -705,8 +682,8 @@
 
     script = Script(flows, set())
     last = len(flows) - 1
-    made = [("d", i) for i in range(tiles)] + [("up", i) for i in range(tiles)]
-    made += [("context", 0)] + [("weight", i) for i in range(tiles)]
+    made = [(D, i) for i in range(tiles)] + [(UP, i) for i in range(tiles)]
+    made += [(CONTEXT, 0)] + [(WEIGHT, i) for i in range(tiles)]
     if moves:
         for point, numbers in moves.items():
             for number in numbers:
@@ -714,11 +691,11 @@
     else:
         for i, point in enumerate(made):
             script.write(point, len(flows) + i)
-            if point[0] == "up" and i + 1 == 2 * tiles:
+            if point[0] == UP and i + 1 == 2 * tiles:
                 for k in range(feed_count):
-                    script.write("sync", k)
+                    script.write((SYNC, 0), k)
         script.write(made[-1], len(flows) + last)
-    script.finish("tail")
+    script.finish((TAIL, 0))
     act_now = script.play
 
     def put(number, target, xs, start, block, cols):
@@ -732,27 +709,23 @@
             target[place, cols] = block[row - start : row - start + length]
             row += length
 
-    def down_grad(number, first_unit, units):
+    def outer_grad(number, rows_t, base, tile_index):
         def both(g):
             xs = x + g - 2 * x * g
             for parity, target in ((0, acc), (1, staging)):
-                s = 2 * g + parity
-                unit = pl.ds(first_unit, units)
-                turned[0:units, :] = jnp.transpose(pool[page_rows(act_at, s), unit])
-
-                def block(j):
-                    cols = tile(j)
-                    value = low(dot(turned[0:units, :], fgrad[:, cols]))
-                    put(number, target, xs, 0, value, cols)
-
-                loop(tiles, block)
+                cols = slice(tile_index * TILE, (tile_index + 1) * TILE)
+                value = low(dot(rows_t[...], pool[page_rows(base, 2 * g + parity), cols]))
+                for q in range(tiles):
+                    lanes = slice(q * TILE, (q + 1) * TILE)
+                    put(number, target, xs, 0, value[q * TILE : (q + 1) * TILE], lanes)
 
         loop(2, both)
 
+    fgrad_t[...] = jnp.transpose(fgrad[...])
     for i in range(tiles):
-        down_grad(i, i * TILE, TILE)
+        outer_grad(i, fgrad_t, act_at, i)
         if i + 1 < tiles:
-            act_now(("d", i))
+            act_now((D, i))
     empty = jnp.zeros((64, 256 - lwidth), BF16)
 
     def layout_grad(g):
@@ -779,7 +752,7 @@
                     put(tiles - 1, target, xs, TILE + 64 * which, piece, cols)
 
     loop(2, layout_grad)
-    act_now(("d", tiles - 1))
+    act_now((D, tiles - 1))
 
     def units_grad(s):
         t = shard_at(s)
@@ -798,30 +771,13 @@
 
             @pl.when(s == k)
             def _():
-                act_now(("units", k))
+                act_now((UNITS, k))
 
     loop(4, units_grad)
 
-    def up_grad(number, start):
-        def both(g):
-            xs = x + g - 2 * x * g
-            for parity, target in ((0, acc), (1, staging)):
-                s = 2 * g + parity
-
-                def block(j):
-                    cols = tile(j)
-                    value = low(
-                        dot(h_t[start : start + TILE, :], pool[page_rows(slope_at, s), cols])
-                    )
-                    put(number, target, xs, 0, value, cols)
-
-                loop(tiles, block)
-
-        loop(2, both)
-
     for i in range(tiles):
-        up_grad(tiles + i, i * TILE)
-        act_now(("up", i))
+        outer_grad(tiles + i, h_t, slope_at, i)
+        act_now((UP, i))
 
     def hidden_back(s):
         t = shard_at(s)
@@ -836,10 +792,10 @@
 
             @pl.when(s == k)
             def _():
-                act_now(("back", k))
+                act_now((BACK, k))
 
     loop(4, hidden_back)
-    for copy in gather_all:
+    for copy in messages:
         copy.wait_send()
     for item in flows[:feed_count]:
         item.steps[0][1].wait_send()
@@ -850,7 +806,7 @@
             device_id=device,
             device_id_type=MESH,
         )
-    act_now("sync")
+    act_now((SYNC, 0))
     wo_again, wq_again, wk_again, wv_again = (
         recv.at[pl.ds(i * width, width)] for i in range(4)
     )
@@ -862,36 +818,34 @@
     ]
     mixed, lmixed = fgrad, lfgrad
 
-    def norm_grad(source, gain, grad, grad_low):
-        gain = wide(gain)
-
-        def rows_of(i, sums):
-            r = tile(i, ROWS)
-            unit, spread = normed(source[r, :])
-            outer = grad[r, :]
-            value = normed_back(unit, spread, outer * gain)
-            grad[r, :] = value
-            rounded = low(value)
-            grad_low[r, :] = rounded
-            return (
-                sums[0] + row_sum(rounded.astype(F32)),
-                sums[1] + row_sum(outer * unit),
-                sums[2] + row_sum(outer),
-            )
-
-        zero = jnp.zeros((1, source.shape[1]), F32)
-        return lax.fori_loop(0, PAGE // ROWS, rows_of, (zero, zero, zero))
-
-    found = norm_grad(asum, attend_gain, feed, mixed)
+    def norm_grad(r, sums, source, gain, grad, grad_low):
+        unit, spread = normed(source[r, 0 : grad.shape[1]])
+        outer = grad[r, :]
+        value = normed_back(unit, spread, outer * gain)
+        grad[r, :] = value
+        rounded = low(value)
+        grad_low[r, :] = rounded
+        return (
+            sums[0] + row_sum(rounded.astype(F32)),
+            sums[1] + row_sum(outer * unit),
+            sums[2] + row_sum(outer),
+        )
+
+    def norm_grads(i, sums):
+        r = tile(i, ROWS)
+        return (
+            norm_grad(r, sums[0], asum, gains[0], feed, mixed),
+            norm_grad(r, sums[1], lasum, gains[2], lfeed, lmixed),
+        )
+
+    found, lfound = lax.fori_loop(0, PAGE // ROWS, norm_grads, start)
     for i in range(3):
         vec[12 + i : 13 + i, :] = found[i]
-    found = norm_grad(lasum, lattend_gain, lfeed, lmixed)
-    for i in range(3):
-        vec[15:16, i * 256 : i * 256 + lwidth] = found[i]
-    act_now(("norm", 0))
+        vec[15:16, i * 256 : i * 256 + lwidth] = lfound[i]
+    act_now((NORM, 0))
     again[0].wait()
     k_t, lk_t, cgrad_t, lcgrad = v_t, lv_t, h_t, lctx
-    masked_c[...] = jnp.zeros_like(masked_c)
+    masks[...] = jnp.zeros_like(masks)
 
     def turn(j):
         x_t[tile(j), :] = jnp.transpose(x_ref[:, tile(j)])
@@ -910,7 +864,7 @@
     lcgrad_t[...] = jnp.transpose(value)
     lk_t[...] = jnp.transpose(lkn[...])
     loop(tiles, turn)
-    act_now(("context", 0))
+    act_now((CONTEXT, 0))
 
     lane = lax.broadcasted_iota(jnp.int32, (PAGE, 128), 1)
     ldv[...] = jnp.zeros_like(ldv)
@@ -952,7 +906,7 @@
 
             @pl.when(pair == k)
             def _():
-                act_now(("attend", k))
+                act_now((ATTEND, k))
 
         @pl.when(pair % 2 == 1)
         def _():
@@ -962,7 +916,7 @@
 
             @pl.when(pair == 2 * k + 1)
             def _():
-                act_now(("weight", k))
+                act_now((WEIGHT, k))
 
     def weight_grad(group):
         cols = tile(group)
@@ -985,7 +939,7 @@
     base += lwidth
     shared[base : base + 16, :] = low(vec[...])
     shared[base + 16 : shared_rows, :] = jnp.zeros((shared_rows - base - 16, width), BF16)
-    act_now(("weight", tiles - 1))
+    act_now((WEIGHT, tiles - 1))
     for copy in again[1:]:
         copy.wait()
 
@@ -1000,55 +954,170 @@
 
             @pl.when(j == k)
             def _():
-                act_now(("input", k))
+                act_now((INPUT, k))
 
     loop(tiles, input_back)
     in_grad_copy = load(4, feed, in_grad_out)
     lin_grad[...] = jnp.transpose(
         lfeed[...] + dot_nt(query, lwq[...]) + dot_nt(key, lwk[...]) + dot_nt(value, lwv[...])
     )
-    act_now(("end", 0))
-    act_now("tail")
-    total = sums.shape[0]
-    outs = [
-        load(0, sums, sums_out.at[pl.ds(0, total)]),
-        load(1, shared_sum, sums_out.at[pl.ds(total, shared_rows)]),
-    ]
+    act_now((END, 0))
+    act_now((TAIL, 0))
     for item in flows:
         item.drain()
-    for copy in outs + [in_grad_copy]:
+    in_grad_copy.wait()
+
+
+def finish_kernel(feed_rows, sums_hbm, *refs):
+    passed, outs = refs[0:4], refs[4:38]
+    sums, wide_sums, vec = refs[38:41]
+    through = refs[41:45]
+    load_sem, store_sem, in_sem, out_sem = refs[45:49]
+    width, lwidth = wide_sums.shape[1], through[1].shape[0]
+    down_rows = width + 128
+    starts = (feed_rows, 0, down_rows, feed_rows + width, feed_rows + 2 * width)
+    starts += (feed_rows + 3 * width, feed_rows + 4 * width)
+    sizes = [width, down_rows] + [width] * 4 + [sums.shape[0] - starts[-1]]
+    loads = []
+    for i, (start, size) in enumerate(zip(starts, sizes)):
+        part = pl.ds(start, size)
+        copy = pltpu.make_async_copy(sums_hbm.at[part], sums.at[part], load_sem.at[i])
+        copy.start()
+        loads.append(copy)
+    takes = [
+        pltpu.make_async_copy(a, b, in_sem.at[i]) for i, (a, b) in enumerate(zip(passed, through))
+    ]
+    gives = [
+        pltpu.make_async_copy(a, b, out_sem.at[i]) for i, (a, b) in enumerate(zip(through, outs))
+    ]
+    for copy in takes:
+        copy.start()
+
+    def widen(slot, start, cols=None, lanes=None):
+        def block(i):
+            source = pl.ds(start + pl.multiple_of(i * 128, 128), 128)
+            target = pl.ds(pl.multiple_of(i * 128, 128), 128)
+            if cols is None:
+                wide_sums[slot, target, :] = sums[source, :].astype(F32)
+            else:
+                wide_sums[slot, target, lanes] = sums[source, cols].astype(F32)
+
+        loop(width // 128, block)
+
+    text, layout = outs[4:19], outs[19:34]
+    stores = []
+
+    def store(slot, out):
+        copy = pltpu.make_async_copy(wide_sums.at[slot], out, store_sem.at[slot])
+        copy.start()
+        stores.append(copy)
+
+    loads[0].wait()
+    widen(0, starts[0])
+    store(0, text[5])
+    blocks = range(width // TILE)
+    for slot, out in ((1, text[11]), (2, text[9])):
+        loads[slot].wait()
+        for i in blocks:
+            for q in blocks:
+                rows = pl.ds(starts[slot] + i * TILE, TILE)
+                value = sums[rows, q * TILE : (q + 1) * TILE].astype(F32)
+                place = (i, q) if slot == 1 else (q, i)
+                value = jnp.transpose(value) if slot == 1 else value
+                down, across = (pl.ds(k * TILE, TILE) for k in place)
+                wide_sums[slot, down, across] = value
+        store(slot, out)
+    for copy, give in zip(takes, gives):
         copy.wait()
+        give.start()
+    for g in range(width // TILE):
+        loads[3 + g].wait()
+        for i in range(3):
+            lanes = slice(g * TILE, (g + 1) * TILE)
+            widen(3 + i, starts[3 + g], slice(i * TILE, (i + 1) * TILE), lanes)
+    for i, out in enumerate((text[0], text[2], text[3])):
+        store(3 + i, out)
+    loads[6].wait()
+    base = starts[6]
+    for i, out in enumerate((layout[0], layout[2], layout[3], layout[5])):
+        out[...] = sums[base : base + lwidth, i * lwidth : (i + 1) * lwidth].astype(F32)
+    for i, out in enumerate((layout[9], layout[11])):
+        for q in range(lwidth // 64):
+            rows = sums[width + 64 * i : width + 64 * i + 64, q * TILE : q * TILE + lwidth]
+            out[q * 64 : q * 64 + 64, :] = rows.astype(F32)
+    vec[...] = sums[base + lwidth : base + lwidth + 16, :].astype(F32)
+    me = lax.axis_index("tensor")
+    for row, out in ((10, 1), (11, 4), (12, 6), (13, 7), (14, 8), (2, 12), (0, 13), (1, 14)):
+        text[out][...] = vec[row, :]
+    text[10][...] = vec[pl.ds(3 + me, 1), :][0]
+
+    def strip(row, part):
+        return vec[row : row + 1, part * TILE : part * TILE + lwidth]
+
+    places = ((9, 1, 1), (9, 2, 4), (15, 0, 6), (15, 1, 7), (15, 2, 8))
+    for row, part, out in places + ((7, 2, 12), (7, 0, 13), (7, 1, 14)):
+        layout[out][...] = strip(row, part)[0]
+    rise = strip(8, 0)
+    for k, (row, part) in enumerate(((8, 1), (8, 2), (9, 0))):
+        rise = jnp.where(me == k + 1, strip(row, part), rise)
+    layout[10][...] = rise[0]
+    for copy in stores + gives:
+        copy.wait()
 
 
 MOVES = {
-    ("d", 0): (11,),
-    ("d", 1): (12,),
-    ("d", 2): (13, 0, 11, 1, 12),
-    ("units", 2): (2, 13),
-    ("up", 0): (14,),
-    ("up", 1): (15,),
-    ("up", 2): (16, 0, 11, 1, 12, 3),
-    ("back", 0): (14, 4, 15, 5),
-    ("back", 3): (0, 11, 1, 12),
-    ("norm", 0): (16, 2, 13, 0, 11),
-    ("context", 0): (17, 1, 12, 3, 14, 4),
-    ("attend", 0): (15, 0, 11, 6, 17, 2),
-    ("attend", 1): (13, 5, 1, 12, 0, 11, 3, 14),
-    ("weight", 0): (18, 16, 4, 15),
-    ("attend", 2): (1, 12, 2, 13, 7, 3, 6),
-    ("attend", 3): (17, 18, 4, 0, 5),
-    ("weight", 1): (19,),
-    ("attend", 4): (16, 1, 2, 13, 8, 19, 14, 6),
-    ("attend", 5): (7, 18, 17),
-    ("weight", 2): (20, 21, 15, 2, 5),
-    ("input", 0): (16, 8, 19, 7, 18, 9, 20, 3, 10, 21, 6),
-    ("input", 1): (17,),
-    ("input", 2): (7,),
-    ("end", 0): (18, 8, 4),
-    "tail": (10, 21, 5, 19, 9, 20, 6, 17, 10, 21, 9, 20, 7, 18, 14, 8, 6, 17, 19, 7, 18, 10, 9, 20, 3, 14, 21, 6, 17, 8, 19, 15, 7, 9, 20, 10, 21, 8, 19, 18, 3, 6, 17, 4, 15, 9, 20, 6, 10, 8, 19, 21, 9, 20, 16, 4, 13, 7, 18, 10, 21, 5, 16, 7, 8, 19, 9, 20, 8, 9, 10, 21, 2, 5, 10),
+    (D, 0): (11,),
+    (D, 1): (12,),
+    (D, 2): (13, 0, 11, 1, 12),
+    (UNITS, 2): (2, 13),
+    (UP, 0): (14,),
+    (UP, 1): (15,),
+    (UP, 2): (16,),
+    (BACK, 1): (3, 0, 11, 1, 12, 4),
+    (BACK, 2): (5, 15),
+    (BACK, 3): (16,),
+    (NORM, 0): (14,),
+    (CONTEXT, 0): (17, 0, 1, 2),
+    (ATTEND, 0): (13, 6, 11, 17),
+    (ATTEND, 1): (12, 4, 5, 3, 16),
+    (WEIGHT, 0): (18, 14, 0, 11),
+    (ATTEND, 2): (1, 15, 12, 2, 6, 17, 7),
+    (ATTEND, 3): (18, 5, 13, 16, 0, 3, 14),
+    (WEIGHT, 1): (19, 6, 1, 12, 17),
+    (ATTEND, 4): (11, 4, 15, 5, 16, 8, 19, 3, 2),
+    (ATTEND, 5): (13, 6, 7, 18, 1, 0, 4),
+    (WEIGHT, 2): (20, 21, 11, 5, 17),
+    (INPUT, 0): (7, 8, 9, 20, 18),
+    (INPUT, 1): (10, 21, 14, 2),
+    (INPUT, 2): (0,),
+    (END, 0): (19, 6),
+    (TAIL, 0): (7, 18, 9, 20, 13, 10, 17, 3, 8, 21, 19, 9, 20, 7, 6, 17, 18, 2, 15, 8, 9, 10, 7, 18, 6, 19, 4, 17, 21, 20, 7, 18, 8, 19, 10, 21, 9, 15, 20, 8, 14, 6, 17, 19, 16, 10, 7, 18, 9, 20, 4, 21, 6, 3, 14, 13, 7, 9, 5, 8, 19, 10, 21, 3, 20, 12, 10, 21, 2, 16, 8, 19, 15, 9, 20, 8, 1, 9, 10, 21, 5, 10, 4),
 }
-FEED_ORDERS = (("x", 0, 1), (0, "x", 1), (1, "x", 0), (0, "x", 1), ("x", 0, 1), (0, "x", 1))
-SHARED_ORDERS = (("x", 0, 1), (1, 0, "x"), ("x", 0, 1), (0, "x", 1), ("x", 0, 1))
+FEED_ORDERS = ((0, 1, ACROSS), (1, 0, ACROSS), (ACROSS, 1, 0), (ACROSS, 0, 1), (1, 0, ACROSS), (0, ACROSS, 1))
+SHARED_ORDERS = ((0, ACROSS, 1), (ACROSS, 0, 1), (ACROSS, 0, 1), (0, ACROSS, 1), (ACROSS, 0, 1))
+
+START = (3, 2, 39, 42, 18, 21, 22, 41, 1, 0, 19, 38, 20, 37)
+GATHER = {
+    (SETUP, 0): (39, 42),
+    (PROJECT, 2): (3, 18),
+    (HEAD, 0): (2, 37),
+    (HEAD, 2): (21, 8),
+    (HEAD, 3): (22, 41),
+    (HEAD, 4): (6, 16),
+    (HEAD, 5): (43, 1),
+    (MIX, 0): (25, 14, 0, 27, 12),
+    (FIRST, 0): (19, 33, 10),
+    (FED, 0): (35, 9, 7, 29),
+    (FED, 1): (4, 38, 5, 17),
+    (FED, 2): (15, 11, 20),
+    (FEED, 3): (40, 13),
+    (FED, 3): (28, 31),
+    (DONE, 0): (26, 23),
+    (DONE, 1): (36,),
+    (DOWN, 2): (24,),
+    (DONE, 2): (34, 30),
+    (DOWN, 3): (32,),
+}
 
 
 def on_device(dp, tensor, *args):
@@ -1115,13 +1184,11 @@
         pltpu.VMEM((256, page), BF16),
         pltpu.VMEM((256, page), BF16),
         pltpu.VMEM((16, page), F32),
-        pltpu.VMEM((512, page), BF16),
-        pltpu.VMEM((512, page), BF16),
+        pltpu.VMEM((1024, page), BF16),
         pltpu.VMEM((width, page), BF16),
         pltpu.VMEM((256, page), BF16),
         pltpu.VMEM((page, 256), BF16),
         pltpu.VMEM((page, width), F32),
-        pltpu.VMEM((page, lwidth), F32),
         pltpu.VMEM((page, width), BF16),
         pltpu.VMEM((page, lwidth), BF16),
         pltpu.VMEM((width, page), BF16),
@@ -1140,10 +1207,11 @@
         pltpu.VMEM((page, 256), F32),
         pltpu.VMEM((16, width), F32),
         pltpu.SemaphoreType.DMA((6,)),
-        pltpu.SemaphoreType.DMA((24,)),
-        pltpu.SemaphoreType.DMA((24,)),
+        pltpu.SemaphoreType.DMA((48,)),
+        pltpu.SemaphoreType.DMA((48,)),
         pltpu.SemaphoreType.DMA((count,)),
         pltpu.SemaphoreType.DMA((count,)),
+        pltpu.SemaphoreType.DMA((len(feed_flows) + len(shared_flows),)),
         pltpu.SemaphoreType.REGULAR((dp_bits + 2,)),
     ]
     text_out, layout_out, in_grad, lin_grad, sums = pl.pallas_call(
@@ -1158,69 +1226,43 @@
         name="layer",
     )(*inputs)
 
-    me = lax.axis_index("tensor")
-    shared = sums[feed_rows:]
-    at = 4 * width
-    packed = shared[at : at + lwidth].astype(F32)
-    vec = shared[at + lwidth : at + lwidth + 16].astype(F32)
-
-    def square(index):
-        parts = [
-            shared[(1 + g) * width : (2 + g) * width, index * TILE : (index + 1) * TILE]
-            for g in range(width // TILE)
-        ]
-        return jnp.concatenate(parts, axis=1).astype(F32)
-
-    def unpack(block):
-        parts = [block[:, q * 256 : q * 256 + lwidth] for q in range(lwidth // 64)]
-        return jnp.concatenate(parts, axis=0).astype(F32)
-
-    def layout_square(index):
-        return packed[:, index * lwidth : (index + 1) * lwidth]
-
-    def strip(index, part):
-        return vec[index, part * 256 : part * 256 + lwidth]
-
-    up_bias = lax.dynamic_index_in_dim(vec, 3 + me, 0, keepdims=False)
-    lup_bias = lax.dynamic_index_in_dim(
-        jnp.stack([strip(8, 0), strip(8, 1), strip(8, 2), strip(9, 0)]), me, 0, keepdims=False
+    big, small_square = shape(width, width, dtype=F32), shape(lwidth, lwidth, dtype=F32)
+
+    def stream(square, size):
+        line = shape(size, dtype=F32)
+        order = (square, line, square, square, line, square, line, line, line)
+        return order + (square, line, square, line, line, line)
+
+    outs = (
+        shape(page, width),
+        shape(lwidth, page),
+        shape(page, width, dtype=F32),
+        shape(lwidth, page, dtype=F32),
     )
-    return (
-        text_out,
-        layout_out.T,
-        in_grad,
-        lin_grad.T,
-        square(0),
-        vec[10],
-        square(1),
-        square(2),
-        vec[11],
-        shared[0:width].astype(F32),
-        vec[12],
-        vec[13],
-        vec[14],
-        sums[width + 128 : 2 * width + 128].astype(F32),
-        up_bias,
-        sums[0:width].astype(F32),
-        vec[2],
-        vec[0],
-        vec[1],
-        layout_square(0),
-        strip(9, 1),
-        layout_square(1),
-        layout_square(2),
-        strip(9, 2),
-        layout_square(3),
-        strip(15, 0),
-        strip(15, 1),
-        strip(15, 2),
-        unpack(sums[width : width + 64]),
-        lup_bias,
-        unpack(sums[width + 64 : width + 128]),
-        strip(7, 2),
-        strip(7, 0),
-        strip(7, 1),
-    )
+    outs += stream(big, width) + stream(small_square, lwidth)
+    specs = [hbm if i < 4 or out.shape == (width, width) else vmem for i, out in enumerate(outs)]
+    done = pl.pallas_call(
+        functools.partial(finish_kernel, feed_rows),
+        out_shape=outs,
+        in_specs=[hbm] * 5,
+        out_specs=specs,
+        scratch_shapes=[
+            pltpu.VMEM((feed_rows + shared_rows, width), BF16),
+            pltpu.VMEM((6, width, width), F32),
+            pltpu.VMEM((16, width), F32),
+            pltpu.VMEM((page, width), BF16),
+            pltpu.VMEM((lwidth, page), BF16),
+            pltpu.VMEM((page, width), F32),
+            pltpu.VMEM((lwidth, page), F32),
+            pltpu.SemaphoreType.DMA((7,)),
+            pltpu.SemaphoreType.DMA((6,)),
+            pltpu.SemaphoreType.DMA((4,)),
+            pltpu.SemaphoreType.DMA((4,)),
+        ],
+        compiler_params=pltpu.CompilerParams(vmem_limit_bytes=60000000),
+        name="finish",
+    )(sums, text_out, layout_out, in_grad, lin_grad)
+    return (done[0], done[1].T, done[2], done[3].T) + tuple(done[4:])
 
 
 def solution(mesh):

time: 207 us -> 171 us (0.83)
  Pallas kernels: 186 us -> 170 us
  other arithmetic: 11.5 us -> 0 us
  local copies, waits for them, and re-layouts: 8.89 us -> 0 us
    pallas_call x1, Pallas kernels: 186 us -> 158 us  [on_device(): pl.pallas_call(functools.partial(layer_kernel, (dp_bits, feed_flows, shar...]
    pallas_call x0 -> x1, Pallas kernels: none -> 11.7 us  [on_device(): pl.pallas_call(functools.partial(finish_kernel, feed_rows), out_shape=out...]
    convert_element_type x5 -> x0, other arithmetic: 10.9 us -> none  [the longest x1 5.83 us: on_device(): sums[0:width].astype(F32)]
    slice x5 -> x0, local copies, waits for them, and re-layouts: 5.31 us -> none  [the longest x1 2.22 us: square(): shared[(1 + g) * width:(2 + g) * width, index * TILE:(index + 1) * TILE]]
    unnamed x12 -> x0, local copies, waits for them, and re-layouts: 3.58 us -> none
where the time goes in v3:
time: 171 us
  Pallas kernels  170 us (99%)
    pallas_call x1, Pallas kernels, on_device(): pl.pallas_call(functools.partial(layer_kernel, (dp_bits, feed_flows, shar...  158 us
    pallas_call x1, Pallas kernels, on_device(): pl.pallas_call(functools.partial(finish_kernel, feed_rows), out_shape=out...  11.7 us

profile of v3, /device:TPU:0, one launch (start us, length us, event | category | flops | bytes accessed | tf_op | source)
XLA Modules:
  0.0 170.5 jit_solution(4028574943134631745)
XLA Ops:
  0.7 157.9 %layer.1 = (bf16[512,768]{1,0:T(8,128)(2,1)}, bf16[192,512]{1,0:T(8,128)(2,1)}, f32[512,768]{1,0:T(8,128)}, f32[192,512]{1,0:T(8,128)}, bf16[4992,768]{1,0:T(8,128)(2,1)}) custom-call(bf16[512,768]{1,0:T(8,128)(2,1)} %refs_0_.1, bf16[192,512]{1,0:T(8,128)(2,1)} %bitcast.6, s32[1,512]{1,0:T(1,128)} %bitcast.8, s32[1,512]{1,0:T(1,128)} %bitcast.9, ...), custom_call_target="tpu_custom_call" | custom-call | tf_op jit(solution)/shard_map/layer/pallas_call | solution.py:1217
  158.6 11.7 %finish.1 = (bf16[512,768]{1,0:T(8,128)(2,1)}, bf16[192,512]{1,0:T(8,128)(2,1)}, f32[512,768]{1,0:T(8,128)}, f32[192,512]{1,0:T(8,128)}, f32[768,768]{1,0:T(8,12...) custom-call(bf16[4992,768]{1,0:T(8,128)(2,1)} %get-tuple-element.73., ...), custom_call_target="tpu_custom_call" | custom-call | tf_op jit(solution)/shard_map/finish/pallas_call | solution.py:1244

commit v4 on v3

--- a/solution.py
+++ b/solution.py
@@ -17,7 +17,7 @@
 ROWS = 128
 CORE, ACROSS = 100, 101
 SETUP, PROJECT, LAYOUT, HEAD, MIX, FIRST, FEED, FED, DOWN, DONE = range(10)
-D, UNITS, UP, BACK, NORM, CONTEXT, ATTEND, WEIGHT, INPUT, END, TAIL, SYNC = range(10, 22)
+D, UNITS, UP, BACK, NORM, CONTEXT, ATTEND, WEIGHT, INPUT, END, TAIL, SYNC, LAY = range(10, 23)
 
 
 def low(values):
@@ -626,7 +626,7 @@
     index, keep_at, recv_at, sum_at = 0, 0, 2 * sums.shape[0], 0
     places = []
     for rows, order in feed_flows:
-        order = order + deep
+        order = order + tuple(axis for axis in deep if axis not in order)
         depth = order.index(ACROSS)
         places.append((keep_at, rows >> depth))
         size = landing(4 * rows, len(order) + 1) - 2 * rows
@@ -681,9 +681,8 @@
         recv_at += size
 
     script = Script(flows, set())
-    last = len(flows) - 1
     made = [(D, i) for i in range(tiles)] + [(UP, i) for i in range(tiles)]
-    made += [(CONTEXT, 0)] + [(WEIGHT, i) for i in range(tiles)]
+    made += [(WEIGHT, group - 1) if group else (CONTEXT, 0) for group in GROUPS]
     if moves:
         for point, numbers in moves.items():
             for number in numbers:
@@ -694,7 +693,6 @@
             if point[0] == UP and i + 1 == 2 * tiles:
                 for k in range(feed_count):
                     script.write((SYNC, 0), k)
-        script.write(made[-1], len(flows) + last)
     script.finish((TAIL, 0))
     act_now = script.play
 
@@ -724,8 +722,7 @@
     fgrad_t[...] = jnp.transpose(fgrad[...])
     for i in range(tiles):
         outer_grad(i, fgrad_t, act_at, i)
-        if i + 1 < tiles:
-            act_now((D, i))
+        act_now((D, i))
     empty = jnp.zeros((64, 256 - lwidth), BF16)
 
     def layout_grad(g):
@@ -749,10 +746,7 @@
                 for q in range(lwidth // 64):
                     piece = jnp.concatenate([block[q * 64 : q * 64 + 64], empty], axis=1)
                     cols = slice(q * 256, q * 256 + 256)
-                    put(tiles - 1, target, xs, TILE + 64 * which, piece, cols)
-
-    loop(2, layout_grad)
-    act_now((D, tiles - 1))
+                    put(2 * tiles - 1, target, xs, TILE + 64 * which, piece, cols)
 
     def units_grad(s):
         t = shard_at(s)
@@ -776,6 +770,9 @@
     loop(4, units_grad)
 
     for i in range(tiles):
+        if i == 0:
+            loop(2, layout_grad)
+            act_now((LAY, 0))
         outer_grad(tiles + i, h_t, slope_at, i)
         act_now((UP, i))
 
@@ -974,10 +971,9 @@
     through = refs[41:45]
     load_sem, store_sem, in_sem, out_sem = refs[45:49]
     width, lwidth = wide_sums.shape[1], through[1].shape[0]
-    down_rows = width + 128
-    starts = (feed_rows, 0, down_rows, feed_rows + width, feed_rows + 2 * width)
+    starts = (feed_rows, 0, width, feed_rows + width, feed_rows + 2 * width)
     starts += (feed_rows + 3 * width, feed_rows + 4 * width)
-    sizes = [width, down_rows] + [width] * 4 + [sums.shape[0] - starts[-1]]
+    sizes = [width, width, width + 128] + [width] * 3 + [sums.shape[0] - starts[-1]]
     loads = []
     for i, (start, size) in enumerate(zip(starts, sizes)):
         part = pl.ds(start, size)
@@ -1043,7 +1039,8 @@
         out[...] = sums[base : base + lwidth, i * lwidth : (i + 1) * lwidth].astype(F32)
     for i, out in enumerate((layout[9], layout[11])):
         for q in range(lwidth // 64):
-            rows = sums[width + 64 * i : width + 64 * i + 64, q * TILE : q * TILE + lwidth]
+            top = 2 * width + 64 * i
+            rows = sums[top : top + 64, q * TILE : q * TILE + lwidth]
             out[q * 64 : q * 64 + 64, :] = rows.astype(F32)
     vec[...] = sums[base + lwidth : base + lwidth + 16, :].astype(F32)
     me = lax.axis_index("tensor")
@@ -1066,35 +1063,38 @@
 
 
 MOVES = {
-    (D, 0): (11,),
-    (D, 1): (12,),
-    (D, 2): (13, 0, 11, 1, 12),
-    (UNITS, 2): (2, 13),
-    (UP, 0): (14,),
-    (UP, 1): (15,),
-    (UP, 2): (16,),
-    (BACK, 1): (3, 0, 11, 1, 12, 4),
-    (BACK, 2): (5, 15),
-    (BACK, 3): (16,),
-    (NORM, 0): (14,),
-    (CONTEXT, 0): (17, 0, 1, 2),
-    (ATTEND, 0): (13, 6, 11, 17),
-    (ATTEND, 1): (12, 4, 5, 3, 16),
-    (WEIGHT, 0): (18, 14, 0, 11),
-    (ATTEND, 2): (1, 15, 12, 2, 6, 17, 7),
-    (ATTEND, 3): (18, 5, 13, 16, 0, 3, 14),
-    (WEIGHT, 1): (19, 6, 1, 12, 17),
-    (ATTEND, 4): (11, 4, 15, 5, 16, 8, 19, 3, 2),
-    (ATTEND, 5): (13, 6, 7, 18, 1, 0, 4),
-    (WEIGHT, 2): (20, 21, 11, 5, 17),
-    (INPUT, 0): (7, 8, 9, 20, 18),
-    (INPUT, 1): (10, 21, 14, 2),
-    (INPUT, 2): (0,),
-    (END, 0): (19, 6),
-    (TAIL, 0): (7, 18, 9, 20, 13, 10, 17, 3, 8, 21, 19, 9, 20, 7, 6, 17, 18, 2, 15, 8, 9, 10, 7, 18, 6, 19, 4, 17, 21, 20, 7, 18, 8, 19, 10, 21, 9, 15, 20, 8, 14, 6, 17, 19, 16, 10, 7, 18, 9, 20, 4, 21, 6, 3, 14, 13, 7, 9, 5, 8, 19, 10, 21, 3, 20, 12, 10, 21, 2, 16, 8, 19, 15, 9, 20, 8, 1, 9, 10, 21, 5, 10, 4),
+    (D, 0): (14,),
+    (D, 1): (15,),
+    (D, 2): (16,),
+    (UNITS, 1): (0, 14),
+    (UNITS, 2): (1, 15),
+    (UNITS, 3): (2, 16),
+    (UP, 0): (17,),
+    (UP, 1): (18,),
+    (UP, 2): (19,),
+    (BACK, 1): (3, 17, 0, 14, 4, 1, 15),
+    (BACK, 2): (2, 18, 5, 19),
+    (NORM, 0): (0, 14),
+    (CONTEXT, 0): (21, 20, 1, 15),
+    (ATTEND, 0): (16, 3, 7, 0, 14, 6, 1, 4, 21),
+    (ATTEND, 1): (18, 15),
+    (WEIGHT, 0): (23, 22, 20, 2, 5, 16, 0, 14),
+    (ATTEND, 2): (19, 9, 23, 8, 7, 1, 15, 4, 18, 6, 0),
+    (ATTEND, 3): (22, 21, 2, 20, 16, 1),
+    (WEIGHT, 1): (25, 24, 17, 14, 9, 4, 18),
+    (ATTEND, 4): (23, 15, 5, 19, 7, 11, 10, 8, 25, 6, 2),
+    (ATTEND, 5): (22, 16, 24, 3, 21, 0, 4, 9, 23),
+    (WEIGHT, 2): (26, 27, 17, 20, 18, 5, 1, 19, 8, 10, 24, 11, 25, 7, 2, 9, 12, 26, 6, 13),
+    (INPUT, 0): (3, 27, 4, 18, 10, 21),
+    (INPUT, 1): (11, 25),
+    (INPUT, 2): (23,),
+    (END, 0): (24, 12, 26),
+    (TAIL, 0): (5, 22, 4, 20, 7, 21, 11, 13, 27, 25, 10, 12, 8, 26, 9, 6, 23, 7, 21, 13, 27, 11, 25, 22, 12, 9, 23, 26, 7, 21, 13, 27, 11, 25, 8, 24, 20, 9, 23, 12, 26, 22, 11, 25, 17, 13, 6, 20, 10, 7, 21, 12, 24, 26, 8, 27, 9, 23, 22, 19, 7, 6, 20, 9, 11, 25, 10, 24, 12, 26, 16, 3, 17, 13, 8, 27, 11, 6, 20, 10, 22, 6, 5, 19, 3, 24, 12, 26, 13, 27, 17, 2, 12, 8, 22, 10, 24, 8, 10, 13, 27, 5, 3, 13),
 }
-FEED_ORDERS = ((0, 1, ACROSS), (1, 0, ACROSS), (ACROSS, 1, 0), (ACROSS, 0, 1), (1, 0, ACROSS), (0, ACROSS, 1))
-SHARED_ORDERS = ((0, ACROSS, 1), (ACROSS, 0, 1), (ACROSS, 0, 1), (0, ACROSS, 1), (ACROSS, 0, 1))
+FEED_ORDERS = ((0, ACROSS, 1), (ACROSS, 0, 1), (1, ACROSS, 0), (1, ACROSS, 0), (ACROSS, 0, 1), (0, ACROSS, 1))
+SHARED_ORDERS = ((ACROSS, 0, 1), (ACROSS, 0, 1), (ACROSS, 0, 1), (0, ACROSS, 1), (1, 0, ACROSS), (ACROSS, 0, 1), (ACROSS, 0, 1), (ACROSS, 0, 1))
+SHARED_ROWS = (256, 512, 256, 512, 256, 512, 512, 512)
+GROUPS = (0, 0, 1, 1, 2, 2, 3, 3)
 
 START = (3, 2, 39, 42, 18, 21, 22, 41, 1, 0, 19, 38, 20, 37)
 GATHER = {
@@ -1133,8 +1133,8 @@
     width, lwidth = text_in.shape[1], layout_in.shape[1]
     dp_bits = dp.bit_length() - 1
     half = width // 2
-    feed_flows = tuple(zip((TILE, TILE, TILE + 128, TILE, TILE, TILE), FEED_ORDERS))
-    shared_flows = tuple(zip((width, width, width, half + 128, half + 128), SHARED_ORDERS))
+    feed_flows = tuple(zip((TILE, TILE, TILE, TILE, TILE, TILE + 128), FEED_ORDERS))
+    shared_flows = tuple(zip(SHARED_ROWS, SHARED_ORDERS))
     moves = MOVES if dp_bits == 3 else {}
     feed_rows = sum(rows for rows, _ in feed_flows)
     shared_rows = sum(rows for rows, _ in shared_flows)

time: 171 us -> 167 us (0.977)
  Pallas kernels: 170 us -> 165 us
    pallas_call x1, Pallas kernels: 158 us -> 153 us  [on_device(): pl.pallas_call(functools.partial(layer_kernel, (dp_bits, feed_flows, shar...]
where the time goes in v4:
time: 167 us; the launch traced here: 166 us
  Pallas kernels  165 us (99%)
    pallas_call x1, Pallas kernels, on_device(): pl.pallas_call(functools.partial(layer_kernel, (dp_bits, feed_flows, shar...  153 us
    pallas_call x1, Pallas kernels, on_device(): pl.pallas_call(functools.partial(finish_kernel, feed_rows), out_shape=out...  11.7 us

profile of v4, /device:TPU:0, one launch (start us, length us, event | category | flops | bytes accessed | tf_op | source)
XLA Modules:
  0.0 166.1 jit_solution(15043394360833466582)
XLA Ops:
  0.7 153.5 %layer.1 = (bf16[512,768]{1,0:T(8,128)(2,1)}, bf16[192,512]{1,0:T(8,128)(2,1)}, f32[512,768]{1,0:T(8,128)}, f32[192,512]{1,0:T(8,128)}, bf16[4992,768]{1,0:T(8,128)(2,1)}) custom-call(bf16[512,768]{1,0:T(8,128)(2,1)} %refs_0_.1, bf16[192,512]{1,0:T(8,128)(2,1)} %bitcast.6, s32[1,512]{1,0:T(1,128)} %bitcast.8, s32[1,512]{1,0:T(1,128)} %bitcast.9, ...), custom_call_target="tpu_custom_call" | custom-call | tf_op jit(solution)/shard_map/layer/pallas_call | solution.py:1217
  154.2 11.7 %finish.1 = (bf16[512,768]{1,0:T(8,128)(2,1)}, bf16[192,512]{1,0:T(8,128)(2,1)}, f32[512,768]{1,0:T(8,128)}, f32[192,512]{1,0:T(8,128)}, f32[768,768]{1,0:T(8,12...) custom-call(bf16[4992,768]{1,0:T(8,128)(2,1)} %get-tuple-element.73., ...), custom_call_target="tpu_custom_call" | custom-call | tf_op jit(solution)/shard_map/finish/pallas_call | solution.py:1244

commit v5 on v4

--- a/solution.py
+++ b/solution.py
@@ -965,11 +965,17 @@
     in_grad_copy.wait()
 
 
+def small_places(outs):
+    large = max(out.shape[0] for out in outs if len(out.shape) == 2)
+    return [i for i, out in enumerate(outs) if i > 3 and out.shape != (large, large)]
+
+
 def finish_kernel(feed_rows, sums_hbm, *refs):
     passed, outs = refs[0:4], refs[4:38]
     sums, wide_sums, vec = refs[38:41]
     through = refs[41:45]
-    load_sem, store_sem, in_sem, out_sem = refs[45:49]
+    load_sem, store_sem, in_sem, out_sem, small_sem = refs[45:50]
+    stage = dict(zip(small_places(outs), refs[50:]))
     width, lwidth = wide_sums.shape[1], through[1].shape[0]
     starts = (feed_rows, 0, width, feed_rows + width, feed_rows + 2 * width)
     starts += (feed_rows + 3 * width, feed_rows + 4 * width)
@@ -1000,7 +1006,8 @@
 
         loop(width // 128, block)
 
-    text, layout = outs[4:19], outs[19:34]
+    results = [stage.get(i, out) for i, out in enumerate(outs)]
+    text, layout = results[4:19], results[19:34]
     stores = []
 
     def store(slot, out):
@@ -1058,6 +1065,10 @@
     for k, (row, part) in enumerate(((8, 1), (8, 2), (9, 0))):
         rise = jnp.where(me == k + 1, strip(row, part), rise)
     layout[10][...] = rise[0]
+    for k, (i, ref) in enumerate(stage.items()):
+        copy = pltpu.make_async_copy(ref, outs[i], small_sem.at[k])
+        copy.start()
+        stores.append(copy)
     for copy in stores + gives:
         copy.wait()
 
@@ -1240,12 +1251,12 @@
         shape(lwidth, page, dtype=F32),
     )
     outs += stream(big, width) + stream(small_square, lwidth)
-    specs = [hbm if i < 4 or out.shape == (width, width) else vmem for i, out in enumerate(outs)]
+    stage = [pltpu.VMEM(outs[i].shape, F32) for i in small_places(outs)]
     done = pl.pallas_call(
         functools.partial(finish_kernel, feed_rows),
         out_shape=outs,
         in_specs=[hbm] * 5,
-        out_specs=specs,
+        out_specs=[hbm] * len(outs),
         scratch_shapes=[
             pltpu.VMEM((feed_rows + shared_rows, width), BF16),
             pltpu.VMEM((6, width, width), F32),
@@ -1258,6 +1269,8 @@
             pltpu.SemaphoreType.DMA((6,)),
             pltpu.SemaphoreType.DMA((4,)),
             pltpu.SemaphoreType.DMA((4,)),
+            pltpu.SemaphoreType.DMA((len(stage),)),
+            *stage,
         ],
         compiler_params=pltpu.CompilerParams(vmem_limit_bytes=60000000),
         name="finish",

time: 167 us -> 166 us (level)
  no operation moved by 1% of the time
where the time goes in v5:
time: 166 us
  Pallas kernels  165 us (99%)
    pallas_call x1, Pallas kernels, on_device(): pl.pallas_call(functools.partial(layer_kernel, (dp_bits, feed_flows, shar...  153 us
    pallas_call x1, Pallas kernels, on_device(): pl.pallas_call(functools.partial(finish_kernel, feed_rows), out_shape=out...  11.2 us

profile of v5, /device:TPU:0, one launch (start us, length us, event | category | flops | bytes accessed | tf_op | source)
XLA Modules:
  0.0 165.6 jit_solution(14813548696594774905)
XLA Ops:
  0.7 153.5 %layer.1 = (bf16[512,768]{1,0:T(8,128)(2,1)}, bf16[192,512]{1,0:T(8,128)(2,1)}, f32[512,768]{1,0:T(8,128)}, f32[192,512]{1,0:T(8,128)}, bf16[4992,768]{1,0:T(8,128)(2,1)}) custom-call(bf16[512,768]{1,0:T(8,128)(2,1)} %refs_0_.1, bf16[192,512]{1,0:T(8,128)(2,1)} %bitcast.6, s32[1,512]{1,0:T(1,128)} %bitcast.8, s32[1,512]{1,0:T(1,128)} %bitcast.9, ...), custom_call_target="tpu_custom_call" | custom-call | tf_op jit(solution)/shard_map/layer/pallas_call | solution.py:1228
  154.2 11.2 %finish.1 = (bf16[512,768]{1,0:T(8,128)(2,1)}, bf16[192,512]{1,0:T(8,128)(2,1)}, f32[512,768]{1,0:T(8,128)}, f32[192,512]{1,0:T(8,128)}, f32[768,768]{1,0:T(8,12...) custom-call(bf16[4992,768]{1,0:T(8,128)(2,1)} %get-tuple-element.73., ...), custom_call_target="tpu_custom_call" | custom-call | tf_op jit(solution)/shard_map/finish/pallas_call | solution.py:1255
